TPU v7x, 128 devices: a whole 4x4x4 slice. The times are simulated.
128 devices in a mesh: ctx: 4 (over y), head: 32 (over x, z, core).
Axes of the slice: x: 4, y: 4, z: 4, core: 2. Of those that a mesh axis runs over, the one named last changes fastest.
Arguments:
- queries: bfloat16 [16384, 4096], P('ctx', 'head'), may hold values from -6 to 6
- key_heads: bfloat16 [16384, 4096], P('ctx', 'head'), may hold values from -8 to 8
- value_heads: bfloat16 [16384, 4096], P('ctx', 'head'), may hold values from -120 to 120
- out_gain: bfloat16 [4096], P('head'), may hold values from 0.099609375 to 1.8984375
- out_weight: bfloat16 [4096, 2048], P('head'), may hold values from -0.09375 to 0.09375
- residual: bfloat16 [16384, 2048], P(('ctx', 'head')), may hold values from -36 to 36
- norm_gain: bfloat16 [2048], replicated, may hold values from 0.099609375 to 1.8984375
- routes: int32 [16384, 8], P(('ctx', 'head')), may hold values from 0 to 127, all different within a row; in each aligned block of 128 rows (0 to 127, 128 to 255, ...) at most 10 rows name the same one
- route_weights: float32 [16384, 8], P(('ctx', 'head')), may hold values from 0.02 to 0.4
- cotangent: bfloat16 [16384, 2048], P(('ctx', 'head')), may hold values from -6 to 6
- w_gate: bfloat16 [128, 2048, 768], P(('ctx', 'head')), may hold values from -0.125 to 0.125
- w_up: bfloat16 [128, 2048, 768], P(('ctx', 'head')), may hold values from -0.125 to 0.125
- w_down: bfloat16 [128, 768, 2048], P(('ctx', 'head')), may hold values from -0.21875 to 0.21875
Outputs:
- hidden_out: bfloat16 [16384, 2048], P(('ctx', 'head'))
- grad_gate: bfloat16 [128, 2048, 768], P(('ctx', 'head'))
- grad_up: bfloat16 [128, 2048, 768], P(('ctx', 'head'))
- grad_down: bfloat16 [128, 768, 2048], P(('ctx', 'head'))
Inputs may be any that keep to these rules, and one draw needn't show every extreme that they name: `routes`: each row names 8 different experts. Within each aligned block of 128 rows no expert is named by more than 10 rows; in some blocks an expert is named by exactly 10 rows.
All inputs are finite; a program needn't handle non-finite values.
Results may differ from a plain program's by a relative error of at most 0.025.
Values may be sent and summed in bfloat16 or wider, within the bound.
No kernel may reach another device: no remote copies, remote signals or barrier semaphores. Data moves between devices by JAX's collectives and lax.ppermute only.
A program may use at most 192 MiB of HBM per device.

v0:
```python
import jax
import jax.numpy as jnp
from jax import lax
from jax.sharding import PartitionSpec as P

HEADS = 32
HD = 128
EXPERTS = 128
TOPK = 8


epsilon = 1e-06


def in_one_piece(arrays, axis, dim, along):
    columns = [a.reshape(*a.shape[:along], -1) for a in arrays]
    both = jnp.concatenate(columns, axis=along)
    filled, at, gathered = (lax.all_gather(both, axis, axis=dim, tiled=True), 0, [])
    for a, column in zip(arrays, columns):
        section = filled[..., at : at + column.shape[along]]
        gathered.append(section.reshape(*section.shape[:along], *a.shape[along:]))
        at += column.shape[along]
    return tuple(gathered)


def sent_together(arrays, axis, split_dim, concat_dim, along):
    widths = [a.shape[along] for a in arrays]
    both = jnp.concatenate(arrays, axis=along)
    filled = lax.all_to_all(both, axis, split_axis=split_dim, concat_axis=concat_dim, tiled=True)
    return tuple(jnp.split(filled, [sum(widths[:k]) for k in range(1, len(widths))], axis=along))


def round_half(values):
    return lax.optimization_barrier(values.astype(jnp.bfloat16)).astype(jnp.float32)


def feature_map(values):
    widened = values.astype(jnp.float32)
    return jnp.where(widened > 0, widened + 1.0, jnp.exp(jnp.minimum(widened, 0.0))).astype(
        jnp.bfloat16
    )


def rms_norm(values, gain):
    widened = values.astype(jnp.float32)
    inverse = lax.rsqrt(jnp.mean(widened * widened, axis=-1, keepdims=True) + epsilon)
    return (widened * inverse * gain.astype(jnp.float32)).astype(jnp.bfloat16)


def attend_blocks(query_raw, key_feat, value_heads, state_sum, key_sum, block_size):
    length = query_raw.shape[0]
    heads_here = key_feat.shape[1]
    head_size = key_feat.shape[2]
    causal_mask = jnp.tril(jnp.ones((block_size, block_size), jnp.bool_))

    def into_blocks(array_in):
        return array_in.reshape(length // block_size, block_size, heads_here, head_size)

    def one_block(carry, inputs):
        running_state, running_keys = carry
        query_block, key_block, value_block = inputs
        query_block = feature_map(query_block)
        query_wide = query_block.astype(jnp.float32)
        scores = jnp.einsum(
            "bhi,chi->hbc", query_block, key_block, preferred_element_type=jnp.float32
        )
        scores = jnp.where(causal_mask[None], scores, 0.0)
        numerator = jnp.einsum("hbc,chj->bhj", scores, value_block.astype(jnp.float32))
        numerator = numerator + jnp.einsum("bhi,hij->bhj", query_wide, running_state)
        denominator = jnp.sum(scores, axis=2).T + jnp.einsum("bhi,hi->bh", query_wide, running_keys)
        result = (numerator / denominator[:, :, None]).astype(jnp.bfloat16)
        running_state = running_state + jnp.einsum(
            "bhi,bhj->hij", key_block, value_block, preferred_element_type=jnp.float32
        )
        running_keys = running_keys + jnp.sum(key_block.astype(jnp.float32), axis=0)
        return ((running_state, running_keys), result)

    carry_out, outputs = lax.scan(
        one_block,
        (state_sum, key_sum),
        (into_blocks(query_raw), into_blocks(key_feat), into_blocks(value_heads)),
    )
    return outputs.reshape(length, heads_here * head_size)


def expert_grads(rows_in, scaled, gate_mat, up_mat, down_mat):
    gate_pre = jnp.dot(rows_in, gate_mat, preferred_element_type=jnp.float32)
    up_pre = jnp.dot(rows_in, up_mat, preferred_element_type=jnp.float32)
    sigmoid_gate = jax.nn.sigmoid(gate_pre)
    active = gate_pre * sigmoid_gate
    hidden_units = (active * up_pre).astype(jnp.bfloat16)
    grad_down = lax.dot_general(
        hidden_units, scaled, (((0,), (0,)), ((), ())), preferred_element_type=jnp.float32
    ).astype(jnp.bfloat16)
    grad_hidden = lax.dot_general(
        scaled, down_mat, (((1,), (1,)), ((), ())), preferred_element_type=jnp.float32
    )
    silu_slope = sigmoid_gate * (1.0 + gate_pre * (1.0 - sigmoid_gate))
    grad_pre_gate = (grad_hidden * up_pre * silu_slope).astype(jnp.bfloat16)
    grad_pre_up = (grad_hidden * active).astype(jnp.bfloat16)
    grad_gate = lax.dot_general(
        rows_in, grad_pre_gate, (((0,), (0,)), ((), ())), preferred_element_type=jnp.float32
    ).astype(jnp.bfloat16)
    grad_up = lax.dot_general(
        rows_in, grad_pre_up, (((0,), (0,)), ((), ())), preferred_element_type=jnp.float32
    ).astype(jnp.bfloat16)
    return (grad_gate, grad_up, grad_down)


def on_device(
    queries,
    key_heads,
    value_heads,
    out_gain,
    out_weight,
    residual,
    norm_gain,
    routes,
    route_weights,
    cotangent,
    w_gate,
    w_up,
    w_down,
):
    length = queries.shape[0]
    heads_here = queries.shape[1] // HD
    block_size = min(512, length)
    key_feat = feature_map(key_heads.reshape(length, heads_here, HD))
    value_split = value_heads.reshape(length, heads_here, HD)
    span_state = jnp.einsum(
        "thi,thj->hij", key_feat, value_split, preferred_element_type=jnp.float32
    )
    span_keys = jnp.sum(key_feat.astype(jnp.float32), axis=0)
    all_states, all_keys = tuple(
        (
            part.astype(jnp.float32)
            for part in in_one_piece(
                (span_state[None].astype(jnp.bfloat16), span_keys[None].astype(jnp.bfloat16)),
                "ctx",
                0,
                3,
            )
        )
    )
    before = (jnp.arange(all_states.shape[0], dtype=jnp.int32) < lax.axis_index("ctx")).astype(
        jnp.float32
    )
    start_state = jnp.einsum("c,chij->hij", before, all_states)
    start_keys = jnp.einsum("c,chi->hi", before, all_keys)
    attention = attend_blocks(
        queries.reshape(length, heads_here, HD),
        key_feat,
        value_split,
        start_state,
        start_keys,
        block_size,
    )
    tok_here = residual.shape[0]
    model_width = residual.shape[1]
    by_token = lax.all_to_all(attention, "head", split_axis=0, concat_axis=1, tiled=True)
    token_wide = by_token.astype(jnp.float32)
    inv_rms = lax.rsqrt(jnp.sum(token_wide * token_wide, axis=1) / (HEADS * HD) + epsilon)
    scaled_rows = token_wide * inv_rms[:, None]
    shard_rows = out_weight.shape[0]
    weight_piece, gain_piece = in_one_piece((out_weight, out_gain), "head", 0, 1)
    row_count = weight_piece.shape[0]
    groups = row_count // shard_rows
    normed_piece = (scaled_rows * gain_piece.astype(jnp.float32)).astype(jnp.bfloat16)
    partial_value = jnp.einsum(
        "tgs,gsd->tgd",
        normed_piece.reshape(tok_here, groups, shard_rows),
        weight_piece.reshape(groups, shard_rows, model_width),
        preferred_element_type=jnp.float32,
    )
    projected = jnp.sum(round_half(partial_value), axis=1)
    hidden_out = (residual.astype(jnp.float32) + projected).astype(jnp.bfloat16)
    moe_in = rms_norm(hidden_out, norm_gain)
    per_block = tok_here * TOPK
    flat_routes = routes.reshape(per_block)
    onehot = (flat_routes[:, None] == jnp.arange(EXPERTS, dtype=jnp.int32)[None, :]).astype(
        jnp.int32
    )
    rank_in_block = jnp.sum(jnp.cumsum(onehot, axis=0) * onehot, axis=1) - 1
    local_experts = w_gate.shape[0]
    devices = lax.axis_size(("ctx", "head"))
    capacity = EXPERTS * 0 + max(2, tok_here * TOPK * 5 // (EXPERTS * 4))
    slot_rows = devices * capacity
    target = (
        flat_routes % local_experts * slot_rows
        + flat_routes // local_experts * capacity
        + rank_in_block
    )
    filler = (
        jnp.full((local_experts * slot_rows,), per_block, jnp.int32)
        .at[target]
        .set(jnp.arange(per_block, dtype=jnp.int32))
    )
    is_filled = filler < per_block
    safe_index = jnp.minimum(filler, per_block - 1)
    token_index = safe_index // TOPK
    rows_in = jnp.where(is_filled[:, None], moe_in[token_index], jnp.zeros((), jnp.bfloat16))
    weighted = route_weights.reshape(per_block)[safe_index][:, None] * cotangent[
        token_index
    ].astype(jnp.float32)
    scaled = jnp.where(is_filled[:, None], weighted, 0.0).astype(jnp.bfloat16)
    rows_in = rows_in.reshape(local_experts, slot_rows, model_width)
    scaled = scaled.reshape(local_experts, slot_rows, model_width)
    rows_in, scaled = sent_together((rows_in, scaled), ("ctx", "head"), 1, 1, 0)

    def per_expert(inputs):
        return expert_grads(inputs[0], inputs[1], inputs[2], inputs[3], inputs[4])

    grad_gate, grad_up, grad_down = lax.map(per_expert, (rows_in, scaled, w_gate, w_up, w_down))
    return (hidden_out, grad_gate, grad_up, grad_down)


def solution(mesh):
    in_specs = (
        P("ctx", "head"),
        P("ctx", "head"),
        P("ctx", "head"),
        P("head"),
        P("head", None),
        P(("ctx", "head"), None),
        P(),
        P(("ctx", "head"), None),
        P(("ctx", "head"), None),
        P(("ctx", "head"), None),
        P(("ctx", "head"), None, None),
        P(("ctx", "head"), None, None),
        P(("ctx", "head"), None, None),
    )
    out_specs = (
        P(("ctx", "head"), None),
        P(("ctx", "head"), None, None),
        P(("ctx", "head"), None, None),
        P(("ctx", "head"), None, None),
    )
    return jax.shard_map(
        on_device, mesh=mesh, in_specs=in_specs, out_specs=out_specs, check_vma=False
    )
```

profile of v0, /device:TPU:1, one launch (start us, length us, event | category | flops | bytes accessed | tf_op | source)
XLA Modules:
  0.0 431.0 jit_solution(9107931611022834208)
XLA Ops:
  8.2 1.9 pad_maximum_fusion.1
  10.1 1.9 fusion.81
  12.9 1.7 fusion.48
  14.6 10.6 %all_gather.7 = bf16[4,1,128,129]{2,3,1,0:T(8,128)(2,1)S(1)} all-gather(bf16[1,1,128,129]{2,3,1,0:T(8,128)(2,1)S(1)} %pad_maximum_fusion.2), channel_id=1, replica_groups=mesh['ctx'=4,'head'=32] {'ctx'}, dimensions={0}, use_global_device_ids=true | all-gather | bytes 165120 | tf_op jit(solution)/shard_map/all_gather | solution.py:18
  25.7 62.0 %while.3 = (s32[]{:T(128)}, f32[1,128,128]{2,1,0:T(8,128)S(1)}, f32[1,128]{1,0:T(1,128)S(1)}, bf16[8,512,1,128]{3,1,0,2:T(8,128)(2,1)}, bf16[8,512,1,128]{3,1,2,...) while((s32[]{:T(128)}, f32[1,128,128]{2,1,0:T(8,128)S(1)}, ...), condition=%wide.region_4.5_spmd.clone, body=%wide.region_1.4_spmd.clone.sunk | while | flops 170475520 | bytes 3490417 | solution.py:78
  35.6 1.3 fusion.124
  66.6 1.4 fusion.124
  87.8 11.8 %all-to-all-start = ((bf16[32,128,128]{2,1,0:T(8,128)(2,1)}), bf16[32,128,128]{2,1,0:T(8,128)(2,1)}, u32[]{:S(2)}, u32[]{:S(2)}) async-start(bf16[32,128,128]{2,1,0:T(8,128)(2,1)} %bitcast.204), calls=%async_computation | async-start | bytes 2097152 | tf_op jit(solution)/shard_map/all_to_all | solution.py:160
  103.0 4.8 %scatter_custom_fusion = s32[1280]{0:T(1024)S(1)} fusion(s32[1024]{0:T(1024)S(1)} %bitcast.208, s32[1024]{0:T(1024)S(1)} %iota.31, s32[]{:T(128)} %constant.111.clone.1), kind=kCustom, calls=%fused_computation.114 | custom fusion | bytes 5124 | tf_op jit(solution)/shard_map/scatter | solution.py:196
  107.9 5.0 %gather_fusion.1 = f32[1280]{0:T(1024)S(1)} fusion(f32[1024]{0:T(1024)S(1)} %reshape.307, s32[2048]{0:T(1024)S(1)} %get-tuple-element.135), kind=kCustom, calls=%fused_computation.1 | custom fusion | bytes 15360 | tf_op jit(solution)/shard_map/gather | solution.py:202
  112.9 11.9 %gather_fusion.2 = bf16[1280,2048]{1,0:T(8,128)(2,1)} fusion(bf16[128,2048]{1,0:T(8,128)(2,1)} %param.24, s32[2048]{0:T(1024)S(1)} %get-tuple-element.136), kind=kCustom, calls=%fused_computation.2 | custom fusion | bytes 10490880 | tf_op jit(solution)/shard_map/gather | solution.py:202
  124.8 6.0 %fusion.31 = bf16[1,1280,2048]{2,1,0:T(8,128)(2,1)} fusion(bf16[1280,2048]{1,0:T(8,128)(2,1)} %gather_fusion.2, f32[1280]{0:T(1024)S(1)} %gather_fusion.1, pred[1280]{0:T(1024)(128)(4,1)S(1)} %broadcast_compare_fusion), kind=kLoop, calls=%fused_computation.45 | loop fusion | flops 10485760 | bytes 10492160 | tf_op jit(solution)/shard_map/convert_element_type | solution.py:205
  130.8 1.5 fusion.42
  132.4 1.6 convert_reduce_fusion.2
  134.0 14.1 %slice.30 = bf16[4096,2048]{1,0:T(8,128)(2,1)} slice(bf16[4096,2049]{1,0:T(8,128)(2,1)} %all-gather.2.cloned.1.call-done), slice={[0:4096], [0:2048]} | slice | bytes 33554432 | tf_op jit(solution)/shard_map/slice | solution.py:20
  148.1 14.1 %convert_bitcast_fusion = bf16[128,32,2048]{0,2,1:T(8,128)(2,1)} fusion(bf16[32,128,2048]{2,1,0:T(8,128)(2,1)} %bitcast.194, bf16[32,128,128]{2,1,0:T(8,128)(2,1)} %all-to-all-done, f32[32,128]{1,0:T(8,128)S(1)} %bitcast.205, f32[128]{0:T(128)S(1)} %add_rsqrt_fusion.1), kind=kOutput, calls=%fused_computation.41 | convolution fusion | flops 2157969408 | bytes 34619904 | tf_op jit(solution)/shard_map/tgs,gsd->tgd/dot_general | solution.py:169
  162.1 7.7 %convert_reduce_fusion.1 = f32[128,2048]{0,1:T(8,128)} fusion(bf16[128,32,2048]{0,2,1:T(8,128)(2,1)} %convert_bitcast_fusion), kind=kLoop, calls=%fused_computation.40 | loop fusion | flops 16515072 | bytes 17825792 | tf_op jit(solution)/shard_map/reduce_sum | solution.py:175
  169.9 2.5 copy.54
  172.4 1.6 fusion.49
  175.8 11.9 %gather_fusion = bf16[1280,2048]{1,0:T(8,128)(2,1)} fusion(bf16[128,2048]{1,0:T(8,128)(2,1)} %fusion.51, s32[2048]{0:T(1024)S(1)} %get-tuple-element.136), kind=kCustom, calls=%fused_computation | custom fusion | bytes 10490880 | tf_op jit(solution)/shard_map/gather | solution.py:201
  187.7 5.3 %bitcast_select_fusion = bf16[1,1280,2048]{2,1,0:T(8,128)(2,1)} fusion(bf16[1280,2048]{1,0:T(8,128)(2,1)} %gather_fusion, pred[1280]{0:T(1024)(128)(4,1)S(1)} %broadcast_compare_fusion), kind=kLoop, calls=%fused_computation.48 | loop fusion | flops 2621440 | bytes 10487040 | tf_op jit(solution)/shard_map/jit(_where)/select_n | solution.py:201
  193.0 9.0 %pad_maximum_fusion = bf16[2,1280,2048]{2,1,0:T(8,128)(2,1)} fusion(bf16[1,1280,2048]{2,1,0:T(8,128)(2,1)} %fusion.31, bf16[1,1280,2048]{2,1,0:T(8,128)(2,1)} %bitcast_select_fusion), kind=kLoop, calls=%fused_computation.42 | loop fusion | flops 5242880 | bytes 20971520 | tf_op jit(solution)/shard_map/concatenate | solution.py:28
  202.0 20.0 %copy.61 = bf16[2,1280,2048]{2,0,1:T(2,128)(2,1)} copy(bf16[2,1280,2048]{2,1,0:T(8,128)(2,1)} %pad_maximum_fusion) | data formatting | bytes 20971520 | tf_op jit(solution)/shard_map/concatenate | solution.py:28
  222.0 129.5 %all_to_all.18 = bf16[2,1280,2048]{2,0,1:T(2,128)(2,1)S(1)} all-to-all(bf16[2,1280,2048]{2,0,1:T(2,128)(2,1)} %copy.61), channel_id=1, replica_groups=mesh['ctx'=4,'head'=32] {'ctx','head'}, dimensions={1} | all-to-all | bytes 20971520 | tf_op jit(solution)/shard_map/all_to_all | solution.py:29
  351.6 16.1 %fusion.84 = (bf16[1,1280,2048]{2,0,1:T(2,128)(2,1)}, bf16[1,1280,2048]{2,0,1:T(2,128)(2,1)}) fusion(bf16[2,1280,2048]{2,0,1:T(2,128)(2,1)S(1)} %all_to_all.18), kind=kLoop, calls=%fused_computation.136 | loop fusion | bytes 20971520 | tf_op jit(solution)/shard_map/split | solution.py:30
  367.7 7.3 %copy.80 = bf16[1,1280,2048]{2,1,0:T(8,128)(2,1)S(1)} copy(bf16[1,1280,2048]{2,0,1:T(2,128)(2,1)} %get-tuple-element.132) | data formatting | bytes 10485760
  375.0 6.3 %fusion.33 = f32[1280,768]{1,0:T(8,128)} fusion(bf16[1280,2048]{1,0:T(8,128)(2,1)S(1)} %bitcast.199, bf16[1,2048,768]{2,1,0:T(8,128)(2,1)S(1)} %copy-done), kind=kOutput, calls=%fused_computation.57 | convolution fusion | flops 4026531840 | bytes 12320768 | tf_op jit(solution)/shard_map/while/body/eval_jaxpr/dot_general | solution.py:87
  381.3 6.2 %fusion.35 = f32[1280,768]{1,0:T(8,128)} fusion(bf16[1280,2048]{1,0:T(8,128)(2,1)S(1)} %bitcast.200, bf16[1,2048,768]{2,1,0:T(8,128)(2,1)S(1)} %copy-done.7), kind=kOutput, calls=%fused_computation.59 | convolution fusion | flops 4026531840 | bytes 12320768 | tf_op jit(solution)/shard_map/while/body/eval_jaxpr/dot_general | solution.py:88
  387.5 8.3 %fusion.37 = f32[1280,768]{1,0:T(8,128)} fusion(bf16[1,768,2048]{2,1,0:T(8,128)(2,1)S(1)} %copy-done.8, bf16[1,1280,2048]{2,0,1:T(2,128)(2,1)S(1)} %bitcast.197), kind=kOutput, calls=%fused_computation.61 | convolution fusion | flops 4026531840 | bytes 12320768 | tf_op jit(solution)/shard_map/while/body/eval_jaxpr/dot_general | solution.py:95
  395.8 10.3 %fusion.41 = bf16[1,768,2048]{2,1,0:T(8,128)(2,1)} fusion(bf16[1,1280,2048]{2,0,1:T(2,128)(2,1)S(1)} %bitcast.197, f32[1280,768]{1,0:T(8,128)} %fusion.35, f32[1280,768]{1,0:T(8,128)} %fusion.33), kind=kOutput, calls=%fused_computation.68 | convolution fusion | flops 4034002944 | bytes 16252928 | tf_op jit(solution)/shard_map/while/body/eval_jaxpr/dot_general | solution.py:92
  406.1 11.2 %fusion.39 = bf16[1,2048,768]{2,1,0:T(8,128)(2,1)} fusion(bf16[1280,2048]{1,0:T(8,128)(2,1)S(1)} %bitcast.201, f32[1280,768]{1,0:T(8,128)} %fusion.33, f32[1280,768]{1,0:T(8,128)} %fusion.37, f32[1280,768]{1,0:T(8,128)} %fusion.35), kind=kOutput, calls=%fused_computation.66 | convolution fusion | flops 4037935104 | bytes 20185088 | tf_op jit(solution)/shard_map/while/body/eval_jaxpr/dot_general | solution.py:101
  417.3 6.5 %fusion.40 = bf16[1,2048,768]{2,1,0:T(8,128)(2,1)} fusion(bf16[1280,2048]{1,0:T(8,128)(2,1)S(1)} %bitcast.202, f32[1280,768]{1,0:T(8,128)S(1)} %copy-done.10, f32[1280,768]{1,0:T(8,128)S(1)} %copy-done.9), kind=kOutput, calls=%fused_computation.67 | convolution fusion | flops 4034002944 | bytes 16252928 | tf_op jit(solution)/shard_map/while/body/eval_jaxpr/dot_general | solution.py:104
  (145 shorter events, 66.7 us)
Async XLA Ops:
  7.2 367.8 %copy-start = (bf16[1,2048,768]{2,1,0:T(8,128)(2,1)S(1)}, bf16[1,2048,768]{2,1,0:T(8,128)(2,1)}, u32[]{:S(2)}) copy-start(bf16[1,2048,768]{2,1,0:T(8,128)(2,1)} %param.25) | copy-start | bytes 9437188
  7.2 125.2 %all-gather.2.cloned.1.call-start = ((), (), s32[]{:S(2)}) async-start(), calls=%async_computation.2 | async-start | bytes 18382848 | tf_op jit(solution)/shard_map/all_gather | solution.py:18
  11.9 1.0 copy-start.1
  25.7 73.8 %copy-start.4 = (s32[128,8]{0,1:T(8,128)S(1)}, s32[128,8]{0,1:T(8,128)}, u32[]{:S(2)}) copy-start(s32[128,8]{0,1:T(8,128)} %param.22) | copy-start | bytes 12292
  25.7 74.1 %copy-start.5 = (bf16[2048]{0:T(1024)(128)(2,1)S(1)}, bf16[2048]{0:T(1024)(128)(2,1)}, u32[]{:S(2)}) copy-start(bf16[2048]{0:T(1024)(128)(2,1)} %param.21) | copy-start | bytes 12292
  25.7 74.4 %copy-start.6 = (f32[128,8]{0,1:T(8,128)S(1)}, f32[128,8]{0,1:T(8,128)}, u32[]{:S(2)}) copy-start(f32[128,8]{0,1:T(8,128)} %param.23) | copy-start | bytes 12292
  87.8 43.1 %all-to-all-start = ((bf16[32,128,128]{2,1,0:T(8,128)(2,1)}), bf16[32,128,128]{2,1,0:T(8,128)(2,1)}, u32[]{:S(2)}, u32[]{:S(2)}) async-start(bf16[32,128,128]{2,1,0:T(8,128)(2,1)} %bitcast.204), calls=%async_computation | async-start | bytes 2097152 | tf_op jit(solution)/shard_map/all_to_all | solution.py:160
  100.6 0.8 copy-start.2
  174.0 0.8 copy-start.3
  375.0 6.3 %copy-start.7 = (bf16[1,2048,768]{2,1,0:T(8,128)(2,1)S(1)}, bf16[1,2048,768]{2,1,0:T(8,128)(2,1)}, u32[]{:S(2)}) copy-start(bf16[1,2048,768]{2,1,0:T(8,128)(2,1)} %param.26) | copy-start | bytes 9437188
  375.0 12.5 %slice-start = ((s8[10485760]{0:T(1024)(128)(4,1)}), s8[4194304]{0:T(1024)(128)(4,1)S(1)}, s32[]{:S(2)}) async-start(s8[10485760]{0:T(1024)(128)(4,1)} %bitcast.196), calls=%async_computation.3 | async-start | bytes 8388608
  375.0 12.5 %slice-start.1 = ((s8[10485760]{0:T(1024)(128)(4,1)}), s8[4194304]{0:T(1024)(128)(4,1)S(1)}, s32[]{:S(2)}) async-start(s8[10485760]{0:T(1024)(128)(4,1)} %bitcast.196), calls=%async_computation.4 | async-start | bytes 8388608
  381.3 6.2 %slice-start.2 = ((s8[10485760]{0:T(1024)(128)(4,1)}), s8[2097152]{0:T(1024)(128)(4,1)S(1)}, s32[]{:S(2)}) async-start(s8[10485760]{0:T(1024)(128)(4,1)} %bitcast.196), calls=%async_computation.5 | async-start | bytes 4194304
  381.3 6.2 %copy-start.8 = (bf16[1,768,2048]{2,1,0:T(8,128)(2,1)S(1)}, bf16[1,768,2048]{2,1,0:T(8,128)(2,1)}, u32[]{:S(2)}) copy-start(bf16[1,768,2048]{2,1,0:T(8,128)(2,1)} %param.27) | copy-start | bytes 9437188
  406.1 11.2 %copy-start.9 = (f32[1280,768]{1,0:T(8,128)S(1)}, f32[1280,768]{1,0:T(8,128)}, u32[]{:S(2)}) copy-start(f32[1280,768]{1,0:T(8,128)} %fusion.33) | copy-start | bytes 11796484
  406.1 11.2 %copy-start.10 = (f32[1280,768]{1,0:T(8,128)S(1)}, f32[1280,768]{1,0:T(8,128)}, u32[]{:S(2)}) copy-start(f32[1280,768]{1,0:T(8,128)} %fusion.37) | copy-start | bytes 11796484
Sparse Core Ops, SparseCore 0:
  10.8 78.8 all-gather.1
where the time goes:
time: 437 us; the launch traced here: 431 us
  blocking collectives  140 us (32%)
  matrix products  112 us (26%)
  local copies, waits for them, and re-layouts  105 us (24%)
  other arithmetic  47.2 us (11%)
  between operations  14.6 us (3%)
  starting transfers between devices  11.8 us (3%)
    all_to_all x1, blocking collectives, sent_together(): lax.all_to_all(both, axis, split_axis=split_dim, concat_axis=concat_dim,...  130 us
    concatenate x1, local copies, waits for them, and re-layouts, sent_together(): both = jnp.concatenate(arrays, axis=along)  20 us
    split x1, local copies, waits for them, and re-layouts, sent_together(): jnp.split(filled, [sum(widths[:k]) for k in range(1, len(widths))], axis=...  16.1 us
    slice x2, local copies, waits for them, and re-layouts, in_one_piece(): section = filled[..., at:at + column.shape[along]]  14.1 us
    dot_general x1, matrix products, on_device(): jnp.einsum('tgs,gsd->tgd', normed_piece.reshape(tok_here, groups, shard_r...  14.1 us
    gather x1, local copies, waits for them, and re-layouts, on_device(): moe_in[token_index]  11.9 us
    gather x1, local copies, waits for them, and re-layouts, on_device(): cotangent[token_index].astype(jnp.float32)  11.9 us
    all_to_all x1, starting transfers between devices, on_device(): lax.all_to_all(attention, 'head', split_axis=0, concat_axis=1, tiled=True)  11.8 us
  transfers between devices with their start and end apart: 2, of which 0 were waited for; matrix products, arithmetic and copies ran while one was open for 23% of the time, Pallas kernels for 0%

commit v1 on v0

v1 whole, which is shorter than its diff:
```python
import jax
import jax.numpy as jnp
from jax import lax
from jax.experimental import pallas as pl
from jax.experimental.pallas import tpu as pltpu
from jax.sharding import Mesh, PartitionSpec as P

HD = 128
HEADS = 32
EXPERTS = 128
TOPK = 8
MAIN = 8
TAIL = 2
QUART = 4
EPS = 1e-06
BF = jnp.bfloat16
F32 = jnp.float32
ALL = ("ctx", "chip", "core")


def phi(values):
    wide = values.astype(F32)
    return jnp.where(wide > 0, wide + 1.0, jnp.exp(jnp.minimum(wide, 0.0))).astype(BF)


def dot(a, b, ca=1, cb=0):
    return lax.dot_general(a, b, (((ca,), (cb,)), ((), ())), preferred_element_type=F32)


def params(**kw):
    return pltpu.CompilerParams(vmem_limit_bytes=56 * 1024 * 1024, **kw)


def state_kernel(k_ref, v_ref, o_ref, acc):
    i = pl.program_id(0)

    @pl.when(i == 0)
    def _():
        acc[...] = jnp.zeros_like(acc)

    kf = phi(k_ref[...])
    v = v_ref[...]
    acc[...] += dot(kf, jnp.concatenate([v, jnp.ones_like(v)], axis=1), 0, 0)

    @pl.when(i == pl.num_programs(0) - 1)
    def _():
        for c in range(o_ref.shape[0]):
            o_ref[c] = acc[...].astype(BF)


def span_states(keys, values, n_ctx):
    length = keys.shape[0]
    block = min(1024, length)
    return pl.pallas_call(
        state_kernel,
        grid=(length // block,),
        in_specs=[pl.BlockSpec((block, HD), lambda i: (i, 0))] * 2,
        out_specs=pl.BlockSpec((n_ctx, HD, 2 * HD), lambda i: (0, 0, 0)),
        out_shape=jax.ShapeDtypeStruct((n_ctx, HD, 2 * HD), BF),
        scratch_shapes=[pltpu.VMEM((HD, 2 * HD), F32)],
        compiler_params=params(),
    )(keys, values)


CHUNK = 256


def attend_kernel(at_ref, q_ref, k_ref, v_ref, s_ref, o_ref, state):
    @pl.when(pl.program_id(0) == 0)
    def _():
        total = jnp.zeros(state.shape, F32)
        for c in range(s_ref.shape[0]):
            total = total + jnp.where(c < at_ref[0], s_ref[c].astype(F32), 0.0)
        state[...] = total

    rows = lax.broadcasted_iota(jnp.int32, (CHUNK, CHUNK), 0)
    cols = lax.broadcasted_iota(jnp.int32, (CHUNK, CHUNK), 1)
    run = state[...]
    for n in range(q_ref.shape[0] // CHUNK):
        part = pl.ds(n * CHUNK, CHUNK)
        qf = phi(q_ref[part, :])
        kf = phi(k_ref[part, :])
        v = v_ref[part, :]
        v1 = jnp.concatenate([v, jnp.ones_like(v)], axis=1)
        scores = jnp.where(rows >= cols, dot(qf, kf, 1, 1), 0.0).astype(BF)
        both = dot(scores, v1) + dot(qf, run.astype(BF))
        o_ref[part, :] = (both[:, :HD] / both[:, HD:]).astype(BF)
        run = run + dot(kf, v1, 0, 0)
    state[...] = run


def attend(at, queries, keys, values, states):
    length = queries.shape[0]
    block = min(1024, length)
    tok = pl.BlockSpec((block, HD), lambda i, at: (i, 0))
    return pl.pallas_call(
        attend_kernel,
        grid_spec=pltpu.PrefetchScalarGridSpec(
            num_scalar_prefetch=1,
            grid=(length // block,),
            in_specs=[tok, tok, tok, pl.BlockSpec(states.shape, lambda i, at: (0, 0, 0))],
            out_specs=tok,
            scratch_shapes=[pltpu.VMEM((HD, 2 * HD), F32)],
        ),
        out_shape=jax.ShapeDtypeStruct(queries.shape, BF),
        compiler_params=params(),
    )(at, queries, keys, values, states)


def ranks(routes_t, expand):
    tokens = routes_t.shape[1]
    experts = lax.broadcasted_iota(jnp.int32, (EXPERTS, tokens), 0)
    named = jnp.zeros((EXPERTS, tokens), F32)
    for k in range(TOPK):
        named = named + jnp.where(routes_t[k : k + 1, :] == experts, 1.0, 0.0)
    earlier = lax.broadcasted_iota(jnp.int32, (tokens, tokens), 0)
    later = lax.broadcasted_iota(jnp.int32, (tokens, tokens), 1)
    before = jnp.where(earlier < later, 1.0, 0.0).astype(BF)
    rank = jnp.where(named > 0.0, dot(named.astype(BF), before), -1.0)
    return dot(expand, rank.astype(BF))


def expander():
    row = lax.broadcasted_iota(jnp.int32, (EXPERTS * MAIN, EXPERTS), 0) // MAIN
    col = lax.broadcasted_iota(jnp.int32, (EXPERTS * MAIN, EXPERTS), 1)
    return jnp.where(row == col, 1.0, 0.0).astype(BF)


def picks(rank8):
    row = lax.broadcasted_iota(jnp.int32, rank8.shape, 0)
    main = rank8 == (row % MAIN).astype(F32)
    tail = rank8 == (MAIN + row % TAIL).astype(F32)
    return main, tail, (row % MAIN) // TAIL


def tail_rows(tail, quarter, table):
    width = table.shape[1] // QUART
    total = None
    for q in range(QUART):
        pick = jnp.where(tail & (quarter == q), 1.0, 0.0).astype(BF)
        piece = dot(pick, table[:, q * width : (q + 1) * width])
        total = piece if total is None else total + piece
    return total


BLOCKS = 4


def pack_cot_kernel(routes_ref, weights_ref, cot_ref, main_ref, tail_ref, rank_s, weight_s):
    step = pl.program_id(0)

    @pl.when(step == 0)
    def _():
        expand = expander()
        routes_t = routes_ref[...]
        rank_s[...] = ranks(routes_t, expand)
        experts = lax.broadcasted_iota(jnp.int32, (EXPERTS, routes_t.shape[1]), 0)
        weight = jnp.zeros(experts.shape, F32)
        for k in range(TOPK):
            weight = weight + jnp.where(
                routes_t[k : k + 1, :] == experts, weights_ref[k : k + 1, :], 0.0
            )
        total = jnp.zeros(rank_s.shape, F32)
        for _ in range(3):
            piece = weight.astype(BF)
            total = total + dot(expand, piece)
            weight = weight - piece.astype(F32)
        weight_s[...] = total

    size = EXPERTS * MAIN // BLOCKS
    part = pl.ds(step * size, size)
    weight8 = weight_s[part, :]
    main, tail, quarter = picks(rank_s[part, :])
    table = cot_ref[...]
    scale = jnp.sum(jnp.where(main, weight8, 0.0), axis=1, keepdims=True)
    main_ref[...] = (dot(jnp.where(main, 1.0, 0.0).astype(BF), table) * scale).astype(BF)
    scale = jnp.sum(jnp.where(tail, weight8, 0.0), axis=1, keepdims=True)
    tail_ref[...] = (tail_rows(tail, quarter, table) * scale).astype(BF)


def packed_shapes(width):
    rows = EXPERTS * MAIN
    size = rows // BLOCKS
    specs = [
        pl.BlockSpec((size, width), lambda i: (i, 0)),
        pl.BlockSpec((size, width // QUART), lambda i: (i, 0)),
    ]
    shapes = [
        jax.ShapeDtypeStruct((rows, width), BF),
        jax.ShapeDtypeStruct((rows, width // QUART), BF),
    ]
    return specs, shapes


def whole(array):
    return pl.BlockSpec(array.shape, lambda *_: (0,) * array.ndim)


def pack_cot(routes_t, weights_t, cotangent):
    tokens, width = cotangent.shape
    specs, shapes = packed_shapes(width)
    return pl.pallas_call(
        pack_cot_kernel,
        grid=(BLOCKS,),
        in_specs=[whole(routes_t), whole(weights_t), whole(cotangent)],
        out_specs=specs,
        out_shape=shapes,
        scratch_shapes=[pltpu.VMEM((EXPERTS * MAIN, tokens), F32)] * 2,
        compiler_params=params(),
    )(routes_t, weights_t, cotangent)


def project_kernel(core_ref, x_ref, w_ref, mine_ref, ss_ref, theirs_ref, own_s, other_s):
    step = pl.program_id(0)
    tokens = mine_ref.shape[0]
    width = mine_ref.shape[1]
    total = pl.num_programs(0) * width

    @pl.when(step == 0)
    def _():
        core = core_ref[0]
        for at, keep in ((core, own_s), (1 - core, other_s)):
            square = jnp.zeros((tokens, HD), F32)
            for s in range(x_ref.shape[0]):
                piece = x_ref[s, pl.ds(pl.multiple_of(at * tokens, tokens), tokens), :]
                keep[:, s * HD : (s + 1) * HD] = piece
                wide = piece.astype(F32)
                square = square + wide * wide
            summed = jnp.broadcast_to(jnp.sum(square, axis=1, keepdims=True), (tokens, HD))
            if keep is own_s:
                ss_ref[...] = summed
            else:
                high = summed.astype(BF)
                theirs_ref[:, total : total + HD] = high
                theirs_ref[:, total + HD :] = (summed - high.astype(F32)).astype(BF)

    w = w_ref[...]
    mine_ref[...] = dot(own_s[...], w)
    theirs_ref[:, pl.ds(pl.multiple_of(step * width, width), width)] = dot(other_s[...], w).astype(BF)


def project(core, x, weight):
    sources, chip_tokens, _ = x.shape
    tokens = chip_tokens // 2
    depth, width = weight.shape
    block = 512
    return pl.pallas_call(
        project_kernel,
        grid_spec=pltpu.PrefetchScalarGridSpec(
            num_scalar_prefetch=1,
            grid=(width // block,),
            in_specs=[
                pl.BlockSpec(x.shape, lambda i, c: (0, 0, 0)),
                pl.BlockSpec((depth, block), lambda i, c: (0, i)),
            ],
            out_specs=[
                pl.BlockSpec((tokens, block), lambda i, c: (0, i)),
                pl.BlockSpec((tokens, HD), lambda i, c: (0, 0)),
                pl.BlockSpec((tokens, width + 2 * HD), lambda i, c: (0, 0)),
            ],
            scratch_shapes=[pltpu.VMEM((tokens, depth), BF)] * 2,
        ),
        out_shape=[
            jax.ShapeDtypeStruct((tokens, width), F32),
            jax.ShapeDtypeStruct((tokens, HD), F32),
            jax.ShapeDtypeStruct((tokens, width + 2 * HD), BF),
        ],
        compiler_params=params(),
    )(core, x, weight)


def norm_pack_kernel(
    mine_ref, ss_ref, got_ref, residual_ref, gain_ref, routes_ref,
    hidden_ref, main_ref, tail_ref, rank_s, table_s,
):
    step = pl.program_id(0)

    @pl.when(step == 0)
    def _():
        width = mine_ref.shape[1]
        squares = (
            ss_ref[...]
            + got_ref[:, width : width + HD].astype(F32)
            + got_ref[:, width + HD :].astype(F32)
        )[:, :1]
        inverse = lax.rsqrt(squares / (HEADS * HD) + EPS)
        projected = (mine_ref[...] + got_ref[:, :width].astype(F32)) * inverse
        hidden = (residual_ref[...].astype(F32) + projected).astype(BF)
        hidden_ref[...] = hidden
        wide = hidden.astype(F32)
        scale = lax.rsqrt(jnp.mean(wide * wide, axis=1, keepdims=True) + EPS)
        table_s[...] = (wide * scale * gain_ref[...].astype(F32)).astype(BF)
        rank_s[...] = ranks(routes_ref[...], expander())

    size = EXPERTS * MAIN // BLOCKS
    main, tail, quarter = picks(rank_s[pl.ds(step * size, size), :])
    table = table_s[...]
    main_ref[...] = dot(jnp.where(main, 1.0, 0.0).astype(BF), table).astype(BF)
    tail_ref[...] = tail_rows(tail, quarter, table).astype(BF)


def norm_pack(mine, squares, got, residual, gain, routes_t):
    tokens, width = residual.shape
    specs, shapes = packed_shapes(width)
    args = (mine, squares, got, residual, gain, routes_t)
    return pl.pallas_call(
        norm_pack_kernel,
        grid=(BLOCKS,),
        in_specs=[whole(a) for a in args],
        out_specs=[pl.BlockSpec((tokens, width), lambda i: (0, 0))] + specs,
        out_shape=[jax.ShapeDtypeStruct((tokens, width), BF)] + shapes,
        scratch_shapes=[
            pltpu.VMEM((EXPERTS * MAIN, tokens), F32),
            pltpu.VMEM((tokens, width), BF),
        ],
        compiler_params=params(),
    )(*args)


def untail(tail):
    sources, rows, width = tail.shape
    split = tail.reshape(sources, QUART, TAIL, width).transpose(0, 2, 1, 3)
    return split.reshape(sources * TAIL, QUART * width)


def expert_grads(rows_in, scaled, gate_mat, up_mat, down_mat):
    gate_pre = dot(rows_in, gate_mat)
    up_pre = dot(rows_in, up_mat)
    sigmoid_gate = jax.nn.sigmoid(gate_pre)
    active = gate_pre * sigmoid_gate
    hidden_units = (active * up_pre).astype(BF)
    grad_down = dot(hidden_units, scaled, 0, 0).astype(BF)
    grad_hidden = dot(scaled, down_mat, 1, 1)
    silu_slope = sigmoid_gate * (1.0 + gate_pre * (1.0 - sigmoid_gate))
    grad_pre_gate = (grad_hidden * up_pre * silu_slope).astype(BF)
    grad_pre_up = (grad_hidden * active).astype(BF)
    grad_gate = dot(rows_in, grad_pre_gate, 0, 0).astype(BF)
    grad_up = dot(rows_in, grad_pre_up, 0, 0).astype(BF)
    return (grad_gate, grad_up, grad_down)


def exchange(array, axes):
    return lax.all_to_all(array, axes, split_axis=0, concat_axis=0, tiled=True)


def on_device(
    queries, key_heads, value_heads, out_gain, out_weight, residual, norm_gain,
    routes, route_weights, cotangent, w_gate, w_up, w_down,
):
    n_ctx = lax.axis_size("ctx")
    n_chip = lax.axis_size("chip")
    width = residual.shape[1]
    at = lax.axis_index("ctx").astype(jnp.int32).reshape(1)
    core = lax.axis_index("core").astype(jnp.int32).reshape(1)

    scaled_weight = (out_weight.astype(F32) * out_gain.astype(F32)[:, None]).astype(BF)
    weight = lax.all_gather(scaled_weight, "chip", axis=0, tiled=True)

    states = exchange(span_states(key_heads, value_heads, n_ctx), "ctx")
    routes_t = routes.T
    cot_main, cot_tail = pack_cot(routes_t, route_weights.T, cotangent)
    attention = attend(at, queries, key_heads, value_heads, states)
    by_chip = exchange(attention.reshape(n_chip, -1, HD), "chip")
    cot_main = exchange(cot_main.reshape(EXPERTS, MAIN, width), ALL)
    cot_tail = exchange(cot_tail.reshape(EXPERTS, MAIN, width // QUART), ALL)

    mine, squares, theirs = project(core, by_chip, weight)
    got = lax.ppermute(theirs, "core", [(0, 1), (1, 0)])
    hidden_out, moe_main, moe_tail = norm_pack(
        mine, squares, got, residual, norm_gain[None], routes_t
    )
    moe_main = exchange(moe_main.reshape(EXPERTS, MAIN, width), ALL)
    moe_tail = exchange(moe_tail.reshape(EXPERTS, MAIN, width // QUART), ALL)

    rows_in = jnp.concatenate([moe_main.reshape(-1, width), untail(moe_tail)], axis=0)
    scaled = jnp.concatenate([cot_main.reshape(-1, width), untail(cot_tail)], axis=0)
    grads = expert_grads(rows_in, scaled, w_gate[0], w_up[0], w_down[0])
    return (hidden_out,) + tuple(g[None] for g in grads)


def solution(mesh):
    n_ctx, n_head = mesh.devices.shape
    fine = Mesh(mesh.devices.reshape(n_ctx, n_head // 2, 2), ALL)
    head = ("chip", "core")
    in_specs = (
        P("ctx", head), P("ctx", head), P("ctx", head), P(head), P(head, None),
        P(ALL, None), P(), P(ALL, None), P(ALL, None), P(ALL, None),
        P(ALL, None, None), P(ALL, None, None), P(ALL, None, None),
    )
    out_specs = (P(ALL, None), P(ALL, None, None), P(ALL, None, None), P(ALL, None, None))
    return jax.shard_map(
        on_device, mesh=fine, in_specs=in_specs, out_specs=out_specs, check_vma=False
    )
```

time: 437 us -> 300 us (0.69); the launches traced: 431 us -> 299 us
  local copies, waits for them, and re-layouts: 105 us -> 5.47 us
  waiting for transfers between devices: 0.04 us -> 97.5 us
  blocking collectives: 140 us -> 63.8 us
  matrix products: 112 us -> 49.7 us
  other arithmetic: 47.2 us -> 2.89 us
  Pallas kernels: 0 us -> 28.1 us
  starting transfers between devices: 11.8 us -> 37.8 us
    all_to_all x1 -> x2, blocking collectives: 130 us -> 63.8 us  [exchange(): return lax.all_to_all(array, axes, split_axis=0, concat_axis=0, tiled=True)]
    dot_general x50 -> x6, matrix products: 112 us -> 49.7 us  [dot(): lax.dot_general(a, b, (((ca,), (cb,)), ((), ())), preferred_element_type=...]
    all_to_all x1 -> x4, waiting for transfers between devices: 0.01 us -> 52.3 us  [exchange(): return lax.all_to_all(array, axes, split_axis=0, concat_axis=0, tiled=True)]
    all_gather x1, waiting for transfers between devices: 0.02 us -> 43.9 us  [on_device(): weight = lax.all_gather(scaled_weight, 'chip', axis=0, tiled=True)]
    gather x3 -> x0, local copies, waits for them, and re-layouts: 28.8 us -> none  [the longest x1 11.9 us: on_device(): moe_in[token_index]]
    pallas_call x0 -> x5, Pallas kernels: none -> 28.1 us  [the longest x1 7.05 us: project(): pl.pallas_call(project_kernel, grid_spec=pltpu.PrefetchScalarGridSpec(num...]
    reduce_sum x13 -> x0, other arithmetic: 21 us -> none  [the longest x8 7.92 us: one_block(): running_keys = running_keys + jnp.sum(key_block.astype(jnp.float32), axis=0)]
    concatenate x1 -> x0, local copies, waits for them, and re-layouts: 20 us -> none  [sent_together(): both = jnp.concatenate(arrays, axis=along)]
  transfers between devices with their start and end apart: 2 -> 6, of which waited for: 0 -> 5; matrix products, arithmetic and copies ran while one was open for 23% -> 4% of each run, Pallas kernels for 0% -> 9%
where the time goes in v1:
time: 300 us; the launch traced here: 299 us
  waiting for transfers between devices  97.5 us (32%)
  blocking collectives  63.8 us (21%)
  matrix products  49.7 us (17%)
  starting transfers between devices  37.8 us (13%)
  Pallas kernels  28.1 us (9%)
  between operations  14.2 us (5%)
  local copies, waits for them, and re-layouts  5.47 us (2%)
    all_to_all x2, blocking collectives, exchange(): return lax.all_to_all(array, axes, split_axis=0, concat_axis=0, tiled=True)  63.8 us
    all_to_all x4, waiting for transfers between devices, exchange(): return lax.all_to_all(array, axes, split_axis=0, concat_axis=0, tiled=True)  52.3 us
    dot_general x6, matrix products, dot(): lax.dot_general(a, b, (((ca,), (cb,)), ((), ())), preferred_element_type=...  49.7 us
    all_gather x1, waiting for transfers between devices, on_device(): weight = lax.all_gather(scaled_weight, 'chip', axis=0, tiled=True)  43.9 us
    all_to_all x4, starting transfers between devices, exchange(): return lax.all_to_all(array, axes, split_axis=0, concat_axis=0, tiled=True)  31.4 us
    pallas_call x1, Pallas kernels, project(): pl.pallas_call(project_kernel, grid_spec=pltpu.PrefetchScalarGridSpec(num...  7.05 us
    ppermute x1, starting transfers between devices, on_device(): got = lax.ppermute(theirs, 'core', [(0, 1), (1, 0)])  6.33 us
  transfers between devices with their start and end apart: 6, of which 5 were waited for; matrix products, arithmetic and copies ran while one was open for 4% of the time, Pallas kernels for 9%

profile of v1, /device:TPU:1, one launch (start us, length us, event | category | flops | bytes accessed | tf_op | source)
XLA Modules:
  0.0 299.4 jit_solution(2174212409373389836)
XLA Ops:
  7.2 0.8 convert_element_type.28
  8.0 2.1 multiply_convert_fusion.6
  10.1 3.9 %shard_map.156 = bf16[4,128,256]{2,1,0:T(8,128)(2,1)} custom-call(bf16[4096,128]{1,0:T(8,128)(2,1)} %k_ref.3, bf16[4096,128]{1,0:T(8,128)(2,1)} %v_ref.3), custom_call_target="tpu_custom_call" | custom-call | tf_op jit(solution)/shard_map/pallas_call | solution.py:54
  14.0 5.0 %all-to-all-start = ((bf16[4,128,256]{2,1,0:T(8,128)(2,1)}), bf16[4,128,256]{2,1,0:T(8,128)(2,1)S(1)}, u32[]{:S(2)}, u32[]{:S(2)}) async-start(bf16[4,128,256]{2,1,0:T(8,128)(2,1)} %shard_map.156), calls=%async_computation | async-start | bytes 524288 | tf_op jit(solution)/shard_map/all_to_all | solution.py:343
  19.0 5.4 %shard_map.160 = (bf16[1024,2048]{1,0:T(8,128)(2,1)}, bf16[1024,512]{1,0:T(8,128)(2,1)}) custom-call(s32[8,128]{1,0:T(8,128)} %bitcast.53, f32[8,128]{1,0:T(8,128)} %bitcast.55, bf16[128,2048]{1,0:T(8,128)(2,1)} %cot_ref.1), custom_call_target="tpu_custom_call" | custom-call | tf_op jit(solution)/shard_map/pallas_call | solution.py:202
  24.6 11.6 %all-to-all-start.5 = ((bf16[128,8,512]{2,1,0:T(8,128)(2,1)}), bf16[128,8,512]{2,1,0:T(8,128)(2,1)}, u32[]{:S(2)}, u32[]{:S(2)}) async-start(bf16[128,8,512]{2,1,0:T(8,128)(2,1)} %bitcast.45), calls=%async_computation.5 | async-start | bytes 2097152 | tf_op jit(solution)/shard_map/all_to_all | solution.py:343
  36.2 5.9 %shard_map.157 = bf16[4096,128]{1,0:T(8,128)(2,1)} custom-call(s32[1]{0:T(128)} %bitcast.1.at_ref, bf16[4096,128]{1,0:T(8,128)(2,1)} %q_ref.1, bf16[4096,128]{1,0:T(8,128)(2,1)} %k_ref.3, bf16[4096,128]{1,0:T(8,128)(2,1)} %v_ref.3, bf16[4,128,256]{2,1,0:T(8,128)(2,1)} %copy-done.3), custom_call_target="tpu_custom_call" | custom-call | tf_op jit(solution)/shard_map/pallas_call | solution.py:96
  42.1 12.8 %all-to-all-done.5 = bf16[128,8,512]{2,1,0:T(8,128)(2,1)} async-done(((bf16[128,8,512]{2,1,0:T(8,128)(2,1)}), bf16[128,8,512]{2,1,0:T(8,128)(2,1)}, u32[]{:S(2)}, u32[]{:S(2)}) %all-to-all-start.5) | async-done | bytes 1048608 | tf_op jit(solution)/shard_map/all_to_all | solution.py:343
  54.9 29.9 %all_to_all.30.x_ref = bf16[16,256,128]{2,1,0:T(8,128)(2,1)} all-to-all(bf16[16,256,128]{2,1,0:T(8,128)(2,1)} %bitcast.38), channel_id=1, replica_groups=mesh['ctx'=4,'chip'=16,'core'=2] {'chip'}, dimensions={0} | all-to-all | bytes 2097152 | tf_op jit(solution)/shard_map/all_to_all | solution.py:343
  84.8 8.8 %all-to-all-start.4 = ((bf16[128,8,2048]{2,1,0:T(8,128)(2,1)}), bf16[128,8,2048]{2,1,0:T(8,128)(2,1)}, u32[]{:S(2)}, u32[]{:S(2)}) async-start(bf16[128,8,2048]{2,1,0:T(8,128)(2,1)} %bitcast.39), calls=%async_computation.4 | async-start | bytes 8388608 | tf_op jit(solution)/shard_map/all_to_all | solution.py:343
  93.5 43.9 %all-gather.2.cloned.1.call-done.w_ref = bf16[2048,2048]{1,0:T(8,128)(2,1)} async-done(((bf16[128,2048]{1,0:T(8,128)(2,1)}), bf16[2048,2048]{1,0:T(8,128)(2,1)}) %all-gather.2.cloned.1.call-update) | async-done | bytes 8388624 | tf_op jit(solution)/shard_map/all_gather | solution.py:357
  137.5 7.0 %shard_map.158 = (f32[128,2048]{1,0:T(8,128)}, f32[128,128]{1,0:T(8,128)}, bf16[128,2304]{1,0:T(8,128)(2,1)}) custom-call(s32[1]{0:T(128)} %bitcast.core_ref, bf16[16,256,128]{2,1,0:T(8,128)(2,1)} %all_to_all.30.x_ref, bf16[2048,2048]{1,0:T(8,128)(2,1)} %all-gather.2.cloned.1.call-done.w_ref), custom_call_target="tpu_custom_call" | custom-call | tf_op jit(solution)/shard_map/pallas_call | solution.py:247
  144.5 6.3 %collective-permute-start = (bf16[128,2304]{1,0:T(8,128)(2,1)}, bf16[128,2304]{1,0:T(8,128)(2,1)S(1)}, u32[]{:S(2)}, u32[]{:S(2)}) collective-permute-start(bf16[128,2304]{1,0:T(8,128)(2,1)} %get-tuple-element.14), channel_id=1, source_target_pairs={{0,1},{1,0},{2,3},{3,2},{4,5},{5,4},{6,7},{7,6},{8,9},{9,8},{10,11... | collective-permute-start | bytes 1769480 | tf_op jit(solution)/shard_map/ppermute | solution.py:368
  150.8 0.6 broadcast_in_dim.13.gain_ref
  151.4 1.2 collective-permute-done.got_ref
  152.7 0.8 copy-done.7
  153.5 5.8 %shard_map.159 = (bf16[128,2048]{1,0:T(8,128)(2,1)}, bf16[1024,2048]{1,0:T(8,128)(2,1)}, bf16[1024,512]{1,0:T(8,128)(2,1)}) custom-call(f32[128,2048]{1,0:T(8,128)} %get-tuple-element.12.mine_ref, f32[128,128]{1,0:T(8,128)} %get-tuple-element.13.ss_ref, bf16[128,2304]{1,0:T(8,128)(2,1)} %copy-done.7, bf16[128,2048]{1,0:T(8,128)(2,1)} %residual_ref.1, ...), custom_call_target="tpu_custom_call" | custom-call | tf_op jit(solution)/shard_map/pallas_call | solution.py:306
  159.3 33.9 %all_to_all.31 = bf16[128,8,512]{2,1,0:T(8,128)(2,1)} all-to-all(bf16[128,8,512]{2,1,0:T(8,128)(2,1)} %bitcast.52), channel_id=1, replica_groups=mesh['ctx'=4,'chip'=16,'core'=2] {'ctx','chip','core'}, dimensions={0} | all-to-all | bytes 2097152 | tf_op jit(solution)/shard_map/all_to_all | solution.py:343
  193.2 6.0 %all-to-all-start.2 = ((bf16[128,8,2048]{2,1,0:T(8,128)(2,1)}), bf16[128,8,2048]{2,1,0:T(8,128)(2,1)}, u32[]{:S(2)}, u32[]{:S(2)}) async-start(bf16[128,8,2048]{2,1,0:T(8,128)(2,1)} %bitcast.40), calls=%async_computation.2 | async-start | bytes 8388608 | tf_op jit(solution)/shard_map/all_to_all | solution.py:343
  199.2 1.5 copy.23
  200.8 0.8 copy.24
  201.6 0.3 copy.26
  201.9 8.7 %fusion.1 = f32[1280,768]{1,0:T(8,128)} fusion(bf16[256,2048]{1,0:T(8,128)(2,1)S(1)} %bitcast.46, bf16[1024,2048]{1,0:T(8,128)(2,1)} %bitcast.11, bf16[1,768,2048]{2,1,0:T(8,128)(2,1)S(1)} %copy-done), kind=kOutput, calls=%fused_computation.10 | convolution fusion | flops 4037017600 | bytes 12320768 | tf_op jit(solution)/shard_map/dot_general | solution.py:27
  210.6 0.3 copy.21
  210.9 0.8 copy.22
  211.8 0.3 copy.25
  212.0 39.4 %all-to-all-done.2 = bf16[128,8,2048]{2,1,0:T(8,128)(2,1)} async-done(((bf16[128,8,2048]{2,1,0:T(8,128)(2,1)}), bf16[128,8,2048]{2,1,0:T(8,128)(2,1)}, u32[]{:S(2)}, u32[]{:S(2)}) %all-to-all-start.2) | async-done | bytes 4194336 | tf_op jit(solution)/shard_map/all_to_all | solution.py:343
  251.4 7.6 %fusion.2 = f32[1280,768]{1,0:T(8,128)S(1)} fusion(bf16[1,2048,768]{2,1,0:T(8,128)(2,1)} %param.23, bf16[256,2048]{1,0:T(8,128)(2,1)S(1)} %bitcast.48, bf16[1024,2048]{1,0:T(8,128)(2,1)} %bitcast.5), kind=kOutput, calls=%fused_computation.11 | convolution fusion | flops 4037017600 | bytes 12320768 | tf_op jit(solution)/shard_map/dot_general | solution.py:27
  259.0 6.8 %fusion.4 = f32[1280,768]{1,0:T(8,128)S(1)} fusion(bf16[1,2048,768]{2,1,0:T(8,128)(2,1)S(1)} %copy-done.9, bf16[256,2048]{1,0:T(8,128)(2,1)S(1)} %bitcast.49, bf16[1024,2048]{1,0:T(8,128)(2,1)} %bitcast.5), kind=kOutput, calls=%fused_computation.13 | convolution fusion | flops 4037017600 | bytes 12320768 | tf_op jit(solution)/shard_map/dot_general | solution.py:27
  265.9 8.6 %fusion.9 = bf16[1,768,2048]{2,1,0:T(8,128)(2,1)} fusion(bf16[256,2048]{1,0:T(8,128)(2,1)S(1)} %bitcast.47, bf16[1024,2048]{1,0:T(8,128)(2,1)} %bitcast.11, f32[1280,768]{1,0:T(8,128)S(1)} %fusion.4, f32[1280,768]{1,0:T(8,128)S(1)} %fusion.2), kind=kOutput, calls=%fused_computation.18 | convolution fusion | flops 4044488704 | bytes 16252928 | tf_op jit(solution)/shard_map/dot_general | solution.py:27
  274.5 8.7 %fusion.7 = bf16[1,2048,768]{2,1,0:T(8,128)(2,1)} fusion(f32[1280,768]{1,0:T(8,128)S(1)} %fusion.2, f32[1280,768]{1,0:T(8,128)S(1)} %copy-done.10, f32[1280,768]{1,0:T(8,128)S(1)} %fusion.4, bf16[256,2048]{1,0:T(8,128)(2,1)S(1)} %bitcast.50, bf16[1024,2048]{1,0:T(8,128)(2,1)} %bitcast.5), kind=kOutput, calls=%fused_computation.16 | convolution fusion | flops 4048420864 | bytes 20185088 | tf_op jit(solution)/shard_map/dot_general | solution.py:27
  283.2 9.3 %fusion.8 = bf16[1,2048,768]{2,1,0:T(8,128)(2,1)} fusion(f32[1280,768]{1,0:T(8,128)S(1)} %copy-done.10, f32[1280,768]{1,0:T(8,128)S(1)} %fusion.2, bf16[256,2048]{1,0:T(8,128)(2,1)} %bitcast.51, bf16[1024,2048]{1,0:T(8,128)(2,1)} %bitcast.5), kind=kOutput, calls=%fused_computation.17 | convolution fusion | flops 4044488704 | bytes 16252928 | tf_op jit(solution)/shard_map/dot_general | solution.py:27
  (25 shorter events, 0.3 us)
Async XLA Ops:
  7.2 194.7 %copy-start = (bf16[1,768,2048]{2,1,0:T(8,128)(2,1)S(1)}, bf16[1,768,2048]{2,1,0:T(8,128)(2,1)}, u32[]{:S(2)}) copy-start(bf16[1,768,2048]{2,1,0:T(8,128)(2,1)} %param.25) | copy-start | bytes 9437188
  7.2 130.3 %all-gather.2.cloned.1.call-start = ((), (), s32[]{:S(2)}) async-start(), calls=%async_computation.6 | async-start | bytes 8912896 | tf_op jit(solution)/shard_map/all_gather | solution.py:357
  14.0 10.6 %all-to-all-start = ((bf16[4,128,256]{2,1,0:T(8,128)(2,1)}), bf16[4,128,256]{2,1,0:T(8,128)(2,1)S(1)}, u32[]{:S(2)}, u32[]{:S(2)}) async-start(bf16[4,128,256]{2,1,0:T(8,128)(2,1)} %shard_map.156), calls=%async_computation | async-start | bytes 524288 | tf_op jit(solution)/shard_map/all_to_all | solution.py:343
  24.6 11.6 %copy-start.3 = (bf16[4,128,256]{2,1,0:T(8,128)(2,1)}, bf16[4,128,256]{2,1,0:T(8,128)(2,1)S(1)}, u32[]{:S(2)}) copy-start(bf16[4,128,256]{2,1,0:T(8,128)(2,1)S(1)} %all-to-all-done.s_ref) | copy-start | bytes 786436
  24.6 30.3 %all-to-all-start.5 = ((bf16[128,8,512]{2,1,0:T(8,128)(2,1)}), bf16[128,8,512]{2,1,0:T(8,128)(2,1)}, u32[]{:S(2)}, u32[]{:S(2)}) async-start(bf16[128,8,512]{2,1,0:T(8,128)(2,1)} %bitcast.45), calls=%async_computation.5 | async-start | bytes 2097152 | tf_op jit(solution)/shard_map/all_to_all | solution.py:343
  84.8 74.6 %all-to-all-start.4 = ((bf16[128,8,2048]{2,1,0:T(8,128)(2,1)}), bf16[128,8,2048]{2,1,0:T(8,128)(2,1)}, u32[]{:S(2)}, u32[]{:S(2)}) async-start(bf16[128,8,2048]{2,1,0:T(8,128)(2,1)} %bitcast.39), calls=%async_computation.4 | async-start | bytes 8388608 | tf_op jit(solution)/shard_map/all_to_all | solution.py:343
  137.5 13.4 %copy-start.8 = (bf16[2048]{0:T(1024)(128)(2,1)S(1)}, bf16[2048]{0:T(1024)(128)(2,1)}, u32[]{:S(2)}) copy-start(bf16[2048]{0:T(1024)(128)(2,1)} %param.19) | copy-start | bytes 12292
  144.5 8.2 %collective-permute-start = (bf16[128,2304]{1,0:T(8,128)(2,1)}, bf16[128,2304]{1,0:T(8,128)(2,1)S(1)}, u32[]{:S(2)}, u32[]{:S(2)}) collective-permute-start(bf16[128,2304]{1,0:T(8,128)(2,1)} %get-tuple-element.14), channel_id=1, source_target_pairs={{0,1},{1,0},{2,3},{3,2},{4,5},{5,4},{6,7},{7,6},{8,9},{9,8},{10,11... | collective-permute-start | bytes 1769480 | tf_op jit(solution)/shard_map/ppermute | solution.py:368
  152.7 0.8 copy-start.7
  193.2 58.2 %all-to-all-start.2 = ((bf16[128,8,2048]{2,1,0:T(8,128)(2,1)}), bf16[128,8,2048]{2,1,0:T(8,128)(2,1)}, u32[]{:S(2)}, u32[]{:S(2)}) async-start(bf16[128,8,2048]{2,1,0:T(8,128)(2,1)} %bitcast.40), calls=%async_computation.2 | async-start | bytes 8388608 | tf_op jit(solution)/shard_map/all_to_all | solution.py:343
  201.9 8.8 %copy-start.4 = (bf16[32,8,4,512]{3,1,2,0:T(8,128)(2,1)}, bf16[32,8,4,512]{3,1,2,0:T(8,128)(2,1)S(1)}, u32[]{:S(2)}) copy-start(bf16[32,8,4,512]{3,1,2,0:T(8,128)(2,1)S(1)} %copy.26) | copy-start | bytes 3145732
  201.9 8.7 %copy-start.2 = (bf16[128,8,512]{2,1,0:T(8,128)(2,1)S(1)}, bf16[128,8,512]{2,1,0:T(8,128)(2,1)}, u32[]{:S(2)}) copy-start(bf16[128,8,512]{2,1,0:T(8,128)(2,1)} %all_to_all.31) | copy-start | bytes 3145732
  212.0 62.5 %copy-start.6 = (bf16[32,8,4,512]{3,1,2,0:T(8,128)(2,1)}, bf16[32,8,4,512]{3,1,2,0:T(8,128)(2,1)S(1)}, u32[]{:S(2)}) copy-start(bf16[32,8,4,512]{3,1,2,0:T(8,128)(2,1)S(1)} %copy.25) | copy-start | bytes 3145732
  251.4 7.6 %copy-start.9 = (bf16[1,2048,768]{2,1,0:T(8,128)(2,1)S(1)}, bf16[1,2048,768]{2,1,0:T(8,128)(2,1)}, u32[]{:S(2)}) copy-start(bf16[1,2048,768]{2,1,0:T(8,128)(2,1)} %param.24) | copy-start | bytes 9437188
  259.0 6.9 %copy-start.5 = (bf16[32,8,4,512]{3,1,2,0:T(8,128)(2,1)S(1)}, bf16[32,8,4,512]{3,1,2,0:T(8,128)(2,1)}, u32[]{:S(2)}) copy-start(bf16[32,8,4,512]{3,1,2,0:T(8,128)(2,1)} %copy-done.4) | copy-start | bytes 3145732
  265.9 8.6 %copy-start.10 = (f32[1280,768]{1,0:T(8,128)S(1)}, f32[1280,768]{1,0:T(8,128)}, u32[]{:S(2)}) copy-start(f32[1280,768]{1,0:T(8,128)} %fusion.1) | copy-start | bytes 11796484
  283.2 9.3 %copy-start.1 = (bf16[1,768,2048]{2,1,0:T(8,128)(2,1)S(1)}, bf16[1,768,2048]{2,1,0:T(8,128)(2,1)}, u32[]{:S(2)}) copy-start(bf16[1,768,2048]{2,1,0:T(8,128)(2,1)} %param.25) | copy-start | bytes 9437188
Sparse Core Ops, SparseCore 0:
  10.7 126.7 all-gather.1

commit v2 on v1

--- a/solution.py
+++ b/solution.py
@@ -63,9 +63,10 @@
 
 
 CHUNK = 256
-
-
-def attend_kernel(at_ref, q_ref, k_ref, v_ref, s_ref, o_ref, state):
+EXTRA = 16
+
+
+def attend_kernel(at_ref, q_ref, k_ref, v_ref, s_ref, g_ref, o_ref, state):
     @pl.when(pl.program_id(0) == 0)
     def _():
         total = jnp.zeros(state.shape, F32)
@@ -76,6 +77,9 @@
     rows = lax.broadcasted_iota(jnp.int32, (CHUNK, CHUNK), 0)
     cols = lax.broadcasted_iota(jnp.int32, (CHUNK, CHUNK), 1)
     run = state[...]
+    per_chip = o_ref.shape[1] - EXTRA
+    for c in range(o_ref.shape[0]):
+        o_ref[c, per_chip:, :] = jnp.broadcast_to(g_ref[...], (EXTRA, HD))
     for n in range(q_ref.shape[0] // CHUNK):
         part = pl.ds(n * CHUNK, CHUNK)
         qf = phi(q_ref[part, :])
@@ -84,27 +88,28 @@
         v1 = jnp.concatenate([v, jnp.ones_like(v)], axis=1)
         scores = jnp.where(rows >= cols, dot(qf, kf, 1, 1), 0.0).astype(BF)
         both = dot(scores, v1) + dot(qf, run.astype(BF))
-        o_ref[part, :] = (both[:, :HD] / both[:, HD:]).astype(BF)
+        o_ref[n, :per_chip, :] = (both[:, :HD] / both[:, HD:]).astype(BF)
         run = run + dot(kf, v1, 0, 0)
     state[...] = run
 
 
-def attend(at, queries, keys, values, states):
+def attend(at, queries, keys, values, states, gain):
     length = queries.shape[0]
     block = min(1024, length)
+    each = block // CHUNK
     tok = pl.BlockSpec((block, HD), lambda i, at: (i, 0))
     return pl.pallas_call(
         attend_kernel,
         grid_spec=pltpu.PrefetchScalarGridSpec(
             num_scalar_prefetch=1,
             grid=(length // block,),
-            in_specs=[tok, tok, tok, pl.BlockSpec(states.shape, lambda i, at: (0, 0, 0))],
-            out_specs=tok,
+            in_specs=[tok, tok, tok, whole(states), whole(gain)],
+            out_specs=pl.BlockSpec((each, CHUNK + EXTRA, HD), lambda i, at: (i, 0, 0)),
             scratch_shapes=[pltpu.VMEM((HD, 2 * HD), F32)],
         ),
-        out_shape=jax.ShapeDtypeStruct(queries.shape, BF),
-        compiler_params=params(),
-    )(at, queries, keys, values, states)
+        out_shape=jax.ShapeDtypeStruct((length // CHUNK, CHUNK + EXTRA, HD), BF),
+        compiler_params=params(),
+    )(at, queries, keys, values, states, gain)
 
 
 def ranks(routes_t, expand):
@@ -146,7 +151,7 @@
 BLOCKS = 4
 
 
-def pack_cot_kernel(routes_ref, weights_ref, cot_ref, main_ref, tail_ref, rank_s, weight_s):
+def pack_cot_kernel(routes_ref, weights_ref, cot_ref, out_ref, rank_s, weight_s):
     step = pl.program_id(0)
 
     @pl.when(step == 0)
@@ -173,23 +178,17 @@
     main, tail, quarter = picks(rank_s[part, :])
     table = cot_ref[...]
     scale = jnp.sum(jnp.where(main, weight8, 0.0), axis=1, keepdims=True)
-    main_ref[...] = (dot(jnp.where(main, 1.0, 0.0).astype(BF), table) * scale).astype(BF)
+    width = table.shape[1]
+    out_ref[:, :width] = (dot(jnp.where(main, 1.0, 0.0).astype(BF), table) * scale).astype(BF)
     scale = jnp.sum(jnp.where(tail, weight8, 0.0), axis=1, keepdims=True)
-    tail_ref[...] = (tail_rows(tail, quarter, table) * scale).astype(BF)
-
-
-def packed_shapes(width):
+    out_ref[:, width:] = (tail_rows(tail, quarter, table) * scale).astype(BF)
+
+
+def packed(width):
     rows = EXPERTS * MAIN
-    size = rows // BLOCKS
-    specs = [
-        pl.BlockSpec((size, width), lambda i: (i, 0)),
-        pl.BlockSpec((size, width // QUART), lambda i: (i, 0)),
-    ]
-    shapes = [
-        jax.ShapeDtypeStruct((rows, width), BF),
-        jax.ShapeDtypeStruct((rows, width // QUART), BF),
-    ]
-    return specs, shapes
+    wide = width + width // QUART
+    spec = pl.BlockSpec((rows // BLOCKS, wide), lambda i: (i, 0))
+    return spec, jax.ShapeDtypeStruct((rows, wide), BF)
 
 
 def whole(array):
@@ -198,13 +197,13 @@
 
 def pack_cot(routes_t, weights_t, cotangent):
     tokens, width = cotangent.shape
-    specs, shapes = packed_shapes(width)
+    spec, shape = packed(width)
     return pl.pallas_call(
         pack_cot_kernel,
         grid=(BLOCKS,),
         in_specs=[whole(routes_t), whole(weights_t), whole(cotangent)],
-        out_specs=specs,
-        out_shape=shapes,
+        out_specs=spec,
+        out_shape=shape,
         scratch_shapes=[pltpu.VMEM((EXPERTS * MAIN, tokens), F32)] * 2,
         compiler_params=params(),
     )(routes_t, weights_t, cotangent)
@@ -223,8 +222,9 @@
             square = jnp.zeros((tokens, HD), F32)
             for s in range(x_ref.shape[0]):
                 piece = x_ref[s, pl.ds(pl.multiple_of(at * tokens, tokens), tokens), :]
-                keep[:, s * HD : (s + 1) * HD] = piece
                 wide = piece.astype(F32)
+                gain = x_ref[s, 2 * tokens : 2 * tokens + 1, :].astype(F32)
+                keep[:, s * HD : (s + 1) * HD] = (wide * gain).astype(BF)
                 square = square + wide * wide
             summed = jnp.broadcast_to(jnp.sum(square, axis=1, keepdims=True), (tokens, HD))
             if keep is own_s:
@@ -240,18 +240,19 @@
 
 
 def project(core, x, weight):
-    sources, chip_tokens, _ = x.shape
-    tokens = chip_tokens // 2
-    depth, width = weight.shape
-    block = 512
+    tokens = (x.shape[1] - EXTRA) // 2
+    depth = x.shape[0] * HD
+    block = weight.shape[1]
+    blocks = weight.shape[0] // depth
+    width = blocks * block
     return pl.pallas_call(
         project_kernel,
         grid_spec=pltpu.PrefetchScalarGridSpec(
             num_scalar_prefetch=1,
-            grid=(width // block,),
+            grid=(blocks,),
             in_specs=[
                 pl.BlockSpec(x.shape, lambda i, c: (0, 0, 0)),
-                pl.BlockSpec((depth, block), lambda i, c: (0, i)),
+                pl.BlockSpec((depth, block), lambda i, c: (i, 0)),
             ],
             out_specs=[
                 pl.BlockSpec((tokens, block), lambda i, c: (0, i)),
@@ -271,7 +272,7 @@
 
 def norm_pack_kernel(
     mine_ref, ss_ref, got_ref, residual_ref, gain_ref, routes_ref,
-    hidden_ref, main_ref, tail_ref, rank_s, table_s,
+    hidden_ref, out_ref, rank_s, table_s,
 ):
     step = pl.program_id(0)
 
@@ -295,20 +296,21 @@
     size = EXPERTS * MAIN // BLOCKS
     main, tail, quarter = picks(rank_s[pl.ds(step * size, size), :])
     table = table_s[...]
-    main_ref[...] = dot(jnp.where(main, 1.0, 0.0).astype(BF), table).astype(BF)
-    tail_ref[...] = tail_rows(tail, quarter, table).astype(BF)
+    width = table.shape[1]
+    out_ref[:, :width] = dot(jnp.where(main, 1.0, 0.0).astype(BF), table).astype(BF)
+    out_ref[:, width:] = tail_rows(tail, quarter, table).astype(BF)
 
 
 def norm_pack(mine, squares, got, residual, gain, routes_t):
     tokens, width = residual.shape
-    specs, shapes = packed_shapes(width)
+    spec, shape = packed(width)
     args = (mine, squares, got, residual, gain, routes_t)
     return pl.pallas_call(
         norm_pack_kernel,
         grid=(BLOCKS,),
         in_specs=[whole(a) for a in args],
-        out_specs=[pl.BlockSpec((tokens, width), lambda i: (0, 0))] + specs,
-        out_shape=[jax.ShapeDtypeStruct((tokens, width), BF)] + shapes,
+        out_specs=[pl.BlockSpec((tokens, width), lambda i: (0, 0)), spec],
+        out_shape=[jax.ShapeDtypeStruct((tokens, width), BF), shape],
         scratch_shapes=[
             pltpu.VMEM((EXPERTS * MAIN, tokens), F32),
             pltpu.VMEM((tokens, width), BF),
@@ -348,33 +350,31 @@
     routes, route_weights, cotangent, w_gate, w_up, w_down,
 ):
     n_ctx = lax.axis_size("ctx")
-    n_chip = lax.axis_size("chip")
     width = residual.shape[1]
     at = lax.axis_index("ctx").astype(jnp.int32).reshape(1)
     core = lax.axis_index("core").astype(jnp.int32).reshape(1)
 
-    scaled_weight = (out_weight.astype(F32) * out_gain.astype(F32)[:, None]).astype(BF)
-    weight = lax.all_gather(scaled_weight, "chip", axis=0, tiled=True)
-
+    strip = width // n_ctx
+    weight = lax.dynamic_slice_in_dim(out_weight, at[0] * strip, strip, 1)
+    weight = lax.all_gather(weight, ("ctx", "chip"), axis=0, tiled=True)
     states = exchange(span_states(key_heads, value_heads, n_ctx), "ctx")
     routes_t = routes.T
-    cot_main, cot_tail = pack_cot(routes_t, route_weights.T, cotangent)
-    attention = attend(at, queries, key_heads, value_heads, states)
-    by_chip = exchange(attention.reshape(n_chip, -1, HD), "chip")
-    cot_main = exchange(cot_main.reshape(EXPERTS, MAIN, width), ALL)
-    cot_tail = exchange(cot_tail.reshape(EXPERTS, MAIN, width // QUART), ALL)
+    cot = pack_cot(routes_t, route_weights.T, cotangent)
+    attention = attend(at, queries, key_heads, value_heads, states, out_gain[None])
+    by_chip = exchange(attention, "chip")
+    cot, by_chip = lax.optimization_barrier((cot, by_chip))
+    cot = exchange(cot.reshape(EXPERTS, MAIN, -1), ALL)
 
     mine, squares, theirs = project(core, by_chip, weight)
     got = lax.ppermute(theirs, "core", [(0, 1), (1, 0)])
-    hidden_out, moe_main, moe_tail = norm_pack(
-        mine, squares, got, residual, norm_gain[None], routes_t
-    )
-    moe_main = exchange(moe_main.reshape(EXPERTS, MAIN, width), ALL)
-    moe_tail = exchange(moe_tail.reshape(EXPERTS, MAIN, width // QUART), ALL)
-
-    rows_in = jnp.concatenate([moe_main.reshape(-1, width), untail(moe_tail)], axis=0)
-    scaled = jnp.concatenate([cot_main.reshape(-1, width), untail(cot_tail)], axis=0)
-    grads = expert_grads(rows_in, scaled, w_gate[0], w_up[0], w_down[0])
+    hidden_out, moe = norm_pack(mine, squares, got, residual, norm_gain[None], routes_t)
+    moe = exchange(moe.reshape(EXPERTS, MAIN, -1), ALL)
+
+    def rows(both):
+        main = both[:, :, :width].reshape(-1, width)
+        return jnp.concatenate([main, untail(both[:, :, width:])], axis=0)
+
+    grads = expert_grads(rows(moe), rows(cot), w_gate[0], w_up[0], w_down[0])
     return (hidden_out,) + tuple(g[None] for g in grads)
 
 

time: 300 us -> 288 us (0.960)
  blocking collectives: 63.8 us -> 10.7 us
  waiting for transfers between devices: 97.5 us -> 143 us
  local copies, waits for them, and re-layouts: 5.47 us -> 16.6 us
  starting transfers between devices: 37.8 us -> 26.8 us
  matrix products: 49.7 us -> 45.9 us
    all_to_all x2 -> x1, blocking collectives: 63.8 us -> 10.7 us  [exchange(): return lax.all_to_all(array, axes, split_axis=0, concat_axis=0, tiled=True)]
    all_gather x1, waiting for transfers between devices: 43.9 us -> 82 us  [on_device(): weight = lax.all_gather(weight, ('ctx', 'chip'), axis=0, tiled=True)]
    all_to_all x4 -> x3, waiting for transfers between devices: 52.3 us -> 60.1 us  [exchange(): return lax.all_to_all(array, axes, split_axis=0, concat_axis=0, tiled=True)]
    ppermute x1, starting transfers between devices: 6.33 us -> 0.56 us  [on_device(): got = lax.ppermute(theirs, 'core', [(0, 1), (1, 0)])]
    reshape x0 -> x2, local copies, waits for them, and re-layouts: none -> 5.53 us  [rows(): main = both[:, :, :width].reshape(-1, width)]
    all_to_all x4 -> x3, starting transfers between devices: 31.4 us -> 26.2 us  [exchange(): return lax.all_to_all(array, axes, split_axis=0, concat_axis=0, tiled=True)]
    dot_general x6, matrix products: 49.7 us -> 45.9 us  [dot(): lax.dot_general(a, b, (((ca,), (cb,)), ((), ())), preferred_element_type=...]
    slice x0 -> x4, local copies, waits for them, and re-layouts: none -> 3.21 us  [rows(): return jnp.concatenate([main, untail(both[:, :, width:])], axis=0)]
  transfers between devices with their start and end apart: 6 -> 5, of which waited for: 5 -> 4; matrix products, arithmetic and copies ran while one was open for 4% -> 4% of each run, Pallas kernels for 9% -> 10%
where the time goes in v2:
time: 288 us; the launch traced here: 287 us
  waiting for transfers between devices  143 us (50%)
  matrix products  45.9 us (16%)
  Pallas kernels  29.3 us (10%)
  starting transfers between devices  26.8 us (9%)
  local copies, waits for them, and re-layouts  16.6 us (6%)
  between operations  14.2 us (5%)
  blocking collectives  10.7 us (4%)
    all_gather x1, waiting for transfers between devices, on_device(): weight = lax.all_gather(weight, ('ctx', 'chip'), axis=0, tiled=True)  82 us
    all_to_all x3, waiting for transfers between devices, exchange(): return lax.all_to_all(array, axes, split_axis=0, concat_axis=0, tiled=True)  60.1 us
    dot_general x6, matrix products, dot(): lax.dot_general(a, b, (((ca,), (cb,)), ((), ())), preferred_element_type=...  45.9 us
    all_to_all x3, starting transfers between devices, exchange(): return lax.all_to_all(array, axes, split_axis=0, concat_axis=0, tiled=True)  26.2 us
    all_to_all x1, blocking collectives, exchange(): return lax.all_to_all(array, axes, split_axis=0, concat_axis=0, tiled=True)  10.7 us
    pallas_call x1, Pallas kernels, project(): pl.pallas_call(project_kernel, grid_spec=pltpu.PrefetchScalarGridSpec(num...  7.04 us
    pallas_call x1, Pallas kernels, norm_pack(): pl.pallas_call(norm_pack_kernel, grid=(BLOCKS,), in_specs=[whole(a) for a...  6.45 us
    pallas_call x1, Pallas kernels, pack_cot(): pl.pallas_call(pack_cot_kernel, grid=(BLOCKS,), in_specs=[whole(routes_t)...  6.04 us
  transfers between devices with their start and end apart: 5, of which 4 were waited for; matrix products, arithmetic and copies ran while one was open for 4% of the time, Pallas kernels for 10%

profile of v2, /device:TPU:1, one launch (start us, length us, event | category | flops | bytes accessed | tf_op | source)
XLA Modules:
  0.0 286.8 jit_solution(4670355704117631365)
XLA Ops:
  7.2 1.7 constant_dynamic-slice_fusion
  9.0 3.9 %shard_map.157 = bf16[4,128,256]{2,1,0:T(8,128)(2,1)} custom-call(bf16[4096,128]{1,0:T(8,128)(2,1)} %k_ref.3, bf16[4096,128]{1,0:T(8,128)(2,1)} %v_ref.3), custom_call_target="tpu_custom_call" | custom-call | tf_op jit(solution)/shard_map/pallas_call | solution.py:54
  12.9 10.7 %all_to_all.20.s_ref = bf16[4,128,256]{2,1,0:T(8,128)(2,1)} all-to-all(bf16[4,128,256]{2,1,0:T(8,128)(2,1)} %shard_map.157), channel_id=1, replica_groups=mesh['ctx'=4,'chip'=16,'core'=2] {'ctx'}, dimensions={0} | all-to-all | bytes 524288 | tf_op jit(solution)/shard_map/all_to_all | solution.py:345
  23.5 5.9 %shard_map.158 = bf16[16,272,128]{2,1,0:T(8,128)(2,1)} custom-call(s32[1]{0:T(128)} %bitcast.3.at_ref, bf16[4096,128]{1,0:T(8,128)(2,1)} %q_ref.1, bf16[4096,128]{1,0:T(8,128)(2,1)} %k_ref.3, bf16[4096,128]{1,0:T(8,128)(2,1)} %v_ref.3, bf16[4,128,256]{2,1,0:T(8,128)(2,1)} %all_to_all.20.s_ref, bf16[1,128]{1,0:T(2,128)(2,1)} %bitcast.53), custom_call_target="tpu_custom_call" | custom-call | tf_op jit(solution)/shard_map/pallas_call | solution.py:101
  29.4 7.7 %all-to-all-start.1 = ((bf16[16,272,128]{2,1,0:T(8,128)(2,1)}), bf16[16,272,128]{2,1,0:T(8,128)(2,1)}, u32[]{:S(2)}, u32[]{:S(2)}) async-start(bf16[16,272,128]{2,1,0:T(8,128)(2,1)} %shard_map.158), calls=%async_computation.1 | async-start | bytes 2228224 | tf_op jit(solution)/shard_map/all_to_all | solution.py:345
  37.1 6.0 %shard_map.156 = bf16[1024,2560]{1,0:T(8,128)(2,1)} custom-call(s32[8,128]{1,0:T(8,128)} %bitcast.50, f32[8,128]{1,0:T(8,128)} %bitcast.52, bf16[128,2048]{1,0:T(8,128)(2,1)} %cot_ref.1), custom_call_target="tpu_custom_call" | custom-call | tf_op jit(solution)/shard_map/pallas_call | solution.py:201
  43.1 10.5 %all-to-all-done.1.x_ref = bf16[16,272,128]{2,1,0:T(8,128)(2,1)} async-done(((bf16[16,272,128]{2,1,0:T(8,128)(2,1)}), bf16[16,272,128]{2,1,0:T(8,128)(2,1)}, u32[]{:S(2)}, u32[]{:S(2)}) %all-to-all-start.1) | async-done | bytes 1114144 | tf_op jit(solution)/shard_map/all_to_all | solution.py:345
  53.6 9.4 %all-to-all-start.3 = ((bf16[128,8,2560]{2,1,0:T(8,128)(2,1)}), bf16[128,8,2560]{2,1,0:T(8,128)(2,1)}, u32[]{:S(2)}, u32[]{:S(2)}) async-start(bf16[128,8,2560]{2,1,0:T(8,128)(2,1)} %bitcast.38), calls=%async_computation.3 | async-start | bytes 10485760 | tf_op jit(solution)/shard_map/all_to_all | solution.py:345
  63.1 82.0 %all-gather.2.cloned.1.call-done.w_ref = bf16[8192,512]{1,0:T(8,128)(2,1)} async-done(((bf16[128,512]{1,0:T(8,128)(2,1)}), bf16[8192,512]{1,0:T(8,128)(2,1)}) %all-gather.2.cloned.1.call-update) | async-done | bytes 8388624 | tf_op jit(solution)/shard_map/all_gather | solution.py:359
  145.1 7.0 %shard_map.159 = (f32[128,2048]{1,0:T(8,128)}, f32[128,128]{1,0:T(8,128)}, bf16[128,2304]{1,0:T(8,128)(2,1)}) custom-call(s32[1]{0:T(128)} %bitcast.core_ref, bf16[16,272,128]{2,1,0:T(8,128)(2,1)} %all-to-all-done.1.x_ref, bf16[8192,512]{1,0:T(8,128)(2,1)} %all-gather.2.cloned.1.call-done.w_ref), custom_call_target="tpu_custom_call" | custom-call | tf_op jit(solution)/shard_map/pallas_call | solution.py:248
  152.1 0.6 collective-permute-start
  152.7 0.6 broadcast_in_dim.16.gain_ref
  153.3 1.2 collective-permute-done.got_ref
  154.6 0.8 copy-done.6
  155.4 6.4 %shard_map.160 = (bf16[128,2048]{1,0:T(8,128)(2,1)}, bf16[1024,2560]{1,0:T(8,128)(2,1)}) custom-call(f32[128,2048]{1,0:T(8,128)} %get-tuple-element.12.mine_ref, f32[128,128]{1,0:T(8,128)} %get-tuple-element.13.ss_ref, bf16[128,2304]{1,0:T(8,128)(2,1)} %copy-done.6, bf16[128,2048]{1,0:T(8,128)(2,1)} %residual_ref.1, ...), custom_call_target="tpu_custom_call" | custom-call | tf_op jit(solution)/shard_map/pallas_call | solution.py:308
  161.8 9.1 %all-to-all-start.2 = ((bf16[128,8,2560]{2,1,0:T(8,128)(2,1)}), bf16[128,8,2560]{2,1,0:T(8,128)(2,1)}, u32[]{:S(2)}, u32[]{:S(2)}) async-start(bf16[128,8,2560]{2,1,0:T(8,128)(2,1)} %bitcast.39), calls=%async_computation.2 | async-start | bytes 10485760 | tf_op jit(solution)/shard_map/all_to_all | solution.py:345
  170.9 1.3 slice.19
  172.2 0.3 copy.23
  172.5 0.8 copy.24
  173.6 2.9 %slice_bitcast_fusion = bf16[1024,2048]{1,0:T(8,128)(2,1)S(1)} fusion(bf16[128,8,2560]{2,1,0:T(8,128)(2,1)} %all-to-all-done.3), kind=kLoop, calls=%fused_computation.2 | loop fusion | bytes 8388608 | tf_op jit(solution)/shard_map/reshape | solution.py:374
  176.5 2.0 copy-done.2
  178.6 6.4 %fusion.1 = f32[1280,768]{1,0:T(8,128)} fusion(bf16[256,2048]{1,0:T(8,128)(2,1)S(1)} %bitcast.44, bf16[1024,2048]{1,0:T(8,128)(2,1)S(1)} %slice_bitcast_fusion, bf16[1,768,2048]{2,1,0:T(8,128)(2,1)S(1)} %copy-done), kind=kOutput, calls=%fused_computation.12 | convolution fusion | flops 4037017600 | bytes 12320768 | tf_op jit(solution)/shard_map/dot_general | solution.py:27
  184.9 49.6 %all-to-all-done.2 = bf16[128,8,2560]{2,1,0:T(8,128)(2,1)} async-done(((bf16[128,8,2560]{2,1,0:T(8,128)(2,1)}), bf16[128,8,2560]{2,1,0:T(8,128)(2,1)}, u32[]{:S(2)}, u32[]{:S(2)}) %all-to-all-start.2) | async-done | bytes 5242912 | tf_op jit(solution)/shard_map/all_to_all | solution.py:345
  234.6 1.3 slice.17
  236.2 0.8 copy.22
  237.3 2.7 slice_bitcast_fusion.1
  239.9 0.5 copy-done.8
  240.4 6.1 %fusion.4 = f32[1280,768]{1,0:T(8,128)} fusion(bf16[1,2048,768]{2,1,0:T(8,128)(2,1)S(1)} %copy-done.8, bf16[256,2048]{1,0:T(8,128)(2,1)S(1)} %bitcast.46, bf16[1024,2048]{1,0:T(8,128)(2,1)S(1)} %slice_bitcast_fusion.1), kind=kOutput, calls=%fused_computation.15 | convolution fusion | flops 4037017600 | bytes 12320768 | tf_op jit(solution)/shard_map/dot_general | solution.py:27
  246.6 6.4 %fusion.2 = f32[1280,768]{1,0:T(8,128)} fusion(bf16[1,2048,768]{2,1,0:T(8,128)(2,1)S(1)} %copy-done.9, bf16[256,2048]{1,0:T(8,128)(2,1)S(1)} %bitcast.47, bf16[1024,2048]{1,0:T(8,128)(2,1)S(1)} %slice_bitcast_fusion.1), kind=kOutput, calls=%fused_computation.13 | convolution fusion | flops 4037017600 | bytes 12320768 | tf_op jit(solution)/shard_map/dot_general | solution.py:27
  253.0 9.4 %fusion.9 = bf16[1,768,2048]{2,1,0:T(8,128)(2,1)} fusion(bf16[256,2048]{1,0:T(8,128)(2,1)S(1)} %bitcast.45, bf16[1024,2048]{1,0:T(8,128)(2,1)S(1)} %copy-done.3, f32[1280,768]{1,0:T(8,128)} %fusion.4, f32[1280,768]{1,0:T(8,128)} %fusion.2), kind=kOutput, calls=%fused_computation.20 | convolution fusion | flops 4044488704 | bytes 16252928 | tf_op jit(solution)/shard_map/dot_general | solution.py:27
  262.4 8.6 %fusion.8 = bf16[1,2048,768]{2,1,0:T(8,128)(2,1)} fusion(f32[1280,768]{1,0:T(8,128)S(1)} %copy-done.10, f32[1280,768]{1,0:T(8,128)} %fusion.2, bf16[256,2048]{1,0:T(8,128)(2,1)S(1)} %bitcast.48, bf16[1024,2048]{1,0:T(8,128)(2,1)S(1)} %slice_bitcast_fusion.1), kind=kOutput, calls=%fused_computation.19 | convolution fusion | flops 4044488704 | bytes 16252928 | tf_op jit(solution)/shard_map/dot_general | solution.py:27
  271.0 8.9 %fusion.7 = bf16[1,2048,768]{2,1,0:T(8,128)(2,1)} fusion(f32[1280,768]{1,0:T(8,128)} %fusion.2, f32[1280,768]{1,0:T(8,128)S(1)} %copy-done.10, f32[1280,768]{1,0:T(8,128)S(1)} %copy-done.11, bf16[256,2048]{1,0:T(8,128)(2,1)S(1)} %bitcast.49, bf16[1024,2048]{1,0:T(8,128)(2,1)S(1)} %slice_bitcast_fusion.1), kind=kOutput, calls=%fused_computation.18 | convolution fusion | flops 4048420864 | bytes 20185088 | tf_op jit(solution)/shard_map/dot_general | solution.py:27
  (27 shorter events, 1.0 us)
Async XLA Ops:
  7.2 171.4 %copy-start = (bf16[1,768,2048]{2,1,0:T(8,128)(2,1)S(1)}, bf16[1,768,2048]{2,1,0:T(8,128)(2,1)}, u32[]{:S(2)}) copy-start(bf16[1,768,2048]{2,1,0:T(8,128)(2,1)} %param.25) | copy-start | bytes 9437188
  7.2 137.9 %all-gather.2.cloned.1.call-start = ((), (), s32[]{:S(2)}) async-start(), calls=%async_computation.4 | async-start | bytes 8519680 | tf_op jit(solution)/shard_map/all_gather | solution.py:359
  29.4 24.2 %all-to-all-start.1 = ((bf16[16,272,128]{2,1,0:T(8,128)(2,1)}), bf16[16,272,128]{2,1,0:T(8,128)(2,1)}, u32[]{:S(2)}, u32[]{:S(2)}) async-start(bf16[16,272,128]{2,1,0:T(8,128)(2,1)} %shard_map.158), calls=%async_computation.1 | async-start | bytes 2228224 | tf_op jit(solution)/shard_map/all_to_all | solution.py:345
  53.6 108.2 %all-to-all-start.3 = ((bf16[128,8,2560]{2,1,0:T(8,128)(2,1)}), bf16[128,8,2560]{2,1,0:T(8,128)(2,1)}, u32[]{:S(2)}, u32[]{:S(2)}) async-start(bf16[128,8,2560]{2,1,0:T(8,128)(2,1)} %bitcast.38), calls=%async_computation.3 | async-start | bytes 10485760 | tf_op jit(solution)/shard_map/all_to_all | solution.py:345
  145.1 7.6 %copy-start.7 = (bf16[2048]{0:T(1024)(128)(2,1)S(1)}, bf16[2048]{0:T(1024)(128)(2,1)}, u32[]{:S(2)}) copy-start(bf16[2048]{0:T(1024)(128)(2,1)} %param.19) | copy-start | bytes 12292
  152.1 2.4 collective-permute-start
  154.6 0.8 copy-start.6
  161.8 72.7 %all-to-all-start.2 = ((bf16[128,8,2560]{2,1,0:T(8,128)(2,1)}), bf16[128,8,2560]{2,1,0:T(8,128)(2,1)}, u32[]{:S(2)}, u32[]{:S(2)}) async-start(bf16[128,8,2560]{2,1,0:T(8,128)(2,1)} %bitcast.39), calls=%async_computation.2 | async-start | bytes 10485760 | tf_op jit(solution)/shard_map/all_to_all | solution.py:345
  173.6 2.9 %copy-start.4 = (bf16[32,8,4,512]{3,1,2,0:T(8,128)(2,1)}, bf16[32,8,4,512]{3,1,2,0:T(8,128)(2,1)S(1)}, u32[]{:S(2)}) copy-start(bf16[32,8,4,512]{3,1,2,0:T(8,128)(2,1)S(1)} %copy.26) | copy-start | bytes 3145732
  176.5 2.0 copy-start.2
  237.3 3.2 %copy-start.8 = (bf16[1,2048,768]{2,1,0:T(8,128)(2,1)S(1)}, bf16[1,2048,768]{2,1,0:T(8,128)(2,1)}, u32[]{:S(2)}) copy-start(bf16[1,2048,768]{2,1,0:T(8,128)(2,1)} %param.24) | copy-start | bytes 9437188
  240.4 6.2 %copy-start.9 = (bf16[1,2048,768]{2,1,0:T(8,128)(2,1)S(1)}, bf16[1,2048,768]{2,1,0:T(8,128)(2,1)}, u32[]{:S(2)}) copy-start(bf16[1,2048,768]{2,1,0:T(8,128)(2,1)} %param.23) | copy-start | bytes 9437188
  246.6 6.4 %copy-start.3 = (bf16[1024,2048]{1,0:T(8,128)(2,1)S(1)}, bf16[1024,2048]{1,0:T(8,128)(2,1)}, u32[]{:S(2)}) copy-start(bf16[1024,2048]{1,0:T(8,128)(2,1)} %copy-done.2) | copy-start | bytes 12582916
  246.6 6.4 %copy-start.5 = (bf16[32,8,4,512]{3,1,2,0:T(8,128)(2,1)S(1)}, bf16[32,8,4,512]{3,1,2,0:T(8,128)(2,1)}, u32[]{:S(2)}) copy-start(bf16[32,8,4,512]{3,1,2,0:T(8,128)(2,1)} %copy-done.4) | copy-start | bytes 3145732
  253.0 9.4 %copy-start.10 = (f32[1280,768]{1,0:T(8,128)S(1)}, f32[1280,768]{1,0:T(8,128)}, u32[]{:S(2)}) copy-start(f32[1280,768]{1,0:T(8,128)} %fusion.1) | copy-start | bytes 11796484
  262.4 8.6 %copy-start.11 = (f32[1280,768]{1,0:T(8,128)S(1)}, f32[1280,768]{1,0:T(8,128)}, u32[]{:S(2)}) copy-start(f32[1280,768]{1,0:T(8,128)} %fusion.4) | copy-start | bytes 11796484
  271.0 8.9 %copy-start.1 = (bf16[1,768,2048]{2,1,0:T(8,128)(2,1)S(1)}, bf16[1,768,2048]{2,1,0:T(8,128)(2,1)}, u32[]{:S(2)}) copy-start(bf16[1,768,2048]{2,1,0:T(8,128)(2,1)} %param.25) | copy-start | bytes 9437188
Sparse Core Ops, SparseCore 0:
  11.4 133.6 all-gather.1

commit v3 on v2

--- a/solution.py
+++ b/solution.py
@@ -4,6 +4,7 @@
 from jax.experimental import pallas as pl
 from jax.experimental.pallas import tpu as pltpu
 from jax.sharding import Mesh, PartitionSpec as P
+
 
 HD = 128
 HEADS = 32
@@ -15,7 +16,9 @@
 EPS = 1e-06
 BF = jnp.bfloat16
 F32 = jnp.float32
-ALL = ("ctx", "chip", "core")
+CHIP = ("x", "z")
+ALL = ("ctx",) + CHIP + ("core",)
+NEAR = (0, -1, 1, 2)
 
 
 def phi(values):
@@ -209,57 +212,62 @@
     )(routes_t, weights_t, cotangent)
 
 
-def project_kernel(core_ref, x_ref, w_ref, mine_ref, ss_ref, theirs_ref, own_s, other_s):
-    step = pl.program_id(0)
-    tokens = mine_ref.shape[0]
-    width = mine_ref.shape[1]
-    total = pl.num_programs(0) * width
-
-    @pl.when(step == 0)
-    def _():
-        core = core_ref[0]
-        for at, keep in ((core, own_s), (1 - core, other_s)):
-            square = jnp.zeros((tokens, HD), F32)
-            for s in range(x_ref.shape[0]):
-                piece = x_ref[s, pl.ds(pl.multiple_of(at * tokens, tokens), tokens), :]
-                wide = piece.astype(F32)
-                gain = x_ref[s, 2 * tokens : 2 * tokens + 1, :].astype(F32)
-                keep[:, s * HD : (s + 1) * HD] = (wide * gain).astype(BF)
-                square = square + wide * wide
-            summed = jnp.broadcast_to(jnp.sum(square, axis=1, keepdims=True), (tokens, HD))
-            if keep is own_s:
-                ss_ref[...] = summed
-            else:
-                high = summed.astype(BF)
-                theirs_ref[:, total : total + HD] = high
-                theirs_ref[:, total + HD :] = (summed - high.astype(F32)).astype(BF)
-
-    w = w_ref[...]
-    mine_ref[...] = dot(own_s[...], w)
-    theirs_ref[:, pl.ds(pl.multiple_of(step * width, width), width)] = dot(other_s[...], w).astype(BF)
-
-
-def project(core, x, weight):
+def project_kernel(place_ref, x_ref, *refs):
+    pieces, (mine_ref, ss_ref, theirs_ref, keep_a, keep_b) = refs[:-5], refs[-5:]
+    tokens, total = mine_ref.shape
+    core = place_ref[0]
+    for half in range(2):
+        at = pl.multiple_of((core if half == 0 else 1 - core) * tokens, tokens)
+        rows = slice(half * tokens, (half + 1) * tokens)
+        square = jnp.zeros((tokens, HD), F32)
+        for s in range(x_ref.shape[0]):
+            chip = place_ref[1 + s]
+            wide = x_ref[chip, pl.ds(at, tokens), :].astype(F32)
+            gain = x_ref[chip, pl.ds(2 * tokens, 8), :].astype(F32)[:1]
+            square = square + wide * wide
+            piece = (wide * gain).astype(BF)
+            other = s % 4 * 4 + s // 4
+            keep_a[rows, s * HD : (s + 1) * HD] = piece
+            keep_b[rows, other * HD : (other + 1) * HD] = piece
+        summed = jnp.broadcast_to(jnp.sum(square, axis=1, keepdims=True), (tokens, HD))
+        if half == 0:
+            ss_ref[...] = summed
+        else:
+            high = summed.astype(BF)
+            theirs_ref[:, total : total + HD] = high
+            theirs_ref[:, total + HD :] = (summed - high.astype(F32)).astype(BF)
+
+    side = total // 2
+    for n, keep in enumerate((keep_a, keep_b)):
+        own, left, right, far_left, far_right = pieces[5 * n : 5 * n + 5]
+        depth = own.shape[0]
+        for j, far in enumerate((far_left, far_right)):
+            width = far.shape[1]
+            cols = slice(j * width, (j + 1) * width)
+            both = dot(keep[:, 3 * depth :], far[...])
+            for g, piece in enumerate((own, left, right)):
+                both = both + dot(keep[:, g * depth : (g + 1) * depth], piece[:, cols])
+            to = slice(n * side + j * width, n * side + (j + 1) * width)
+            mine_ref[:, to] = both[:tokens]
+            theirs_ref[:, to] = both[tokens:].astype(BF)
+
+
+def project(place, x, pieces, width):
     tokens = (x.shape[1] - EXTRA) // 2
     depth = x.shape[0] * HD
-    block = weight.shape[1]
-    blocks = weight.shape[0] // depth
-    width = blocks * block
+    args = (x,) + tuple(pieces)
     return pl.pallas_call(
         project_kernel,
         grid_spec=pltpu.PrefetchScalarGridSpec(
             num_scalar_prefetch=1,
-            grid=(blocks,),
-            in_specs=[
-                pl.BlockSpec(x.shape, lambda i, c: (0, 0, 0)),
-                pl.BlockSpec((depth, block), lambda i, c: (i, 0)),
-            ],
+            grid=(1,),
+            in_specs=[whole(a) for a in args],
             out_specs=[
-                pl.BlockSpec((tokens, block), lambda i, c: (0, i)),
+                pl.BlockSpec((tokens, width), lambda i, c: (0, 0)),
                 pl.BlockSpec((tokens, HD), lambda i, c: (0, 0)),
                 pl.BlockSpec((tokens, width + 2 * HD), lambda i, c: (0, 0)),
             ],
-            scratch_shapes=[pltpu.VMEM((tokens, depth), BF)] * 2,
+            scratch_shapes=[pltpu.VMEM((2 * tokens, depth), BF)] * 2,
         ),
         out_shape=[
             jax.ShapeDtypeStruct((tokens, width), F32),
@@ -267,7 +275,7 @@
             jax.ShapeDtypeStruct((tokens, width + 2 * HD), BF),
         ],
         compiler_params=params(),
-    )(core, x, weight)
+    )(place, *args)
 
 
 def norm_pack_kernel(
@@ -319,26 +327,177 @@
     )(*args)
 
 
-def untail(tail):
-    sources, rows, width = tail.shape
-    split = tail.reshape(sources, QUART, TAIL, width).transpose(0, 2, 1, 3)
-    return split.reshape(sources * TAIL, QUART * width)
-
-
-def expert_grads(rows_in, scaled, gate_mat, up_mat, down_mat):
-    gate_pre = dot(rows_in, gate_mat)
-    up_pre = dot(rows_in, up_mat)
-    sigmoid_gate = jax.nn.sigmoid(gate_pre)
-    active = gate_pre * sigmoid_gate
-    hidden_units = (active * up_pre).astype(BF)
-    grad_down = dot(hidden_units, scaled, 0, 0).astype(BF)
-    grad_hidden = dot(scaled, down_mat, 1, 1)
-    silu_slope = sigmoid_gate * (1.0 + gate_pre * (1.0 - sigmoid_gate))
-    grad_pre_gate = (grad_hidden * up_pre * silu_slope).astype(BF)
-    grad_pre_up = (grad_hidden * active).astype(BF)
-    grad_gate = dot(rows_in, grad_pre_gate, 0, 0).astype(BF)
-    grad_up = dot(rows_in, grad_pre_up, 0, 0).astype(BF)
-    return (grad_gate, grad_up, grad_down)
+ROWS = 256
+
+
+def untail(tail, keep):
+    sources = tail.shape[0] // MAIN
+    to = lax.broadcasted_iota(jnp.int32, (sources * TAIL, tail.shape[0]), 0)
+    of = lax.broadcasted_iota(jnp.int32, (sources * TAIL, tail.shape[0]), 1)
+    width = tail.shape[1]
+    for q in range(QUART):
+        pick = of == to // TAIL * MAIN + q * TAIL + to % TAIL
+        piece = dot(jnp.where(pick, 1.0, 0.0).astype(BF), tail)
+        keep(slice(q * width, (q + 1) * width), piece.astype(BF))
+
+
+def hidden_kernel(rows_ref, tail_ref, down_ref, out_ref, scaled_ref):
+    step = pl.program_id(0)
+    last = pl.num_programs(0) - 1
+
+    @pl.when(step < last)
+    def _():
+        out_ref[...] = dot(rows_ref[...], down_ref[...], 1, 1)
+
+    @pl.when(step == last)
+    def _():
+        def keep(cols, piece):
+            scaled_ref[:, cols] = piece
+
+        untail(tail_ref[...], keep)
+        out_ref[...] = dot(scaled_ref[...], down_ref[...], 1, 1)
+
+
+def hidden_grad(cot, down):
+    rows = cot.shape[0]
+    units, width = down.shape
+    blocks = rows // ROWS
+    tails = rows // MAIN * TAIL
+    return pl.pallas_call(
+        hidden_kernel,
+        grid=(blocks + 1,),
+        in_specs=[
+            pl.BlockSpec((ROWS, width), lambda i: (jnp.minimum(i, blocks - 1), 0)),
+            pl.BlockSpec((rows, width // QUART), lambda i: (0, QUART)),
+            whole(down),
+        ],
+        out_specs=[
+            pl.BlockSpec((ROWS, units), lambda i: (i, 0)),
+            pl.BlockSpec((tails, width), lambda i: (0, 0)),
+        ],
+        out_shape=[
+            jax.ShapeDtypeStruct((rows + tails, units), F32),
+            jax.ShapeDtypeStruct((tails, width), BF),
+        ],
+        compiler_params=params(),
+    )(cot, cot, down)
+
+
+def grads_kernel(
+    x_ref, tail_ref, back_ref, gate_ref, up_ref, scaled_ref, scaled_tail_ref,
+    grad_gate_ref, grad_up_ref, grad_down_ref, x_s, hidden_s, pre_s,
+):
+    step = pl.program_id(0)
+    total, _ = x_s.shape
+    units = gate_ref.shape[1]
+    blocks = total // ROWS
+    part = pl.ds(pl.multiple_of(step * ROWS, ROWS), ROWS)
+
+    @pl.when(step < blocks - 1)
+    def _():
+        x_s[part, :] = x_ref[...]
+
+    @pl.when(step == blocks - 1)
+    def _():
+        def keep(cols, piece):
+            x_s[total - ROWS :, cols] = piece
+
+        untail(tail_ref[...], keep)
+
+    @pl.when(step < blocks)
+    def _():
+        x = x_s[part, :]
+        piece = 256
+        for c in range(units // piece):
+            cols = slice(c * piece, (c + 1) * piece)
+            gate = dot(x, gate_ref[:, cols])
+            up = dot(x, up_ref[:, cols])
+            back = back_ref[:, cols]
+            sig = jax.nn.sigmoid(gate)
+            active = gate * sig
+            hidden_s[cols, part] = jnp.transpose(active * up).astype(BF)
+            slope = sig * (1.0 + gate * (1.0 - sig))
+            pre_s[part, cols] = (back * up * slope).astype(BF)
+            pre_s[part, units + c * piece : units + (c + 1) * piece] = (back * active).astype(BF)
+
+    @pl.when(step >= blocks)
+    def _():
+        block = grad_gate_ref.shape[0]
+        x = x_s[:, pl.ds(pl.multiple_of((step - blocks) * block, block), block)]
+        both = dot(x, pre_s[...], 0, 0)
+        grad_gate_ref[...] = both[:, :units].astype(BF)
+        grad_up_ref[...] = both[:, units:].astype(BF)
+        main = scaled_ref.shape[0]
+        down = dot(hidden_s[:, :main], scaled_ref[...])
+        down = down + dot(hidden_s[:, main:], scaled_tail_ref[...])
+        grad_down_ref[...] = down.astype(BF)
+
+
+def expert_grads(moe, cot, scaled_tail, back, gate, up):
+    main = moe.shape[0]
+    width, units = gate.shape
+    total = back.shape[0]
+    blocks = total // ROWS
+    block = 256
+    at_rows = lambda i: (jnp.minimum(i, blocks - 2), 0)
+    at_cols = lambda i: (0, jnp.maximum(i - blocks, 0))
+    at_out = lambda i: (jnp.maximum(i - blocks, 0), 0)
+    return pl.pallas_call(
+        grads_kernel,
+        grid=(blocks + width // block,),
+        in_specs=[
+            pl.BlockSpec((ROWS, width), at_rows),
+            pl.BlockSpec((main, width // QUART), lambda i: (0, QUART)),
+            pl.BlockSpec((ROWS, units), lambda i: (jnp.minimum(i, blocks - 1), 0)),
+            whole(gate),
+            whole(up),
+            pl.BlockSpec((main, block), at_cols),
+            pl.BlockSpec((total - main, block), at_cols),
+        ],
+        out_specs=[
+            pl.BlockSpec((block, units), at_out),
+            pl.BlockSpec((block, units), at_out),
+            pl.BlockSpec((units, block), at_cols),
+        ],
+        out_shape=[
+            jax.ShapeDtypeStruct((width, units), BF),
+            jax.ShapeDtypeStruct((width, units), BF),
+            jax.ShapeDtypeStruct((units, width), BF),
+        ],
+        scratch_shapes=[
+            pltpu.VMEM((total, width), BF),
+            pltpu.VMEM((units, total), BF),
+            pltpu.VMEM((total, 2 * units), BF),
+        ],
+        compiler_params=params(),
+    )(moe, moe, back, gate, up, cot, scaled_tail)
+
+
+def shift(array, axis, by):
+    size = lax.axis_size(axis)
+    return lax.ppermute(array, axis, [(i, (i + by) % size) for i in range(size)])
+
+
+def around(array, axis):
+    left = shift(array, axis, 1)
+    right = shift(array, axis, -1)
+    half = array.shape[1] // 2
+    far_left = shift(left[:, :half], axis, 1)
+    far_right = shift(right[:, half:], axis, -1)
+    return array, left, right, far_left, far_right
+
+
+def joined(parts):
+    own, left, right, far_left, far_right = parts
+    far = jnp.concatenate([far_left, far_right], axis=1)
+    return jnp.concatenate([own, left, right, far], axis=0)
+
+
+def spread_weight(weight):
+    half = weight.shape[1] // 2
+    first = joined(around(weight[:, :half], "z"))
+    second = joined(around(weight[:, half:], "x"))
+    return around(first, "x") + around(second, "z")
 
 
 def exchange(array, axes):
@@ -352,42 +511,47 @@
     n_ctx = lax.axis_size("ctx")
     width = residual.shape[1]
     at = lax.axis_index("ctx").astype(jnp.int32).reshape(1)
-    core = lax.axis_index("core").astype(jnp.int32).reshape(1)
-
-    strip = width // n_ctx
-    weight = lax.dynamic_slice_in_dim(out_weight, at[0] * strip, strip, 1)
-    weight = lax.all_gather(weight, ("ctx", "chip"), axis=0, tiled=True)
-    states = exchange(span_states(key_heads, value_heads, n_ctx), "ctx")
+    n_x, n_z = lax.axis_size("x"), lax.axis_size("z")
+    near = jnp.array(NEAR, jnp.int32)
+    at_x = (lax.axis_index("x") + near) % n_x
+    at_z = (lax.axis_index("z") + near) % n_z
+    order = (at_x[:, None] * n_z + at_z[None, :]).reshape(-1)
+    place = jnp.concatenate([lax.axis_index("core").reshape(1), order]).astype(jnp.int32)
+
+    pieces = spread_weight(out_weight)
+    states = span_states(key_heads, value_heads, n_ctx)
+    states = exchange(states, "ctx")
+    attention = attend(at, queries, key_heads, value_heads, states, out_gain[None])
+    by_chip = exchange(attention, CHIP)
     routes_t = routes.T
     cot = pack_cot(routes_t, route_weights.T, cotangent)
-    attention = attend(at, queries, key_heads, value_heads, states, out_gain[None])
-    by_chip = exchange(attention, "chip")
     cot, by_chip = lax.optimization_barrier((cot, by_chip))
     cot = exchange(cot.reshape(EXPERTS, MAIN, -1), ALL)
 
-    mine, squares, theirs = project(core, by_chip, weight)
+    mine, squares, theirs = project(place, by_chip, pieces, width)
     got = lax.ppermute(theirs, "core", [(0, 1), (1, 0)])
     hidden_out, moe = norm_pack(mine, squares, got, residual, norm_gain[None], routes_t)
     moe = exchange(moe.reshape(EXPERTS, MAIN, -1), ALL)
 
-    def rows(both):
-        main = both[:, :, :width].reshape(-1, width)
-        return jnp.concatenate([main, untail(both[:, :, width:])], axis=0)
-
-    grads = expert_grads(rows(moe), rows(cot), w_gate[0], w_up[0], w_down[0])
+    moe = moe.reshape(EXPERTS * MAIN, -1)
+    cot = cot.reshape(EXPERTS * MAIN, -1)
+    back, scaled_tail = hidden_grad(cot, w_down[0])
+    grads = expert_grads(moe, cot, scaled_tail, back, w_gate[0], w_up[0])
     return (hidden_out,) + tuple(g[None] for g in grads)
 
 
 def solution(mesh):
     n_ctx, n_head = mesh.devices.shape
-    fine = Mesh(mesh.devices.reshape(n_ctx, n_head // 2, 2), ALL)
-    head = ("chip", "core")
+    side = 4
+    fine = Mesh(mesh.devices.reshape(n_ctx, side, n_head // (2 * side), 2), ALL)
+    head = CHIP + ("core",)
     in_specs = (
         P("ctx", head), P("ctx", head), P("ctx", head), P(head), P(head, None),
         P(ALL, None), P(), P(ALL, None), P(ALL, None), P(ALL, None),
         P(ALL, None, None), P(ALL, None, None), P(ALL, None, None),
     )
     out_specs = (P(ALL, None), P(ALL, None, None), P(ALL, None, None), P(ALL, None, None))
+
     return jax.shard_map(
         on_device, mesh=fine, in_specs=in_specs, out_specs=out_specs, check_vma=False
     )

time: 288 us -> 297 us (1.031)
  matrix products: 45.9 us -> 0 us
  Pallas kernels: 29.3 us -> 72.3 us
  starting transfers between devices: 26.8 us -> 52.4 us
  waiting for transfers between devices: 143 us -> 159 us
  between operations: 14.2 us -> 0.76 us
  blocking collectives: 10.7 us -> 0 us
  local copies, waits for them, and re-layouts: 16.6 us -> 10.6 us
    ppermute x0 -> x16, waiting for transfers between devices: none -> 89.8 us  [shift(): lax.ppermute(array, axis, [(i, (i + by) % size) for i in range(size)])]
    all_gather x1 -> x0, waiting for transfers between devices: 82 us -> none  [on_device(): weight = lax.all_gather(weight, ('ctx', 'chip'), axis=0, tiled=True)]
    dot_general x6 -> x0, matrix products: 45.9 us -> none  [dot(): lax.dot_general(a, b, (((ca,), (cb,)), ((), ())), preferred_element_type=...]
    pallas_call x0 -> x2, Pallas kernels: none -> 42.1 us  [the longest x1 31.3 us: expert_grads(): pl.pallas_call(grads_kernel, grid=(blocks + width // block,), in_specs=[p...]
    ppermute x0 -> x16, starting transfers between devices: none -> 20.1 us  [shift(): lax.ppermute(array, axis, [(i, (i + by) % size) for i in range(size)])]
    all_to_all x1 -> x0, blocking collectives: 10.7 us -> none  [exchange(): return lax.all_to_all(array, axes, split_axis=0, concat_axis=0, tiled=True)]
    all_to_all x3 -> x4, waiting for transfers between devices: 60.1 us -> 67.9 us  [exchange(): return lax.all_to_all(array, axes, split_axis=0, concat_axis=0, tiled=True)]
    reshape x2 -> x0, local copies, waits for them, and re-layouts: 5.53 us -> none  [rows(): main = both[:, :, :width].reshape(-1, width)]
  transfers between devices with their start and end apart: 5 -> 21, of which waited for: 4 -> 12; matrix products, arithmetic and copies ran while one was open for 4% -> 3% of each run, Pallas kernels for 10% -> 11%
where the time goes in v3:
time: 297 us; the launch traced here: 296 us
  waiting for transfers between devices  159 us (54%)
  Pallas kernels  72.3 us (24%)
  starting transfers between devices  52.4 us (18%)
  local copies, waits for them, and re-layouts  10.6 us (4%)
    ppermute x16, waiting for transfers between devices, shift(): lax.ppermute(array, axis, [(i, (i + by) % size) for i in range(size)])  89.8 us
    all_to_all x4, waiting for transfers between devices, exchange(): return lax.all_to_all(array, axes, split_axis=0, concat_axis=0, tiled=True)  67.9 us
    pallas_call x1, Pallas kernels, expert_grads(): pl.pallas_call(grads_kernel, grid=(blocks + width // block,), in_specs=[p...  31.3 us
    all_to_all x4, starting transfers between devices, exchange(): return lax.all_to_all(array, axes, split_axis=0, concat_axis=0, tiled=True)  28.7 us
    ppermute x16, starting transfers between devices, shift(): lax.ppermute(array, axis, [(i, (i + by) % size) for i in range(size)])  20.1 us
    pallas_call x1, Pallas kernels, hidden_grad(): pl.pallas_call(hidden_kernel, grid=(blocks + 1,), in_specs=[pl.BlockSpec(...  10.7 us
    pallas_call x1, Pallas kernels, project(): pl.pallas_call(project_kernel, grid_spec=pltpu.PrefetchScalarGridSpec(num...  7.9 us
    pallas_call x1, Pallas kernels, norm_pack(): pl.pallas_call(norm_pack_kernel, grid=(BLOCKS,), in_specs=[whole(a) for a...  6.52 us
  transfers between devices with their start and end apart: 21, of which 12 were waited for; matrix products, arithmetic and copies ran while one was open for 3% of the time, Pallas kernels for 11%

profile of v3, /device:TPU:1, one launch (start us, length us, event | category | flops | bytes accessed | tf_op | source)
XLA Modules:
  0.0 295.9 jit_solution(9893257354229720640)
XLA Ops:
  0.6 3.9 %shard_map.166 = bf16[4,128,256]{2,1,0:T(8,128)(2,1)} custom-call(bf16[4096,128]{1,0:T(8,128)(2,1)} %k_ref.3, bf16[4096,128]{1,0:T(8,128)(2,1)} %v_ref.3), custom_call_target="tpu_custom_call" | custom-call | tf_op jit(solution)/shard_map/pallas_call | solution.py:57
  4.5 5.0 %all-to-all-start = ((bf16[4,128,256]{2,1,0:T(8,128)(2,1)}), bf16[4,128,256]{2,1,0:T(8,128)(2,1)S(1)}, u32[]{:S(2)}, u32[]{:S(2)}) async-start(bf16[4,128,256]{2,1,0:T(8,128)(2,1)} %shard_map.166), calls=%async_computation | async-start | bytes 524288 | tf_op jit(solution)/shard_map/all_to_all | solution.py:504
  9.5 5.6 %all-to-all-done.s_ref = bf16[4,128,256]{2,1,0:T(8,128)(2,1)S(1)} async-done(((bf16[4,128,256]{2,1,0:T(8,128)(2,1)}), bf16[4,128,256]{2,1,0:T(8,128)(2,1)S(1)}, u32[]{:S(2)}, u32[]{:S(2)}) %all-to-all-start) | async-done | bytes 262176 | tf_op jit(solution)/shard_map/all_to_all | solution.py:504
  15.8 5.9 %shard_map.167 = bf16[16,272,128]{2,1,0:T(8,128)(2,1)} custom-call(s32[1]{0:T(128)} %bitcast.3.at_ref, bf16[4096,128]{1,0:T(8,128)(2,1)} %q_ref.1, bf16[4096,128]{1,0:T(8,128)(2,1)} %k_ref.3, bf16[4096,128]{1,0:T(8,128)(2,1)} %v_ref.3, bf16[4,128,256]{2,1,0:T(8,128)(2,1)} %copy-done.4, bf16[1,128]{1,0:T(2,128)(2,1)} %bitcast.23), custom_call_target="tpu_custom_call" | custom-call | tf_op jit(solution)/shard_map/pallas_call | solution.py:104
  21.7 7.6 %all-to-all-start.1 = ((bf16[16,272,128]{2,1,0:T(8,128)(2,1)}), bf16[16,272,128]{2,1,0:T(8,128)(2,1)S(1)}, u32[]{:S(2)}, u32[]{:S(2)}) async-start(bf16[16,272,128]{2,1,0:T(8,128)(2,1)} %shard_map.167), calls=%async_computation.1 | async-start | bytes 2228224 | tf_op jit(solution)/shard_map/all_to_all | solution.py:504
  29.3 6.1 %shard_map.165 = bf16[1024,2560]{1,0:T(8,128)(2,1)} custom-call(s32[8,128]{1,0:T(8,128)} %bitcast.20, f32[8,128]{1,0:T(8,128)} %bitcast.22, bf16[128,2048]{1,0:T(8,128)(2,1)} %cot_ref.1), custom_call_target="tpu_custom_call" | custom-call | tf_op jit(solution)/shard_map/pallas_call | solution.py:204
  35.3 9.2 %all-to-all-done.1.x_ref = bf16[16,272,128]{2,1,0:T(8,128)(2,1)S(1)} async-done(((bf16[16,272,128]{2,1,0:T(8,128)(2,1)}), bf16[16,272,128]{2,1,0:T(8,128)(2,1)S(1)}, u32[]{:S(2)}, u32[]{:S(2)}) %all-to-all-start.1) | async-done | bytes 1114144 | tf_op jit(solution)/shard_map/all_to_all | solution.py:504
  45.5 8.0 %all-to-all-start.3 = ((bf16[128,8,2560]{2,1,0:T(8,128)(2,1)}), bf16[128,8,2560]{2,1,0:T(8,128)(2,1)}, u32[]{:S(2)}, u32[]{:S(2)}) async-start(bf16[128,8,2560]{2,1,0:T(8,128)(2,1)} %bitcast.15), calls=%async_computation.3 | async-start | bytes 10485760 | tf_op jit(solution)/shard_map/all_to_all | solution.py:504
  53.6 3.4 %collective-permute-start.1 = (bf16[128,1024]{1,0:T(8,128)(2,1)S(1)}, bf16[128,1024]{1,0:T(8,128)(2,1)S(1)}, u32[]{:S(2)}, u32[]{:S(2)}) collective-permute-start(bf16[128,1024]{1,0:T(8,128)(2,1)S(1)} %get-tuple-element.29), channel_id=1, source_target_pairs={{0,6},{2,0},{4,2},{6,4},{1,7},{3,1},{5,3},{7,5},{8,14},{10,8},{12,... | collective-permute-start | bytes 786440 | tf_op jit(solution)/shard_map/ppermute | solution.py:478
  57.1 2.4 collective-permute-start.9
  59.5 58.3 %collective-permute-done.1 = bf16[128,1024]{1,0:T(8,128)(2,1)S(1)} collective-permute-done((bf16[128,1024]{1,0:T(8,128)(2,1)S(1)}, bf16[128,1024]{1,0:T(8,128)(2,1)S(1)}, u32[]{:S(2)}, u32[]{:S(2)}) %collective-permute-start.1) | collective-permute-done | bytes 262176 | tf_op jit(solution)/shard_map/ppermute | solution.py:478
  117.8 1.2 collective-permute-start.3
  119.9 3.4 %collective-permute-start.11 = (bf16[128,512]{1,0:T(8,128)(2,1)S(1)}, bf16[128,512]{1,0:T(8,128)(2,1)S(1)}, u32[]{:S(2)}, u32[]{:S(2)}) collective-permute-start(bf16[128,512]{1,0:T(8,128)(2,1)S(1)} %slice.45), channel_id=1, source_target_pairs={{0,24},{8,0},{16,8},{24,16},{1,25},{9,1},{17,9},{25,17},{2,26},{10... | collective-permute-start | bytes 393224 | tf_op jit(solution)/shard_map/ppermute | solution.py:478
  124.2 3.0 %collective-permute-start.5 = (bf16[512,1024]{1,0:T(8,128)(2,1)S(1)}, bf16[512,1024]{1,0:T(8,128)(2,1)S(1)}, u32[]{:S(2)}, u32[]{:S(2)}) collective-permute-start(bf16[512,1024]{1,0:T(8,128)(2,1)S(1)} %maximum_maximum_fusion.refs_0_), channel_id=1, source_target_pairs={{0,24},{8,0},{16,8},{24,16},{1,25},{9,1},{17,9},{25,17},{2,26},{10... | collective-permute-start | bytes 3145736 | tf_op jit(solution)/shard_map/ppermute | solution.py:478
  128.5 1.3 collective-permute-start.13
  130.0 20.5 %collective-permute-done.5.refs_2_ = bf16[512,1024]{1,0:T(8,128)(2,1)S(1)} collective-permute-done((bf16[512,1024]{1,0:T(8,128)(2,1)S(1)}, bf16[512,1024]{1,0:T(8,128)(2,1)S(1)}, u32[]{:S(2)}, u32[]{:S(2)}) %collective-permute-start.5) | collective-permute-done | bytes 1048608 | tf_op jit(solution)/shard_map/ppermute | solution.py:478
  152.4 1.9 slice.42
  154.7 1.9 slice.47
  157.1 1.9 slice.46
  159.0 1.0 collective-permute-start.14
  160.8 2.7 collective-permute-done.7.refs_4_
  163.5 3.0 %collective-permute-done.6.refs_3_ = bf16[512,512]{1,0:T(8,128)(2,1)} collective-permute-done((bf16[512,512]{1,0:T(8,128)(2,1)}, bf16[512,512]{1,0:T(8,128)(2,1)}, u32[]{:S(2)}, u32[]{:S(2)}) %collective-permute-start.6) | collective-permute-done | bytes 524320 | tf_op jit(solution)/shard_map/ppermute | solution.py:478
  166.4 1.6 collective-permute-done.15.refs_9_
  168.1 3.1 %collective-permute-done.14.refs_8_ = bf16[512,512]{1,0:T(8,128)(2,1)S(1)} collective-permute-done((bf16[512,512]{1,0:T(8,128)(2,1)}, bf16[512,512]{1,0:T(8,128)(2,1)S(1)}, u32[]{:S(2)}, u32[]{:S(2)}) %collective-permute-start.14) | collective-permute-done | bytes 524320 | tf_op jit(solution)/shard_map/ppermute | solution.py:478
  171.9 7.9 %shard_map.168 = (f32[128,2048]{1,0:T(8,128)}, f32[128,128]{1,0:T(8,128)}, bf16[128,2304]{1,0:T(8,128)(2,1)}) custom-call(s32[17]{0:T(128)} %pad_add_fusion.place_ref, bf16[16,272,128]{2,1,0:T(8,128)(2,1)} %copy-done, bf16[512,1024]{1,0:T(8,128)(2,1)} %copy-done.1, bf16[512,1024]{1,0:T(8,128)(2,1)} %collective-permute-done.4.refs_1_, ...), custom_call_target="tpu_custom_call" | custom-call | tf_op jit(solution)/shard_map/pallas_call | solution.py:259
  179.8 3.6 %collective-permute-start.16 = (bf16[128,2304]{1,0:T(8,128)(2,1)}, bf16[128,2304]{1,0:T(8,128)(2,1)S(1)}, u32[]{:S(2)}, u32[]{:S(2)}) collective-permute-start(bf16[128,2304]{1,0:T(8,128)(2,1)} %get-tuple-element.19), channel_id=1, source_target_pairs={{0,1},{1,0},{2,3},{3,2},{4,5},{5,4},{6,7},{7,6},{8,9},{9,8},{10,11... | collective-permute-start | bytes 1769480 | tf_op jit(solution)/shard_map/ppermute | solution.py:532
  184.0 1.2 collective-permute-done.16.got_ref
  186.1 6.5 %shard_map.169 = (bf16[128,2048]{1,0:T(8,128)(2,1)}, bf16[1024,2560]{1,0:T(8,128)(2,1)}) custom-call(f32[128,2048]{1,0:T(8,128)} %get-tuple-element.17.mine_ref, f32[128,128]{1,0:T(8,128)} %get-tuple-element.18.ss_ref, bf16[128,2304]{1,0:T(8,128)(2,1)} %copy-done.5, bf16[128,2048]{1,0:T(8,128)(2,1)} %residual_ref.1, ...), custom_call_target="tpu_custom_call" | custom-call | tf_op jit(solution)/shard_map/pallas_call | solution.py:316
  192.6 8.1 %all-to-all-start.2 = ((bf16[128,8,2560]{2,1,0:T(8,128)(2,1)}), bf16[128,8,2560]{2,1,0:T(8,128)(2,1)}, u32[]{:S(2)}, u32[]{:S(2)}) async-start(bf16[128,8,2560]{2,1,0:T(8,128)(2,1)} %bitcast.16), calls=%async_computation.2 | async-start | bytes 10485760 | tf_op jit(solution)/shard_map/all_to_all | solution.py:504
  200.7 10.7 %shard_map.170 = (f32[1280,768]{1,0:T(8,128)}, bf16[256,2048]{1,0:T(8,128)(2,1)}) custom-call(bf16[1024,2560]{1,0:T(8,128)(2,1)} %bitcast.8.rows_ref.tail_ref.scaled_ref, bf16[1024,2560]{1,0:T(8,128)(2,1)} %bitcast.8.rows_ref.tail_ref.scaled_ref, bf16[768,2048]{1,0:T(8,128)(2,1)} %bitcast.19), custom_call_target="tpu_custom_call" | custom-call | tf_op jit(solution)/shard_map/pallas_call | solution.py:366
  211.4 53.1 %all-to-all-done.2 = bf16[128,8,2560]{2,1,0:T(8,128)(2,1)} async-done(((bf16[128,8,2560]{2,1,0:T(8,128)(2,1)}), bf16[128,8,2560]{2,1,0:T(8,128)(2,1)}, u32[]{:S(2)}, u32[]{:S(2)}) %all-to-all-start.2) | async-done | bytes 5242912 | tf_op jit(solution)/shard_map/all_to_all | solution.py:504
  264.5 31.3 %shard_map.171 = (bf16[2048,768]{1,0:T(8,128)(2,1)}, bf16[2048,768]{1,0:T(8,128)(2,1)}, bf16[768,2048]{1,0:T(8,128)(2,1)}) custom-call(bf16[1024,2560]{1,0:T(8,128)(2,1)} %bitcast.6.x_ref.tail_ref, bf16[1024,2560]{1,0:T(8,128)(2,1)} %bitcast.6.x_ref.tail_ref, f32[1280,768]{1,0:T(8,128)} %get-tuple-element.23.back_ref, bf16[2048,768]{1,0:T(8,128)(2,1)} %bitcast.17, ...), custom_call_target="tpu_custom_call" | custom-call | tf_op jit(solution)/shard_map/pallas_call | solution.py:445
  (55 shorter events, 10.9 us)
Async XLA Ops:
  4.5 10.6 %all-to-all-start = ((bf16[4,128,256]{2,1,0:T(8,128)(2,1)}), bf16[4,128,256]{2,1,0:T(8,128)(2,1)S(1)}, u32[]{:S(2)}, u32[]{:S(2)}) async-start(bf16[4,128,256]{2,1,0:T(8,128)(2,1)} %shard_map.166), calls=%async_computation | async-start | bytes 524288 | tf_op jit(solution)/shard_map/all_to_all | solution.py:504
  15.1 0.7 copy-start.4
  21.7 22.9 %all-to-all-start.1 = ((bf16[16,272,128]{2,1,0:T(8,128)(2,1)}), bf16[16,272,128]{2,1,0:T(8,128)(2,1)S(1)}, u32[]{:S(2)}, u32[]{:S(2)}) async-start(bf16[16,272,128]{2,1,0:T(8,128)(2,1)} %shard_map.167), calls=%async_computation.1 | async-start | bytes 2228224 | tf_op jit(solution)/shard_map/all_to_all | solution.py:504
  44.5 1.0 copy-start
  44.5 9.0 %copy-start.8 = (bf16[128,2048]{1,0:T(8,128)(2,1)S(1)}, bf16[128,2048]{1,0:T(8,128)(2,1)}, u32[]{:S(2)}) copy-start(bf16[128,2048]{1,0:T(8,128)(2,1)} %param.18) | copy-start | bytes 1572868
  45.5 147.1 %all-to-all-start.3 = ((bf16[128,8,2560]{2,1,0:T(8,128)(2,1)}), bf16[128,8,2560]{2,1,0:T(8,128)(2,1)}, u32[]{:S(2)}, u32[]{:S(2)}) async-start(bf16[128,8,2560]{2,1,0:T(8,128)(2,1)} %bitcast.15), calls=%async_computation.3 | async-start | bytes 10485760 | tf_op jit(solution)/shard_map/all_to_all | solution.py:504
  53.6 64.2 %collective-permute-start.1 = (bf16[128,1024]{1,0:T(8,128)(2,1)S(1)}, bf16[128,1024]{1,0:T(8,128)(2,1)S(1)}, u32[]{:S(2)}, u32[]{:S(2)}) collective-permute-start(bf16[128,1024]{1,0:T(8,128)(2,1)S(1)} %get-tuple-element.29), channel_id=1, source_target_pairs={{0,6},{2,0},{4,2},{6,4},{1,7},{3,1},{5,3},{7,5},{8,14},{10,8},{12,... | collective-permute-start | bytes 786440 | tf_op jit(solution)/shard_map/ppermute | solution.py:478
  57.1 61.9 %collective-permute-start = (bf16[128,1024]{1,0:T(8,128)(2,1)S(1)}, bf16[128,1024]{1,0:T(8,128)(2,1)S(1)}, u32[]{:S(2)}, u32[]{:S(2)}) collective-permute-start(bf16[128,1024]{1,0:T(8,128)(2,1)S(1)} %get-tuple-element.29), channel_id=1, source_target_pairs={{0,2},{2,4},{4,6},{6,0},{1,3},{3,5},{5,7},{7,1},{8,10},{10,12},{12... | collective-permute-start | bytes 786440 | tf_op jit(solution)/shard_map/ppermute | solution.py:478
  57.1 62.8 %collective-permute-start.9 = (bf16[128,1024]{1,0:T(8,128)(2,1)S(1)}, bf16[128,1024]{1,0:T(8,128)(2,1)S(1)}, u32[]{:S(2)}, u32[]{:S(2)}) collective-permute-start(bf16[128,1024]{1,0:T(8,128)(2,1)S(1)} %get-tuple-element.28), channel_id=1, source_target_pairs={{0,24},{8,0},{16,8},{24,16},{1,25},{9,1},{17,9},{25,17},{2,26},{10... | collective-permute-start | bytes 786440 | tf_op jit(solution)/shard_map/ppermute | solution.py:478
  59.5 63.8 %collective-permute-start.8 = (bf16[128,1024]{1,0:T(8,128)(2,1)S(1)}, bf16[128,1024]{1,0:T(8,128)(2,1)S(1)}, u32[]{:S(2)}, u32[]{:S(2)}) collective-permute-start(bf16[128,1024]{1,0:T(8,128)(2,1)S(1)} %get-tuple-element.28), channel_id=1, source_target_pairs={{0,8},{8,16},{16,24},{24,0},{1,9},{9,17},{17,25},{25,1},{2,10},{10... | collective-permute-start | bytes 786440 | tf_op jit(solution)/shard_map/ppermute | solution.py:478
  117.8 5.8 %collective-permute-start.3 = (bf16[128,512]{1,0:T(8,128)(2,1)S(1)}, bf16[128,512]{1,0:T(8,128)(2,1)S(1)}, u32[]{:S(2)}, u32[]{:S(2)}) collective-permute-start(bf16[128,512]{1,0:T(8,128)(2,1)S(1)} %slice.41), channel_id=1, source_target_pairs={{0,6},{2,0},{4,2},{6,4},{1,7},{3,1},{5,3},{7,5},{8,14},{10,8},{12,... | collective-permute-start | bytes 393224 | tf_op jit(solution)/shard_map/ppermute | solution.py:478
  119.0 5.1 %collective-permute-start.2 = (bf16[128,512]{1,0:T(8,128)(2,1)S(1)}, bf16[128,512]{1,0:T(8,128)(2,1)S(1)}, u32[]{:S(2)}, u32[]{:S(2)}) collective-permute-start(bf16[128,512]{1,0:T(8,128)(2,1)S(1)} %slice.40), channel_id=1, source_target_pairs={{0,2},{2,4},{4,6},{6,0},{1,3},{3,5},{5,7},{7,1},{8,10},{10,12},{12... | collective-permute-start | bytes 393224 | tf_op jit(solution)/shard_map/ppermute | solution.py:478
  119.9 8.3 %collective-permute-start.11 = (bf16[128,512]{1,0:T(8,128)(2,1)S(1)}, bf16[128,512]{1,0:T(8,128)(2,1)S(1)}, u32[]{:S(2)}, u32[]{:S(2)}) collective-permute-start(bf16[128,512]{1,0:T(8,128)(2,1)S(1)} %slice.45), channel_id=1, source_target_pairs={{0,24},{8,0},{16,8},{24,16},{1,25},{9,1},{17,9},{25,17},{2,26},{10... | collective-permute-start | bytes 393224 | tf_op jit(solution)/shard_map/ppermute | solution.py:478
  123.3 5.1 %collective-permute-start.10 = (bf16[128,512]{1,0:T(8,128)(2,1)S(1)}, bf16[128,512]{1,0:T(8,128)(2,1)S(1)}, u32[]{:S(2)}, u32[]{:S(2)}) collective-permute-start(bf16[128,512]{1,0:T(8,128)(2,1)S(1)} %slice.44), channel_id=1, source_target_pairs={{0,8},{8,16},{16,24},{24,0},{1,9},{9,17},{17,25},{25,1},{2,10},{10... | collective-permute-start | bytes 393224 | tf_op jit(solution)/shard_map/ppermute | solution.py:478
  124.2 30.1 %copy-start.1 = (bf16[512,1024]{1,0:T(8,128)(2,1)}, bf16[512,1024]{1,0:T(8,128)(2,1)S(1)}, u32[]{:S(2)}) copy-start(bf16[512,1024]{1,0:T(8,128)(2,1)S(1)} %maximum_maximum_fusion.refs_0_) | copy-start | bytes 3145732
  124.2 26.3 %collective-permute-start.5 = (bf16[512,1024]{1,0:T(8,128)(2,1)S(1)}, bf16[512,1024]{1,0:T(8,128)(2,1)S(1)}, u32[]{:S(2)}, u32[]{:S(2)}) collective-permute-start(bf16[512,1024]{1,0:T(8,128)(2,1)S(1)} %maximum_maximum_fusion.refs_0_), channel_id=1, source_target_pairs={{0,24},{8,0},{16,8},{24,16},{1,25},{9,1},{17,9},{25,17},{2,26},{10... | collective-permute-start | bytes 3145736 | tf_op jit(solution)/shard_map/ppermute | solution.py:478
  127.2 25.2 %collective-permute-start.4 = (bf16[512,1024]{1,0:T(8,128)(2,1)S(1)}, bf16[512,1024]{1,0:T(8,128)(2,1)}, u32[]{:S(2)}, u32[]{:S(2)}) collective-permute-start(bf16[512,1024]{1,0:T(8,128)(2,1)S(1)} %maximum_maximum_fusion.refs_0_), channel_id=1, source_target_pairs={{0,8},{8,16},{16,24},{24,0},{1,9},{9,17},{17,25},{25,1},{2,10},{10... | collective-permute-start | bytes 3145736 | tf_op jit(solution)/shard_map/ppermute | solution.py:478
  128.5 30.5 %copy-start.2 = (bf16[512,1024]{1,0:T(8,128)(2,1)}, bf16[512,1024]{1,0:T(8,128)(2,1)S(1)}, u32[]{:S(2)}) copy-start(bf16[512,1024]{1,0:T(8,128)(2,1)S(1)} %maximum_maximum_fusion.1.refs_5_) | copy-start | bytes 3145732
  128.5 26.3 %collective-permute-start.13 = (bf16[512,1024]{1,0:T(8,128)(2,1)S(1)}, bf16[512,1024]{1,0:T(8,128)(2,1)}, u32[]{:S(2)}, u32[]{:S(2)}) collective-permute-start(bf16[512,1024]{1,0:T(8,128)(2,1)S(1)} %maximum_maximum_fusion.1.refs_5_), channel_id=1, source_target_pairs={{0,6},{2,0},{4,2},{6,4},{1,7},{3,1},{5,3},{7,5},{8,14},{10,8},{12,... | collective-permute-start | bytes 3145736 | tf_op jit(solution)/shard_map/ppermute | solution.py:478
  129.8 27.3 %collective-permute-start.12 = (bf16[512,1024]{1,0:T(8,128)(2,1)S(1)}, bf16[512,1024]{1,0:T(8,128)(2,1)}, u32[]{:S(2)}, u32[]{:S(2)}) collective-permute-start(bf16[512,1024]{1,0:T(8,128)(2,1)S(1)} %maximum_maximum_fusion.1.refs_5_), channel_id=1, source_target_pairs={{0,2},{2,4},{4,6},{6,0},{1,3},{3,5},{5,7},{7,1},{8,10},{10,12},{12... | collective-permute-start | bytes 3145736 | tf_op jit(solution)/shard_map/ppermute | solution.py:478
  130.0 30.0 %copy-start.10 = (s32[4]{0:T(128)S(1)}, s32[4]{0:T(128)}, u32[]{:S(2)}) copy-start(s32[4]{0:T(128)} %constant.38.clone) | copy-start | bytes 52
  150.5 8.5 %copy-start.3 = (bf16[512,1024]{1,0:T(8,128)(2,1)}, bf16[512,1024]{1,0:T(8,128)(2,1)S(1)}, u32[]{:S(2)}) copy-start(bf16[512,1024]{1,0:T(8,128)(2,1)S(1)} %collective-permute-done.5.refs_2_) | copy-start | bytes 3145732
  151.4 12.1 %collective-permute-start.7 = (bf16[512,512]{1,0:T(8,128)(2,1)}, bf16[512,512]{1,0:T(8,128)(2,1)}, u32[]{:S(2)}, u32[]{:S(2)}) collective-permute-start(bf16[512,512]{1,0:T(8,128)(2,1)} %slice.43), channel_id=1, source_target_pairs={{0,24},{8,0},{16,8},{24,16},{1,25},{9,1},{17,9},{25,17},{2,26},{10... | collective-permute-start | bytes 1572872 | tf_op jit(solution)/shard_map/ppermute | solution.py:478
  154.3 12.2 %collective-permute-start.6 = (bf16[512,512]{1,0:T(8,128)(2,1)}, bf16[512,512]{1,0:T(8,128)(2,1)}, u32[]{:S(2)}, u32[]{:S(2)}) collective-permute-start(bf16[512,512]{1,0:T(8,128)(2,1)} %slice.42), channel_id=1, source_target_pairs={{0,8},{8,16},{16,24},{24,0},{1,9},{9,17},{17,25},{25,1},{2,10},{10... | collective-permute-start | bytes 1572872 | tf_op jit(solution)/shard_map/ppermute | solution.py:478
  156.6 11.4 %collective-permute-start.15 = (bf16[512,512]{1,0:T(8,128)(2,1)}, bf16[512,512]{1,0:T(8,128)(2,1)S(1)}, u32[]{:S(2)}, u32[]{:S(2)}) collective-permute-start(bf16[512,512]{1,0:T(8,128)(2,1)} %slice.47), channel_id=1, source_target_pairs={{0,6},{2,0},{4,2},{6,4},{1,7},{3,1},{5,3},{7,5},{8,14},{10,8},{12,... | collective-permute-start | bytes 1572872 | tf_op jit(solution)/shard_map/ppermute | solution.py:478
  159.0 12.2 %collective-permute-start.14 = (bf16[512,512]{1,0:T(8,128)(2,1)}, bf16[512,512]{1,0:T(8,128)(2,1)S(1)}, u32[]{:S(2)}, u32[]{:S(2)}) collective-permute-start(bf16[512,512]{1,0:T(8,128)(2,1)} %slice.46), channel_id=1, source_target_pairs={{0,2},{2,4},{4,6},{6,0},{1,3},{3,5},{5,7},{7,1},{8,10},{10,12},{12... | collective-permute-start | bytes 1572872 | tf_op jit(solution)/shard_map/ppermute | solution.py:478
  160.8 22.6 %copy-start.9 = (bf16[2048]{0:T(1024)(128)(2,1)S(1)}, bf16[2048]{0:T(1024)(128)(2,1)}, u32[]{:S(2)}) copy-start(bf16[2048]{0:T(1024)(128)(2,1)} %param.20) | copy-start | bytes 12292
  168.0 3.1 %copy-start.6 = (bf16[512,512]{1,0:T(8,128)(2,1)}, bf16[512,512]{1,0:T(8,128)(2,1)S(1)}, u32[]{:S(2)}) copy-start(bf16[512,512]{1,0:T(8,128)(2,1)S(1)} %collective-permute-done.15.refs_9_) | copy-start | bytes 1572868
  171.1 0.8 copy-start.7
  179.8 5.4 %collective-permute-start.16 = (bf16[128,2304]{1,0:T(8,128)(2,1)}, bf16[128,2304]{1,0:T(8,128)(2,1)S(1)}, u32[]{:S(2)}, u32[]{:S(2)}) collective-permute-start(bf16[128,2304]{1,0:T(8,128)(2,1)} %get-tuple-element.19), channel_id=1, source_target_pairs={{0,1},{1,0},{2,3},{3,2},{4,5},{5,4},{6,7},{7,6},{8,9},{9,8},{10,11... | collective-permute-start | bytes 1769480 | tf_op jit(solution)/shard_map/ppermute | solution.py:532
  185.3 0.8 copy-start.5
  192.6 71.9 %all-to-all-start.2 = ((bf16[128,8,2560]{2,1,0:T(8,128)(2,1)}), bf16[128,8,2560]{2,1,0:T(8,128)(2,1)}, u32[]{:S(2)}, u32[]{:S(2)}) async-start(bf16[128,8,2560]{2,1,0:T(8,128)(2,1)} %bitcast.16), calls=%async_computation.2 | async-start | bytes 10485760 | tf_op jit(solution)/shard_map/all_to_all | solution.py:504

commit v4 on v3

--- a/solution.py
+++ b/solution.py
@@ -237,19 +237,15 @@
             theirs_ref[:, total : total + HD] = high
             theirs_ref[:, total + HD :] = (summed - high.astype(F32)).astype(BF)
 
-    side = total // 2
-    for n, keep in enumerate((keep_a, keep_b)):
-        own, left, right, far_left, far_right = pieces[5 * n : 5 * n + 5]
-        depth = own.shape[0]
-        for j, far in enumerate((far_left, far_right)):
-            width = far.shape[1]
-            cols = slice(j * width, (j + 1) * width)
-            both = dot(keep[:, 3 * depth :], far[...])
-            for g, piece in enumerate((own, left, right)):
-                both = both + dot(keep[:, g * depth : (g + 1) * depth], piece[:, cols])
-            to = slice(n * side + j * width, n * side + (j + 1) * width)
-            mine_ref[:, to] = both[:tokens]
-            theirs_ref[:, to] = both[tokens:].astype(BF)
+    depth, side = pieces[0].shape
+    for n in range(total // side):
+        keep = keep_a if 2 * n < total // side else keep_b
+        both = jnp.zeros((2 * tokens, side), F32)
+        for g in range(4):
+            both = both + dot(keep[:, g * depth : (g + 1) * depth], pieces[4 * n + g][...])
+        to = slice(n * side, (n + 1) * side)
+        mine_ref[:, to] = both[:tokens]
+        theirs_ref[:, to] = both[tokens:].astype(BF)
 
 
 def project(place, x, pieces, width):
@@ -438,7 +434,7 @@
     width, units = gate.shape
     total = back.shape[0]
     blocks = total // ROWS
-    block = 256
+    block = 512
     at_rows = lambda i: (jnp.minimum(i, blocks - 2), 0)
     at_cols = lambda i: (0, jnp.maximum(i - blocks, 0))
     at_out = lambda i: (jnp.maximum(i - blocks, 0), 0)
@@ -478,26 +474,26 @@
     return lax.ppermute(array, axis, [(i, (i + by) % size) for i in range(size)])
 
 
-def around(array, axis):
-    left = shift(array, axis, 1)
-    right = shift(array, axis, -1)
-    half = array.shape[1] // 2
-    far_left = shift(left[:, :half], axis, 1)
-    far_right = shift(right[:, half:], axis, -1)
-    return array, left, right, far_left, far_right
-
-
-def joined(parts):
-    own, left, right, far_left, far_right = parts
-    far = jnp.concatenate([far_left, far_right], axis=1)
-    return jnp.concatenate([own, left, right, far], axis=0)
+def around(first, second, axis):
+    left_first = shift(first, axis, 1)
+    right_second = shift(second, axis, -1)
+    left_second = shift(second, axis, 1)
+    right_first = shift(first, axis, -1)
+    far_first = shift(left_first, axis, 1)
+    far_second = shift(right_second, axis, -1)
+    return [first, left_first, right_first, far_first], [second, left_second, right_second, far_second]
 
 
 def spread_weight(weight):
-    half = weight.shape[1] // 2
-    first = joined(around(weight[:, :half], "z"))
-    second = joined(around(weight[:, half:], "x"))
-    return around(first, "x") + around(second, "z")
+    quarter = weight.shape[1] // 4
+    parts = [weight[:, n * quarter : (n + 1) * quarter] for n in range(4)]
+    pieces = []
+    for n, (near, far) in enumerate((("z", "x"), ("x", "z"))):
+        halves = around(parts[2 * n], parts[2 * n + 1], near)
+        first, second = (jnp.concatenate(half, axis=0) for half in halves)
+        for half in around(first, second, far):
+            pieces += half
+    return tuple(pieces)
 
 
 def exchange(array, axes):
@@ -525,7 +521,7 @@
     by_chip = exchange(attention, CHIP)
     routes_t = routes.T
     cot = pack_cot(routes_t, route_weights.T, cotangent)
-    cot, by_chip = lax.optimization_barrier((cot, by_chip))
+    cot, by_chip, pieces = lax.optimization_barrier((cot, by_chip, pieces))
     cot = exchange(cot.reshape(EXPERTS, MAIN, -1), ALL)
 
     mine, squares, theirs = project(place, by_chip, pieces, width)

time: 297 us -> 281 us (0.946)
  waiting for transfers between devices: 159 us -> 139 us
  starting transfers between devices: 52.4 us -> 58.6 us
  local copies, waits for them, and re-layouts: 10.6 us -> 5.8 us
    ppermute x16 -> x24, waiting for transfers between devices: 89.8 us -> 40.5 us  [shift(): lax.ppermute(array, axis, [(i, (i + by) % size) for i in range(size)])]
    all_to_all x4, waiting for transfers between devices: 67.9 us -> 97.7 us  [exchange(): return lax.all_to_all(array, axes, split_axis=0, concat_axis=0, tiled=True)]
    ppermute x16 -> x24, starting transfers between devices: 20.1 us -> 26.7 us  [shift(): lax.ppermute(array, axis, [(i, (i + by) % size) for i in range(size)])]
    slice x9 -> x1, local copies, waits for them, and re-layouts: 6.61 us -> 1.14 us  [spread_weight(): parts = [weight[:, n * quarter:(n + 1) * quarter] for n in range(4)]]
  transfers between devices with their start and end apart: 21 -> 29, of which waited for: 12 -> 8; matrix products, arithmetic and copies ran while one was open for 3% -> 2% of each run, Pallas kernels for 11% -> 15%
where the time goes in v4:
time: 281 us; the launch traced here: 280 us
  waiting for transfers between devices  139 us (49%)
  Pallas kernels  71.8 us (26%)
  starting transfers between devices  58.6 us (21%)
  local copies, waits for them, and re-layouts  5.8 us (2%)
  other arithmetic  3.62 us (1%)
    all_to_all x4, waiting for transfers between devices, exchange(): return lax.all_to_all(array, axes, split_axis=0, concat_axis=0, tiled=True)  97.7 us
    ppermute x24, waiting for transfers between devices, shift(): lax.ppermute(array, axis, [(i, (i + by) % size) for i in range(size)])  40.5 us
    all_to_all x4, starting transfers between devices, exchange(): return lax.all_to_all(array, axes, split_axis=0, concat_axis=0, tiled=True)  30.8 us
    pallas_call x1, Pallas kernels, expert_grads(): pl.pallas_call(grads_kernel, grid=(blocks + width // block,), in_specs=[p...  30.6 us
    ppermute x24, starting transfers between devices, shift(): lax.ppermute(array, axis, [(i, (i + by) % size) for i in range(size)])  26.7 us
    pallas_call x1, Pallas kernels, hidden_grad(): pl.pallas_call(hidden_kernel, grid=(blocks + 1,), in_specs=[pl.BlockSpec(...  10.8 us
    pallas_call x1, Pallas kernels, project(): pl.pallas_call(project_kernel, grid_spec=pltpu.PrefetchScalarGridSpec(num...  8.02 us
    pallas_call x1, Pallas kernels, norm_pack(): pl.pallas_call(norm_pack_kernel, grid=(BLOCKS,), in_specs=[whole(a) for a...  6.52 us
  transfers between devices with their start and end apart: 29, of which 8 were waited for; matrix products, arithmetic and copies ran while one was open for 2% of the time, Pallas kernels for 15%

profile of v4, /device:TPU:1, one launch (start us, length us, event | category | flops | bytes accessed | tf_op | source)
XLA Modules:
  0.0 280.2 jit_solution(14978468178537407265)
XLA Ops:
  1.8 2.1 collective-permute-start.12
  3.9 1.3 collective-permute-start.13
  5.2 2.8 collective-permute-done.12
  8.2 2.4 collective-permute-start.19
  10.7 4.0 %collective-permute-start.7 = (bf16[128,512]{1,0:T(8,128)(2,1)S(1)}, bf16[128,512]{1,0:T(8,128)(2,1)S(1)}, u32[]{:S(2)}, u32[]{:S(2)}) collective-permute-start(bf16[128,512]{1,0:T(8,128)(2,1)S(1)} %get-tuple-element.61), channel_id=1, source_target_pairs={{0,6},{2,0},{4,2},{6,4},{1,7},{3,1},{5,3},{7,5},{8,14},{10,8},{12,... | collective-permute-start | bytes 393224 | tf_op jit(solution)/shard_map/ppermute | solution.py:474
  14.8 2.7 collective-permute-start.16
  17.6 2.7 collective-permute-start.1
  20.3 14.6 %collective-permute-done.6 = bf16[128,512]{1,0:T(8,128)(2,1)S(1)} collective-permute-done((bf16[128,512]{1,0:T(8,128)(2,1)S(1)}, bf16[128,512]{1,0:T(8,128)(2,1)S(1)}, u32[]{:S(2)}, u32[]{:S(2)}) %collective-permute-start.6) | collective-permute-done | bytes 131104 | tf_op jit(solution)/shard_map/ppermute | solution.py:474
  34.9 3.9 %shard_map.166 = bf16[4,128,256]{2,1,0:T(8,128)(2,1)} custom-call(bf16[4096,128]{1,0:T(8,128)(2,1)} %k_ref.3, bf16[4096,128]{1,0:T(8,128)(2,1)} %v_ref.3), custom_call_target="tpu_custom_call" | custom-call | tf_op jit(solution)/shard_map/pallas_call | solution.py:57
  38.8 4.2 %all-to-all-start = ((bf16[4,128,256]{2,1,0:T(8,128)(2,1)}), bf16[4,128,256]{2,1,0:T(8,128)(2,1)S(1)}, u32[]{:S(2)}, u32[]{:S(2)}) async-start(bf16[4,128,256]{2,1,0:T(8,128)(2,1)} %shard_map.166), calls=%async_computation | async-start | bytes 524288 | tf_op jit(solution)/shard_map/all_to_all | solution.py:500
  43.6 2.7 collective-permute-start.20
  49.0 1.5 collective-permute-start.3
  50.5 1.2 collective-permute-start.10
  53.9 5.9 %shard_map.167 = bf16[16,272,128]{2,1,0:T(8,128)(2,1)} custom-call(s32[1]{0:T(128)} %bitcast.3.at_ref, bf16[4096,128]{1,0:T(8,128)(2,1)} %q_ref.1, bf16[4096,128]{1,0:T(8,128)(2,1)} %k_ref.3, bf16[4096,128]{1,0:T(8,128)(2,1)} %v_ref.3, bf16[4,128,256]{2,1,0:T(8,128)(2,1)} %copy-done.5, bf16[1,128]{1,0:T(2,128)(2,1)} %bitcast.23), custom_call_target="tpu_custom_call" | custom-call | tf_op jit(solution)/shard_map/pallas_call | solution.py:104
  59.8 6.7 %all-to-all-start.1 = ((bf16[16,272,128]{2,1,0:T(8,128)(2,1)}), bf16[16,272,128]{2,1,0:T(8,128)(2,1)S(1)}, u32[]{:S(2)}, u32[]{:S(2)}) async-start(bf16[16,272,128]{2,1,0:T(8,128)(2,1)} %shard_map.167), calls=%async_computation.1 | async-start | bytes 2228224 | tf_op jit(solution)/shard_map/all_to_all | solution.py:500
  66.5 1.4 collective-permute-start.21
  67.9 1.2 collective-permute-start.17
  69.1 1.9 collective-permute-done.10.refs_6_
  71.0 2.7 collective-permute-start.11
  73.7 6.1 %shard_map.165 = bf16[1024,2560]{1,0:T(8,128)(2,1)} custom-call(s32[8,128]{1,0:T(8,128)} %bitcast.20, f32[8,128]{1,0:T(8,128)} %bitcast.22, bf16[128,2048]{1,0:T(8,128)(2,1)} %cot_ref.1), custom_call_target="tpu_custom_call" | custom-call | tf_op jit(solution)/shard_map/pallas_call | solution.py:204
  79.7 8.0 %collective-permute-done.21.refs_13_ = bf16[512,512]{1,0:T(8,128)(2,1)S(1)} collective-permute-done((bf16[512,512]{1,0:T(8,128)(2,1)S(1)}, bf16[512,512]{1,0:T(8,128)(2,1)S(1)}, u32[]{:S(2)}, u32[]{:S(2)}) %collective-permute-start.21) | collective-permute-done | bytes 524320 | tf_op jit(solution)/shard_map/ppermute | solution.py:474
  87.8 13.2 %collective-permute-done.17.refs_11_ = bf16[512,512]{1,0:T(8,128)(2,1)S(1)} collective-permute-done((bf16[512,512]{1,0:T(8,128)(2,1)}, bf16[512,512]{1,0:T(8,128)(2,1)S(1)}, u32[]{:S(2)}, u32[]{:S(2)}) %collective-permute-start.17) | collective-permute-done | bytes 524320 | tf_op jit(solution)/shard_map/ppermute | solution.py:474
  102.0 11.6 %all-to-all-start.3 = ((bf16[128,8,2560]{2,1,0:T(8,128)(2,1)}), bf16[128,8,2560]{2,1,0:T(8,128)(2,1)}, u32[]{:S(2)}, u32[]{:S(2)}) async-start(bf16[128,8,2560]{2,1,0:T(8,128)(2,1)} %bitcast.15), calls=%async_computation.3 | async-start | bytes 10485760 | tf_op jit(solution)/shard_map/all_to_all | solution.py:500
  114.3 8.0 %shard_map.168 = (f32[128,2048]{1,0:T(8,128)}, f32[128,128]{1,0:T(8,128)}, bf16[128,2304]{1,0:T(8,128)(2,1)}) custom-call(s32[17]{0:T(128)} %pad_add_fusion.place_ref, bf16[16,272,128]{2,1,0:T(8,128)(2,1)} %copy-done, bf16[512,512]{1,0:T(8,128)(2,1)} %copy-done.2, bf16[512,512]{1,0:T(8,128)(2,1)} %collective-permute-done.3.refs_1_, ...), custom_call_target="tpu_custom_call" | custom-call | tf_op jit(solution)/shard_map/pallas_call | solution.py:255
  122.4 1.1 collective-permute-start.24
  124.1 1.2 collective-permute-done.24.got_ref
  126.1 6.5 %shard_map.169 = (bf16[128,2048]{1,0:T(8,128)(2,1)}, bf16[1024,2560]{1,0:T(8,128)(2,1)}) custom-call(f32[128,2048]{1,0:T(8,128)} %get-tuple-element.49.mine_ref, f32[128,128]{1,0:T(8,128)} %get-tuple-element.50.ss_ref, bf16[128,2304]{1,0:T(8,128)(2,1)} %copy-done.6, bf16[128,2048]{1,0:T(8,128)(2,1)} %residual_ref.1, ...), custom_call_target="tpu_custom_call" | custom-call | tf_op jit(solution)/shard_map/pallas_call | solution.py:312
  132.7 44.7 %all-to-all-done.3 = bf16[128,8,2560]{2,1,0:T(8,128)(2,1)} async-done(((bf16[128,8,2560]{2,1,0:T(8,128)(2,1)}), bf16[128,8,2560]{2,1,0:T(8,128)(2,1)}, u32[]{:S(2)}, u32[]{:S(2)}) %all-to-all-start.3) | async-done | bytes 5242912 | tf_op jit(solution)/shard_map/all_to_all | solution.py:500
  177.3 8.4 %all-to-all-start.2 = ((bf16[128,8,2560]{2,1,0:T(8,128)(2,1)}), bf16[128,8,2560]{2,1,0:T(8,128)(2,1)}, u32[]{:S(2)}, u32[]{:S(2)}) async-start(bf16[128,8,2560]{2,1,0:T(8,128)(2,1)} %bitcast.16), calls=%async_computation.2 | async-start | bytes 10485760 | tf_op jit(solution)/shard_map/all_to_all | solution.py:500
  185.8 10.8 %shard_map.170 = (f32[1280,768]{1,0:T(8,128)}, bf16[256,2048]{1,0:T(8,128)(2,1)}) custom-call(bf16[1024,2560]{1,0:T(8,128)(2,1)} %bitcast.8.rows_ref.tail_ref.scaled_ref, bf16[1024,2560]{1,0:T(8,128)(2,1)} %bitcast.8.rows_ref.tail_ref.scaled_ref, bf16[768,2048]{1,0:T(8,128)(2,1)} %bitcast.19), custom_call_target="tpu_custom_call" | custom-call | tf_op jit(solution)/shard_map/pallas_call | solution.py:362
  196.5 53.0 %all-to-all-done.2 = bf16[128,8,2560]{2,1,0:T(8,128)(2,1)} async-done(((bf16[128,8,2560]{2,1,0:T(8,128)(2,1)}), bf16[128,8,2560]{2,1,0:T(8,128)(2,1)}, u32[]{:S(2)}, u32[]{:S(2)}) %all-to-all-start.2) | async-done | bytes 5242912 | tf_op jit(solution)/shard_map/all_to_all | solution.py:500
  249.6 30.6 %shard_map.171 = (bf16[2048,768]{1,0:T(8,128)(2,1)}, bf16[2048,768]{1,0:T(8,128)(2,1)}, bf16[768,2048]{1,0:T(8,128)(2,1)}) custom-call(bf16[1024,2560]{1,0:T(8,128)(2,1)} %bitcast.6.x_ref.tail_ref, bf16[1024,2560]{1,0:T(8,128)(2,1)} %bitcast.6.x_ref.tail_ref, f32[1280,768]{1,0:T(8,128)} %get-tuple-element.55.back_ref, bf16[2048,768]{1,0:T(8,128)(2,1)} %bitcast.17, ...), custom_call_target="tpu_custom_call" | custom-call | tf_op jit(solution)/shard_map/pallas_call | solution.py:441
  (79 shorter events, 10.2 us)
Async XLA Ops:
  1.8 6.2 %collective-permute-start.12 = (bf16[128,512]{1,0:T(8,128)(2,1)S(1)}, bf16[128,512]{1,0:T(8,128)(2,1)S(1)}, u32[]{:S(2)}, u32[]{:S(2)}) collective-permute-start(bf16[128,512]{1,0:T(8,128)(2,1)S(1)} %get-tuple-element.63), channel_id=1, source_target_pairs={{0,8},{8,16},{16,24},{24,0},{1,9},{9,17},{17,25},{25,1},{2,10},{10... | collective-permute-start | bytes 393224 | tf_op jit(solution)/shard_map/ppermute | solution.py:474
  3.9 10.8 %collective-permute-start.13 = (bf16[128,512]{1,0:T(8,128)(2,1)S(1)}, bf16[128,512]{1,0:T(8,128)(2,1)S(1)}, u32[]{:S(2)}, u32[]{:S(2)}) collective-permute-start(bf16[128,512]{1,0:T(8,128)(2,1)S(1)} %get-tuple-element.63), channel_id=1, source_target_pairs={{0,24},{8,0},{16,8},{24,16},{1,25},{9,1},{17,9},{25,17},{2,26},{10... | collective-permute-start | bytes 393224 | tf_op jit(solution)/shard_map/ppermute | solution.py:474
  8.0 6.7 %collective-permute-start.14 = (bf16[128,512]{1,0:T(8,128)(2,1)S(1)}, bf16[128,512]{1,0:T(8,128)(2,1)S(1)}, u32[]{:S(2)}, u32[]{:S(2)}) collective-permute-start(bf16[128,512]{1,0:T(8,128)(2,1)S(1)} %collective-permute-done.12), channel_id=1, source_target_pairs={{0,8},{8,16},{16,24},{24,0},{1,9},{9,17},{17,25},{25,1},{2,10},{10... | collective-permute-start | bytes 393224 | tf_op jit(solution)/shard_map/ppermute | solution.py:474
  8.2 9.2 %collective-permute-start.19 = (bf16[128,512]{1,0:T(8,128)(2,1)S(1)}, bf16[128,512]{1,0:T(8,128)(2,1)S(1)}, u32[]{:S(2)}, u32[]{:S(2)}) collective-permute-start(bf16[128,512]{1,0:T(8,128)(2,1)S(1)} %get-tuple-element.60), channel_id=1, source_target_pairs={{0,24},{8,0},{16,8},{24,16},{1,25},{9,1},{17,9},{25,17},{2,26},{10... | collective-permute-start | bytes 393224 | tf_op jit(solution)/shard_map/ppermute | solution.py:474
  10.7 6.9 %collective-permute-start.7 = (bf16[128,512]{1,0:T(8,128)(2,1)S(1)}, bf16[128,512]{1,0:T(8,128)(2,1)S(1)}, u32[]{:S(2)}, u32[]{:S(2)}) collective-permute-start(bf16[128,512]{1,0:T(8,128)(2,1)S(1)} %get-tuple-element.61), channel_id=1, source_target_pairs={{0,6},{2,0},{4,2},{6,4},{1,7},{3,1},{5,3},{7,5},{8,14},{10,8},{12,... | collective-permute-start | bytes 393224 | tf_op jit(solution)/shard_map/ppermute | solution.py:474
  14.7 5.6 %collective-permute-start = (bf16[128,512]{1,0:T(8,128)(2,1)S(1)}, bf16[128,512]{1,0:T(8,128)(2,1)S(1)}, u32[]{:S(2)}, u32[]{:S(2)}) collective-permute-start(bf16[128,512]{1,0:T(8,128)(2,1)S(1)} %get-tuple-element.62), channel_id=1, source_target_pairs={{0,2},{2,4},{4,6},{6,0},{1,3},{3,5},{5,7},{7,1},{8,10},{10,12},{12... | collective-permute-start | bytes 393224 | tf_op jit(solution)/shard_map/ppermute | solution.py:474
  14.7 45.0 %copy-start.1 = (bf16[512,512]{1,0:T(8,128)(2,1)}, bf16[512,512]{1,0:T(8,128)(2,1)S(1)}, u32[]{:S(2)}) copy-start(bf16[512,512]{1,0:T(8,128)(2,1)S(1)} %pad_maximum_fusion.2.refs_8_) | copy-start | bytes 1572868
  14.8 38.0 %collective-permute-start.16 = (bf16[512,512]{1,0:T(8,128)(2,1)S(1)}, bf16[512,512]{1,0:T(8,128)(2,1)S(1)}, u32[]{:S(2)}, u32[]{:S(2)}) collective-permute-start(bf16[512,512]{1,0:T(8,128)(2,1)S(1)} %pad_maximum_fusion.2.refs_8_), channel_id=1, source_target_pairs={{0,6},{2,0},{4,2},{6,4},{1,7},{3,1},{5,3},{7,5},{8,14},{10,8},{12,... | collective-permute-start | bytes 1572872 | tf_op jit(solution)/shard_map/ppermute | solution.py:474
  17.5 35.6 %collective-permute-start.15 = (bf16[512,512]{1,0:T(8,128)(2,1)S(1)}, bf16[512,512]{1,0:T(8,128)(2,1)S(1)}, u32[]{:S(2)}, u32[]{:S(2)}) collective-permute-start(bf16[512,512]{1,0:T(8,128)(2,1)S(1)} %pad_maximum_fusion.2.refs_8_), channel_id=1, source_target_pairs={{0,2},{2,4},{4,6},{6,0},{1,3},{3,5},{5,7},{7,1},{8,10},{10,12},{12... | collective-permute-start | bytes 1572872 | tf_op jit(solution)/shard_map/ppermute | solution.py:474
  17.5 33.1 %copy-start.12 = (bf16[128,512]{1,0:T(8,128)(2,1)}, bf16[128,512]{1,0:T(8,128)(2,1)S(1)}, u32[]{:S(2)}) copy-start(bf16[128,512]{1,0:T(8,128)(2,1)S(1)} %collective-permute-done.19) | copy-start | bytes 393220
  17.5 17.4 %collective-permute-start.6 = (bf16[128,512]{1,0:T(8,128)(2,1)S(1)}, bf16[128,512]{1,0:T(8,128)(2,1)S(1)}, u32[]{:S(2)}, u32[]{:S(2)}) collective-permute-start(bf16[128,512]{1,0:T(8,128)(2,1)S(1)} %get-tuple-element.61), channel_id=1, source_target_pairs={{0,2},{2,4},{4,6},{6,0},{1,3},{3,5},{5,7},{7,1},{8,10},{10,12},{12... | collective-permute-start | bytes 393224 | tf_op jit(solution)/shard_map/ppermute | solution.py:474
  17.6 29.7 %copy-start.13 = (bf16[128,512]{1,0:T(8,128)(2,1)}, bf16[128,512]{1,0:T(8,128)(2,1)S(1)}, u32[]{:S(2)}) copy-start(bf16[128,512]{1,0:T(8,128)(2,1)S(1)} %collective-permute-done.7) | copy-start | bytes 393220
  17.6 25.3 %collective-permute-start.1 = (bf16[128,512]{1,0:T(8,128)(2,1)S(1)}, bf16[128,512]{1,0:T(8,128)(2,1)S(1)}, u32[]{:S(2)}, u32[]{:S(2)}) collective-permute-start(bf16[128,512]{1,0:T(8,128)(2,1)S(1)} %get-tuple-element.62), channel_id=1, source_target_pairs={{0,6},{2,0},{4,2},{6,4},{1,7},{3,1},{5,3},{7,5},{8,14},{10,8},{12,... | collective-permute-start | bytes 393224 | tf_op jit(solution)/shard_map/ppermute | solution.py:474
  20.3 22.7 %collective-permute-start.2 = (bf16[128,512]{1,0:T(8,128)(2,1)S(1)}, bf16[128,512]{1,0:T(8,128)(2,1)S(1)}, u32[]{:S(2)}, u32[]{:S(2)}) collective-permute-start(bf16[128,512]{1,0:T(8,128)(2,1)S(1)} %collective-permute-done), channel_id=1, source_target_pairs={{0,2},{2,4},{4,6},{6,0},{1,3},{3,5},{5,7},{7,1},{8,10},{10,12},{12... | collective-permute-start | bytes 393224 | tf_op jit(solution)/shard_map/ppermute | solution.py:474
  34.9 12.4 %collective-permute-start.8 = (bf16[128,512]{1,0:T(8,128)(2,1)S(1)}, bf16[128,512]{1,0:T(8,128)(2,1)S(1)}, u32[]{:S(2)}, u32[]{:S(2)}) collective-permute-start(bf16[128,512]{1,0:T(8,128)(2,1)S(1)} %collective-permute-done.7), channel_id=1, source_target_pairs={{0,6},{2,0},{4,2},{6,4},{1,7},{3,1},{5,3},{7,5},{8,14},{10,8},{12,... | collective-permute-start | bytes 393224 | tf_op jit(solution)/shard_map/ppermute | solution.py:474
  38.8 14.3 %all-to-all-start = ((bf16[4,128,256]{2,1,0:T(8,128)(2,1)}), bf16[4,128,256]{2,1,0:T(8,128)(2,1)S(1)}, u32[]{:S(2)}, u32[]{:S(2)}) async-start(bf16[4,128,256]{2,1,0:T(8,128)(2,1)} %shard_map.166), calls=%async_computation | async-start | bytes 524288 | tf_op jit(solution)/shard_map/all_to_all | solution.py:500
  42.9 6.1 %collective-permute-start.18 = (bf16[128,512]{1,0:T(8,128)(2,1)S(1)}, bf16[128,512]{1,0:T(8,128)(2,1)S(1)}, u32[]{:S(2)}, u32[]{:S(2)}) collective-permute-start(bf16[128,512]{1,0:T(8,128)(2,1)S(1)} %get-tuple-element.60), channel_id=1, source_target_pairs={{0,8},{8,16},{16,24},{24,0},{1,9},{9,17},{17,25},{25,1},{2,10},{10... | collective-permute-start | bytes 393224 | tf_op jit(solution)/shard_map/ppermute | solution.py:474
  43.6 6.9 %collective-permute-start.20 = (bf16[128,512]{1,0:T(8,128)(2,1)S(1)}, bf16[128,512]{1,0:T(8,128)(2,1)S(1)}, u32[]{:S(2)}, u32[]{:S(2)}) collective-permute-start(bf16[128,512]{1,0:T(8,128)(2,1)S(1)} %collective-permute-done.19), channel_id=1, source_target_pairs={{0,24},{8,0},{16,8},{24,16},{1,25},{9,1},{17,9},{25,17},{2,26},{10... | collective-permute-start | bytes 393224 | tf_op jit(solution)/shard_map/ppermute | solution.py:474
  48.0 18.5 %collective-permute-start.4 = (bf16[512,512]{1,0:T(8,128)(2,1)S(1)}, bf16[512,512]{1,0:T(8,128)(2,1)}, u32[]{:S(2)}, u32[]{:S(2)}) collective-permute-start(bf16[512,512]{1,0:T(8,128)(2,1)S(1)} %pad_maximum_fusion.refs_0_), channel_id=1, source_target_pairs={{0,24},{8,0},{16,8},{24,16},{1,25},{9,1},{17,9},{25,17},{2,26},{10... | collective-permute-start | bytes 1572872 | tf_op jit(solution)/shard_map/ppermute | solution.py:474
  49.0 18.9 %collective-permute-start.3 = (bf16[512,512]{1,0:T(8,128)(2,1)S(1)}, bf16[512,512]{1,0:T(8,128)(2,1)}, u32[]{:S(2)}, u32[]{:S(2)}) collective-permute-start(bf16[512,512]{1,0:T(8,128)(2,1)S(1)} %pad_maximum_fusion.refs_0_), channel_id=1, source_target_pairs={{0,8},{8,16},{16,24},{24,0},{1,9},{9,17},{17,25},{25,1},{2,10},{10... | collective-permute-start | bytes 1572872 | tf_op jit(solution)/shard_map/ppermute | solution.py:474
  50.5 20.4 %collective-permute-start.10 = (bf16[512,512]{1,0:T(8,128)(2,1)S(1)}, bf16[512,512]{1,0:T(8,128)(2,1)}, u32[]{:S(2)}, u32[]{:S(2)}) collective-permute-start(bf16[512,512]{1,0:T(8,128)(2,1)S(1)} %pad_maximum_fusion.1.refs_4_), channel_id=1, source_target_pairs={{0,24},{8,0},{16,8},{24,16},{1,25},{9,1},{17,9},{25,17},{2,26},{10... | collective-permute-start | bytes 1572872 | tf_op jit(solution)/shard_map/ppermute | solution.py:474
  52.7 18.3 %collective-permute-start.9 = (bf16[512,512]{1,0:T(8,128)(2,1)S(1)}, bf16[512,512]{1,0:T(8,128)(2,1)}, u32[]{:S(2)}, u32[]{:S(2)}) collective-permute-start(bf16[512,512]{1,0:T(8,128)(2,1)S(1)} %pad_maximum_fusion.1.refs_4_), channel_id=1, source_target_pairs={{0,8},{8,16},{16,24},{24,0},{1,9},{9,17},{17,25},{25,1},{2,10},{10... | collective-permute-start | bytes 1572872 | tf_op jit(solution)/shard_map/ppermute | solution.py:474
  53.1 20.6 %collective-permute-start.22 = (bf16[512,512]{1,0:T(8,128)(2,1)S(1)}, bf16[512,512]{1,0:T(8,128)(2,1)}, u32[]{:S(2)}, u32[]{:S(2)}) collective-permute-start(bf16[512,512]{1,0:T(8,128)(2,1)S(1)} %pad_maximum_fusion.3.refs_12_), channel_id=1, source_target_pairs={{0,6},{2,0},{4,2},{6,4},{1,7},{3,1},{5,3},{7,5},{8,14},{10,8},{12,... | collective-permute-start | bytes 1572872 | tf_op jit(solution)/shard_map/ppermute | solution.py:474
  59.8 28.0 %all-to-all-start.1 = ((bf16[16,272,128]{2,1,0:T(8,128)(2,1)}), bf16[16,272,128]{2,1,0:T(8,128)(2,1)S(1)}, u32[]{:S(2)}, u32[]{:S(2)}) async-start(bf16[16,272,128]{2,1,0:T(8,128)(2,1)} %shard_map.167), calls=%async_computation.1 | async-start | bytes 2228224 | tf_op jit(solution)/shard_map/all_to_all | solution.py:500
  66.5 21.3 %collective-permute-start.21 = (bf16[512,512]{1,0:T(8,128)(2,1)S(1)}, bf16[512,512]{1,0:T(8,128)(2,1)S(1)}, u32[]{:S(2)}, u32[]{:S(2)}) collective-permute-start(bf16[512,512]{1,0:T(8,128)(2,1)S(1)} %pad_maximum_fusion.3.refs_12_), channel_id=1, source_target_pairs={{0,2},{2,4},{4,6},{6,0},{1,3},{3,5},{5,7},{7,1},{8,10},{10,12},{12... | collective-permute-start | bytes 1572872 | tf_op jit(solution)/shard_map/ppermute | solution.py:474
  67.9 33.0 %collective-permute-start.17 = (bf16[512,512]{1,0:T(8,128)(2,1)}, bf16[512,512]{1,0:T(8,128)(2,1)S(1)}, u32[]{:S(2)}, u32[]{:S(2)}) collective-permute-start(bf16[512,512]{1,0:T(8,128)(2,1)} %copy-done.8), channel_id=1, source_target_pairs={{0,2},{2,4},{4,6},{6,0},{1,3},{3,5},{5,7},{7,1},{8,10},{10,12},{12... | collective-permute-start | bytes 1572872 | tf_op jit(solution)/shard_map/ppermute | solution.py:474
  71.0 30.0 %collective-permute-start.5 = (bf16[512,512]{1,0:T(8,128)(2,1)}, bf16[512,512]{1,0:T(8,128)(2,1)}, u32[]{:S(2)}, u32[]{:S(2)}) collective-permute-start(bf16[512,512]{1,0:T(8,128)(2,1)} %collective-permute-done.3.refs_1_), channel_id=1, source_target_pairs={{0,8},{8,16},{16,24},{24,0},{1,9},{9,17},{17,25},{25,1},{2,10},{10... | collective-permute-start | bytes 1572872 | tf_op jit(solution)/shard_map/ppermute | solution.py:474
  71.0 30.0 %collective-permute-start.11 = (bf16[512,512]{1,0:T(8,128)(2,1)}, bf16[512,512]{1,0:T(8,128)(2,1)S(1)}, u32[]{:S(2)}, u32[]{:S(2)}) collective-permute-start(bf16[512,512]{1,0:T(8,128)(2,1)} %collective-permute-done.10.refs_6_), channel_id=1, source_target_pairs={{0,24},{8,0},{16,8},{24,16},{1,25},{9,1},{17,9},{25,17},{2,26},{10... | collective-permute-start | bytes 1572872 | tf_op jit(solution)/shard_map/ppermute | solution.py:474
  73.7 27.3 %collective-permute-start.23 = (bf16[512,512]{1,0:T(8,128)(2,1)}, bf16[512,512]{1,0:T(8,128)(2,1)}, u32[]{:S(2)}, u32[]{:S(2)}) collective-permute-start(bf16[512,512]{1,0:T(8,128)(2,1)} %collective-permute-done.22.refs_14_), channel_id=1, source_target_pairs={{0,6},{2,0},{4,2},{6,4},{1,7},{3,1},{5,3},{7,5},{8,14},{10,8},{12,... | collective-permute-start | bytes 1572872 | tf_op jit(solution)/shard_map/ppermute | solution.py:474
  102.0 75.4 %all-to-all-start.3 = ((bf16[128,8,2560]{2,1,0:T(8,128)(2,1)}), bf16[128,8,2560]{2,1,0:T(8,128)(2,1)}, u32[]{:S(2)}, u32[]{:S(2)}) async-start(bf16[128,8,2560]{2,1,0:T(8,128)(2,1)} %bitcast.15), calls=%async_computation.3 | async-start | bytes 10485760 | tf_op jit(solution)/shard_map/all_to_all | solution.py:500
  122.4 3.0 %collective-permute-start.24 = (bf16[128,2304]{1,0:T(8,128)(2,1)}, bf16[128,2304]{1,0:T(8,128)(2,1)S(1)}, u32[]{:S(2)}, u32[]{:S(2)}) collective-permute-start(bf16[128,2304]{1,0:T(8,128)(2,1)} %get-tuple-element.51), channel_id=1, source_target_pairs={{0,1},{1,0},{2,3},{3,2},{4,5},{5,4},{6,7},{7,6},{8,9},{9,8},{10,11... | collective-permute-start | bytes 1769480 | tf_op jit(solution)/shard_map/ppermute | solution.py:528
  177.3 72.2 %all-to-all-start.2 = ((bf16[128,8,2560]{2,1,0:T(8,128)(2,1)}), bf16[128,8,2560]{2,1,0:T(8,128)(2,1)}, u32[]{:S(2)}, u32[]{:S(2)}) async-start(bf16[128,8,2560]{2,1,0:T(8,128)(2,1)} %bitcast.16), calls=%async_computation.2 | async-start | bytes 10485760 | tf_op jit(solution)/shard_map/all_to_all | solution.py:500
  (15 other events, 103.9 us)

commit v5 on v4

--- a/solution.py
+++ b/solution.py
@@ -80,9 +80,10 @@
     rows = lax.broadcasted_iota(jnp.int32, (CHUNK, CHUNK), 0)
     cols = lax.broadcasted_iota(jnp.int32, (CHUNK, CHUNK), 1)
     run = state[...]
-    per_chip = o_ref.shape[1] - EXTRA
-    for c in range(o_ref.shape[0]):
-        o_ref[c, per_chip:, :] = jnp.broadcast_to(g_ref[...], (EXTRA, HD))
+    cores, rows_out, _ = o_ref.shape
+    own = CHUNK // cores
+    for c in range(cores):
+        o_ref[c, rows_out - EXTRA :, :] = jnp.broadcast_to(g_ref[...], (EXTRA, HD))
     for n in range(q_ref.shape[0] // CHUNK):
         part = pl.ds(n * CHUNK, CHUNK)
         qf = phi(q_ref[part, :])
@@ -91,26 +92,28 @@
         v1 = jnp.concatenate([v, jnp.ones_like(v)], axis=1)
         scores = jnp.where(rows >= cols, dot(qf, kf, 1, 1), 0.0).astype(BF)
         both = dot(scores, v1) + dot(qf, run.astype(BF))
-        o_ref[n, :per_chip, :] = (both[:, :HD] / both[:, HD:]).astype(BF)
+        result = (both[:, :HD] / both[:, HD:]).astype(BF)
+        for c in range(cores):
+            o_ref[c, n * own : (n + 1) * own, :] = result[c * own : (c + 1) * own]
         run = run + dot(kf, v1, 0, 0)
     state[...] = run
 
 
-def attend(at, queries, keys, values, states, gain):
+def attend(at, queries, keys, values, states, gain, groups, cores):
     length = queries.shape[0]
-    block = min(1024, length)
-    each = block // CHUNK
+    block = length // groups
+    rows = block // cores + EXTRA
     tok = pl.BlockSpec((block, HD), lambda i, at: (i, 0))
     return pl.pallas_call(
         attend_kernel,
         grid_spec=pltpu.PrefetchScalarGridSpec(
             num_scalar_prefetch=1,
-            grid=(length // block,),
+            grid=(groups,),
             in_specs=[tok, tok, tok, whole(states), whole(gain)],
-            out_specs=pl.BlockSpec((each, CHUNK + EXTRA, HD), lambda i, at: (i, 0, 0)),
+            out_specs=pl.BlockSpec((cores, rows, HD), lambda i, at: (i, 0, 0)),
             scratch_shapes=[pltpu.VMEM((HD, 2 * HD), F32)],
         ),
-        out_shape=jax.ShapeDtypeStruct((length // CHUNK, CHUNK + EXTRA, HD), BF),
+        out_shape=jax.ShapeDtypeStruct((groups * cores, rows, HD), BF),
         compiler_params=params(),
     )(at, queries, keys, values, states, gain)
 
@@ -213,69 +216,58 @@
 
 
 def project_kernel(place_ref, x_ref, *refs):
-    pieces, (mine_ref, ss_ref, theirs_ref, keep_a, keep_b) = refs[:-5], refs[-5:]
+    pieces, (mine_ref, ss_ref, *out_refs), keep = refs[:8], refs[8:-1], refs[-1]
     tokens, total = mine_ref.shape
-    core = place_ref[0]
-    for half in range(2):
-        at = pl.multiple_of((core if half == 0 else 1 - core) * tokens, tokens)
-        rows = slice(half * tokens, (half + 1) * tokens)
+    for d in range(4):
+        at = pl.multiple_of(place_ref[d] * tokens, tokens)
+        rows = slice(d * tokens, (d + 1) * tokens)
         square = jnp.zeros((tokens, HD), F32)
-        for s in range(x_ref.shape[0]):
-            chip = place_ref[1 + s]
-            wide = x_ref[chip, pl.ds(at, tokens), :].astype(F32)
-            gain = x_ref[chip, pl.ds(2 * tokens, 8), :].astype(F32)[:1]
+        for s in range(8):
+            source = place_ref[4 + s]
+            wide = x_ref[source, pl.ds(at, tokens), :].astype(F32)
+            gain = x_ref[source, pl.ds(4 * tokens, 8), :].astype(F32)[:1]
             square = square + wide * wide
-            piece = (wide * gain).astype(BF)
-            other = s % 4 * 4 + s // 4
-            keep_a[rows, s * HD : (s + 1) * HD] = piece
-            keep_b[rows, other * HD : (other + 1) * HD] = piece
+            keep[rows, s * HD : (s + 1) * HD] = (wide * gain).astype(BF)
         summed = jnp.broadcast_to(jnp.sum(square, axis=1, keepdims=True), (tokens, HD))
-        if half == 0:
+        if d == 0:
             ss_ref[...] = summed
         else:
             high = summed.astype(BF)
-            theirs_ref[:, total : total + HD] = high
-            theirs_ref[:, total + HD :] = (summed - high.astype(F32)).astype(BF)
-
-    depth, side = pieces[0].shape
+            out_refs[d - 1][:, total : total + HD] = high
+            out_refs[d - 1][:, total + HD :] = (summed - high.astype(F32)).astype(BF)
+
+    side = 512
     for n in range(total // side):
-        keep = keep_a if 2 * n < total // side else keep_b
-        both = jnp.zeros((2 * tokens, side), F32)
-        for g in range(4):
-            both = both + dot(keep[:, g * depth : (g + 1) * depth], pieces[4 * n + g][...])
-        to = slice(n * side, (n + 1) * side)
-        mine_ref[:, to] = both[:tokens]
-        theirs_ref[:, to] = both[tokens:].astype(BF)
-
-
-def project(place, x, pieces, width):
-    tokens = (x.shape[1] - EXTRA) // 2
-    depth = x.shape[0] * HD
+        cols = slice(n * side, (n + 1) * side)
+        both = jnp.zeros((4 * tokens, side), F32)
+        for s in range(8):
+            both = both + dot(keep[:, s * HD : (s + 1) * HD], pieces[s][:, cols])
+        mine_ref[:, cols] = both[:tokens]
+        for d in range(1, 4):
+            out_refs[d - 1][:, cols] = both[d * tokens : (d + 1) * tokens].astype(BF)
+
+
+def project(place, x, pieces):
+    tokens = (x.shape[1] - EXTRA) // 4
+    width = pieces[0].shape[1]
     args = (x,) + tuple(pieces)
+    shapes = [(width, F32), (HD, F32)] + [(width + 2 * HD, BF)] * 3
     return pl.pallas_call(
         project_kernel,
         grid_spec=pltpu.PrefetchScalarGridSpec(
             num_scalar_prefetch=1,
             grid=(1,),
             in_specs=[whole(a) for a in args],
-            out_specs=[
-                pl.BlockSpec((tokens, width), lambda i, c: (0, 0)),
-                pl.BlockSpec((tokens, HD), lambda i, c: (0, 0)),
-                pl.BlockSpec((tokens, width + 2 * HD), lambda i, c: (0, 0)),
-            ],
-            scratch_shapes=[pltpu.VMEM((2 * tokens, depth), BF)] * 2,
+            out_specs=[pl.BlockSpec((tokens, n), lambda i, c: (0, 0)) for n, _ in shapes],
+            scratch_shapes=[pltpu.VMEM((4 * tokens, 8 * HD), BF)],
         ),
-        out_shape=[
-            jax.ShapeDtypeStruct((tokens, width), F32),
-            jax.ShapeDtypeStruct((tokens, HD), F32),
-            jax.ShapeDtypeStruct((tokens, width + 2 * HD), BF),
-        ],
+        out_shape=[jax.ShapeDtypeStruct((tokens, n), kind) for n, kind in shapes],
         compiler_params=params(),
     )(place, *args)
 
 
 def norm_pack_kernel(
-    mine_ref, ss_ref, got_ref, residual_ref, gain_ref, routes_ref,
+    mine_ref, ss_ref, got_a, got_b, got_c, residual_ref, gain_ref, routes_ref,
     hidden_ref, out_ref, rank_s, table_s,
 ):
     step = pl.program_id(0)
@@ -283,13 +275,14 @@
     @pl.when(step == 0)
     def _():
         width = mine_ref.shape[1]
-        squares = (
-            ss_ref[...]
-            + got_ref[:, width : width + HD].astype(F32)
-            + got_ref[:, width + HD :].astype(F32)
-        )[:, :1]
-        inverse = lax.rsqrt(squares / (HEADS * HD) + EPS)
-        projected = (mine_ref[...] + got_ref[:, :width].astype(F32)) * inverse
+        squares = ss_ref[...]
+        projected = mine_ref[...]
+        for got in (got_a, got_b, got_c):
+            squares = squares + got[:, width : width + HD].astype(F32)
+            squares = squares + got[:, width + HD :].astype(F32)
+            projected = projected + got[:, :width].astype(F32)
+        inverse = lax.rsqrt(squares[:, :1] / (HEADS * HD) + EPS)
+        projected = projected * inverse
         hidden = (residual_ref[...].astype(F32) + projected).astype(BF)
         hidden_ref[...] = hidden
         wide = hidden.astype(F32)
@@ -305,10 +298,10 @@
     out_ref[:, width:] = tail_rows(tail, quarter, table).astype(BF)
 
 
-def norm_pack(mine, squares, got, residual, gain, routes_t):
+def norm_pack(mine, squares, arrived, residual, gain, routes_t):
     tokens, width = residual.shape
     spec, shape = packed(width)
-    args = (mine, squares, got, residual, gain, routes_t)
+    args = (mine, squares) + tuple(arrived) + (residual, gain, routes_t)
     return pl.pallas_call(
         norm_pack_kernel,
         grid=(BLOCKS,),
@@ -474,28 +467,6 @@
     return lax.ppermute(array, axis, [(i, (i + by) % size) for i in range(size)])
 
 
-def around(first, second, axis):
-    left_first = shift(first, axis, 1)
-    right_second = shift(second, axis, -1)
-    left_second = shift(second, axis, 1)
-    right_first = shift(first, axis, -1)
-    far_first = shift(left_first, axis, 1)
-    far_second = shift(right_second, axis, -1)
-    return [first, left_first, right_first, far_first], [second, left_second, right_second, far_second]
-
-
-def spread_weight(weight):
-    quarter = weight.shape[1] // 4
-    parts = [weight[:, n * quarter : (n + 1) * quarter] for n in range(4)]
-    pieces = []
-    for n, (near, far) in enumerate((("z", "x"), ("x", "z"))):
-        halves = around(parts[2 * n], parts[2 * n + 1], near)
-        first, second = (jnp.concatenate(half, axis=0) for half in halves)
-        for half in around(first, second, far):
-            pieces += half
-    return tuple(pieces)
-
-
 def exchange(array, axes):
     return lax.all_to_all(array, axes, split_axis=0, concat_axis=0, tiled=True)
 
@@ -505,28 +476,34 @@
     routes, route_weights, cotangent, w_gate, w_up, w_down,
 ):
     n_ctx = lax.axis_size("ctx")
-    width = residual.shape[1]
     at = lax.axis_index("ctx").astype(jnp.int32).reshape(1)
     n_x, n_z = lax.axis_size("x"), lax.axis_size("z")
+    n_core = lax.axis_size("core")
     near = jnp.array(NEAR, jnp.int32)
     at_x = (lax.axis_index("x") + near) % n_x
     at_z = (lax.axis_index("z") + near) % n_z
-    order = (at_x[:, None] * n_z + at_z[None, :]).reshape(-1)
-    place = jnp.concatenate([lax.axis_index("core").reshape(1), order]).astype(jnp.int32)
-
-    pieces = spread_weight(out_weight)
+    core = lax.axis_index("core")
+    sources = at_x[None, :] * n_core + jnp.stack([core, 1 - core])[:, None]
+    place = jnp.concatenate([at_z, sources.reshape(-1)]).astype(jnp.int32)
+
+    pieces = [out_weight] + [shift(out_weight, "x", -d) for d in NEAR[1:]]
+    pieces += [shift(piece, "core", 1) for piece in pieces]
     states = span_states(key_heads, value_heads, n_ctx)
     states = exchange(states, "ctx")
-    attention = attend(at, queries, key_heads, value_heads, states, out_gain[None])
-    by_chip = exchange(attention, CHIP)
+    attention = attend(
+        at, queries, key_heads, value_heads, states, out_gain[None], n_x, n_core
+    )
+    heads = exchange(attention, ("x", "core"))
     routes_t = routes.T
     cot = pack_cot(routes_t, route_weights.T, cotangent)
-    cot, by_chip, pieces = lax.optimization_barrier((cot, by_chip, pieces))
+    cot, heads = lax.optimization_barrier((cot, heads))
     cot = exchange(cot.reshape(EXPERTS, MAIN, -1), ALL)
 
-    mine, squares, theirs = project(place, by_chip, pieces, width)
-    got = lax.ppermute(theirs, "core", [(0, 1), (1, 0)])
-    hidden_out, moe = norm_pack(mine, squares, got, residual, norm_gain[None], routes_t)
+    mine, squares, *partial = project(place, heads, pieces)
+    arrived = [shift(part, "z", d) for part, d in zip(partial, NEAR[1:])]
+    hidden_out, moe = norm_pack(
+        mine, squares, arrived, residual, norm_gain[None], routes_t
+    )
     moe = exchange(moe.reshape(EXPERTS, MAIN, -1), ALL)
 
     moe = moe.reshape(EXPERTS * MAIN, -1)

time: 281 us -> 287 us (1.021)
  waiting for transfers between devices: 139 us -> 167 us
  starting transfers between devices: 58.6 us -> 41.2 us
    ppermute x24 -> x10, waiting for transfers between devices: 40.5 us -> 98.8 us  [shift(): lax.ppermute(array, axis, [(i, (i + by) % size) for i in range(size)])]
    all_to_all x4, waiting for transfers between devices: 97.7 us -> 67.9 us  [exchange(): return lax.all_to_all(array, axes, split_axis=0, concat_axis=0, tiled=True)]
    ppermute x24 -> x10, starting transfers between devices: 26.7 us -> 13.5 us  [shift(): lax.ppermute(array, axis, [(i, (i + by) % size) for i in range(size)])]
    all_to_all x4, starting transfers between devices: 30.8 us -> 27.7 us  [exchange(): return lax.all_to_all(array, axes, split_axis=0, concat_axis=0, tiled=True)]
    concatenate x5 -> x1, other arithmetic: 3.53 us -> 0.62 us  [on_device(): place = jnp.concatenate([at_z, sources.reshape(-1)]).astype(jnp.int32)]
  transfers between devices with their start and end apart: 29 -> 14, of which waited for: 8 -> 9; matrix products, arithmetic and copies ran while one was open for 2% -> 1% of each run, Pallas kernels for 15% -> 11%
where the time goes in v5:
time: 287 us; the launch traced here: 286 us
  waiting for transfers between devices  167 us (58%)
  Pallas kernels  73.3 us (26%)
  starting transfers between devices  41.2 us (14%)
  local copies, waits for them, and re-layouts  3.32 us (1%)
    ppermute x10, waiting for transfers between devices, shift(): lax.ppermute(array, axis, [(i, (i + by) % size) for i in range(size)])  98.8 us
    all_to_all x4, waiting for transfers between devices, exchange(): return lax.all_to_all(array, axes, split_axis=0, concat_axis=0, tiled=True)  67.9 us
    pallas_call x1, Pallas kernels, expert_grads(): pl.pallas_call(grads_kernel, grid=(blocks + width // block,), in_specs=[p...  30.6 us
    all_to_all x4, starting transfers between devices, exchange(): return lax.all_to_all(array, axes, split_axis=0, concat_axis=0, tiled=True)  27.7 us
    ppermute x10, starting transfers between devices, shift(): lax.ppermute(array, axis, [(i, (i + by) % size) for i in range(size)])  13.5 us
    pallas_call x1, Pallas kernels, hidden_grad(): pl.pallas_call(hidden_kernel, grid=(blocks + 1,), in_specs=[pl.BlockSpec(...  10.7 us
    pallas_call x1, Pallas kernels, project(): pl.pallas_call(project_kernel, grid_spec=pltpu.PrefetchScalarGridSpec(num...  9.1 us
    pallas_call x1, Pallas kernels, norm_pack(): pl.pallas_call(norm_pack_kernel, grid=(BLOCKS,), in_specs=[whole(a) for a...  7.02 us
  transfers between devices with their start and end apart: 14, of which 9 were waited for; matrix products, arithmetic and copies ran while one was open for 1% of the time, Pallas kernels for 11%

profile of v5, /device:TPU:1, one launch (start us, length us, event | category | flops | bytes accessed | tf_op | source)
XLA Modules:
  0.0 286.0 jit_solution(16761593479331694074)
XLA Ops:
  0.6 3.9 %shard_map.166 = bf16[4,128,256]{2,1,0:T(8,128)(2,1)} custom-call(bf16[4096,128]{1,0:T(8,128)(2,1)} %k_ref.3, bf16[4096,128]{1,0:T(8,128)(2,1)} %v_ref.3), custom_call_target="tpu_custom_call" | custom-call | tf_op jit(solution)/shard_map/pallas_call | solution.py:57
  4.5 5.0 %all-to-all-start = ((bf16[4,128,256]{2,1,0:T(8,128)(2,1)}), bf16[4,128,256]{2,1,0:T(8,128)(2,1)S(1)}, u32[]{:S(2)}, u32[]{:S(2)}) async-start(bf16[4,128,256]{2,1,0:T(8,128)(2,1)} %shard_map.166), calls=%async_computation | async-start | bytes 524288 | tf_op jit(solution)/shard_map/all_to_all | solution.py:471
  9.5 5.6 %all-to-all-done.s_ref = bf16[4,128,256]{2,1,0:T(8,128)(2,1)S(1)} async-done(((bf16[4,128,256]{2,1,0:T(8,128)(2,1)}), bf16[4,128,256]{2,1,0:T(8,128)(2,1)S(1)}, u32[]{:S(2)}, u32[]{:S(2)}) %all-to-all-start) | async-done | bytes 262176 | tf_op jit(solution)/shard_map/all_to_all | solution.py:471
  15.1 0.7 copy-done.1
  15.8 5.9 %shard_map.167 = bf16[8,528,128]{2,1,0:T(8,128)(2,1)} custom-call(s32[1]{0:T(128)} %bitcast.4.at_ref, bf16[4096,128]{1,0:T(8,128)(2,1)} %q_ref.1, bf16[4096,128]{1,0:T(8,128)(2,1)} %k_ref.3, bf16[4096,128]{1,0:T(8,128)(2,1)} %v_ref.3, bf16[4,128,256]{2,1,0:T(8,128)(2,1)} %copy-done.1, bf16[1,128]{1,0:T(2,128)(2,1)} %bitcast.24), custom_call_target="tpu_custom_call" | custom-call | tf_op jit(solution)/shard_map/pallas_call | solution.py:107
  21.7 6.4 %all-to-all-start.1 = ((bf16[8,528,128]{2,1,0:T(8,128)(2,1)}), bf16[8,528,128]{2,1,0:T(8,128)(2,1)S(1)}, u32[]{:S(2)}, u32[]{:S(2)}) async-start(bf16[8,528,128]{2,1,0:T(8,128)(2,1)} %shard_map.167), calls=%async_computation.1 | async-start | bytes 2162688 | tf_op jit(solution)/shard_map/all_to_all | solution.py:471
  28.0 6.0 %shard_map.165 = bf16[1024,2560]{1,0:T(8,128)(2,1)} custom-call(s32[8,128]{1,0:T(8,128)} %bitcast.21, f32[8,128]{1,0:T(8,128)} %bitcast.23, bf16[128,2048]{1,0:T(8,128)(2,1)} %cot_ref.1), custom_call_target="tpu_custom_call" | custom-call | tf_op jit(solution)/shard_map/pallas_call | solution.py:207
  34.1 9.3 %all-to-all-done.1.x_ref = bf16[8,528,128]{2,1,0:T(8,128)(2,1)S(1)} async-done(((bf16[8,528,128]{2,1,0:T(8,128)(2,1)}), bf16[8,528,128]{2,1,0:T(8,128)(2,1)S(1)}, u32[]{:S(2)}, u32[]{:S(2)}) %all-to-all-start.1) | async-done | bytes 1081376 | tf_op jit(solution)/shard_map/all_to_all | solution.py:471
  43.4 1.0 copy-done
  44.3 7.5 %all-to-all-start.3 = ((bf16[128,8,2560]{2,1,0:T(8,128)(2,1)}), bf16[128,8,2560]{2,1,0:T(8,128)(2,1)}, u32[]{:S(2)}, u32[]{:S(2)}) async-start(bf16[128,8,2560]{2,1,0:T(8,128)(2,1)} %bitcast.16), calls=%async_computation.3 | async-start | bytes 10485760 | tf_op jit(solution)/shard_map/all_to_all | solution.py:471
  51.8 2.9 %collective-permute-start.2 = (bf16[128,2048]{1,0:T(8,128)(2,1)S(1)}, bf16[128,2048]{1,0:T(8,128)(2,1)S(1)}, u32[]{:S(2)}, u32[]{:S(2)}) collective-permute-start(bf16[128,2048]{1,0:T(8,128)(2,1)S(1)} %copy-done.5), channel_id=1, source_target_pairs={{0,16},{8,24},{16,0},{24,8},{1,17},{9,25},{17,1},{25,9},{2,18},{10... | collective-permute-start | bytes 1572872 | tf_op jit(solution)/shard_map/ppermute | solution.py:467
  54.8 0.9 collective-permute-start.1
  56.2 1.2 collective-permute-start.3
  57.6 64.2 %collective-permute-done.2.refs_3_ = bf16[128,2048]{1,0:T(8,128)(2,1)S(1)} collective-permute-done((bf16[128,2048]{1,0:T(8,128)(2,1)S(1)}, bf16[128,2048]{1,0:T(8,128)(2,1)S(1)}, u32[]{:S(2)}, u32[]{:S(2)}) %collective-permute-start.2) | collective-permute-done | bytes 524320 | tf_op jit(solution)/shard_map/ppermute | solution.py:467
  121.8 1.4 collective-permute-start.6
  123.2 8.3 %collective-permute-done.1.refs_2_ = bf16[128,2048]{1,0:T(8,128)(2,1)S(1)} collective-permute-done((bf16[128,2048]{1,0:T(8,128)(2,1)S(1)}, bf16[128,2048]{1,0:T(8,128)(2,1)S(1)}, u32[]{:S(2)}, u32[]{:S(2)}) %collective-permute-start.1) | collective-permute-done | bytes 524320 | tf_op jit(solution)/shard_map/ppermute | solution.py:467
  131.6 1.0 collective-permute-start.5
  132.8 0.8 collective-permute-start.4
  133.8 0.6 pad_add_fusion.1.place_ref
  134.4 0.8 collective-permute-done.4.refs_5_
  135.4 9.1 %shard_map.168 = (f32[128,2048]{1,0:T(8,128)}, f32[128,128]{1,0:T(8,128)}, bf16[128,2304]{1,0:T(8,128)(2,1)}, bf16[128,2304]{1,0:T(8,128)(2,1)}, bf16[128,2304]{1,0:T(8,128)(2,1)}) custom-call(s32[12]{0:T(128)} %pad_add_fusion.1.place_ref, bf16[8,528,128]{2,1,0:T(8,128)(2,1)} %copy-done, bf16[128,2048]{1,0:T(8,128)(2,1)} %refs_0_.1, ...), custom_call_target="tpu_custom_call" | custom-call | tf_op jit(solution)/shard_map/pallas_call | solution.py:255
  144.5 3.1 %collective-permute-start.7 = (bf16[128,2304]{1,0:T(8,128)(2,1)}, bf16[128,2304]{1,0:T(8,128)(2,1)S(1)}, u32[]{:S(2)}, u32[]{:S(2)}) collective-permute-start(bf16[128,2304]{1,0:T(8,128)(2,1)} %get-tuple-element.21), channel_id=1, source_target_pairs={{0,6},{2,0},{4,2},{6,4},{1,7},{3,1},{5,3},{7,5},{8,14},{10,8},{12,... | collective-permute-start | bytes 1769480 | tf_op jit(solution)/shard_map/ppermute | solution.py:467
  147.6 1.5 collective-permute-start.9
  149.1 0.6 broadcast_in_dim.18.gain_ref
  149.7 23.1 %collective-permute-done.7.got_a = bf16[128,2304]{1,0:T(8,128)(2,1)S(1)} collective-permute-done((bf16[128,2304]{1,0:T(8,128)(2,1)}, bf16[128,2304]{1,0:T(8,128)(2,1)S(1)}, u32[]{:S(2)}, u32[]{:S(2)}) %collective-permute-start.7) | collective-permute-done | bytes 589856 | tf_op jit(solution)/shard_map/ppermute | solution.py:467
  172.8 2.1 collective-permute-done.9.got_c
  174.9 0.8 copy-done.4
  175.7 7.0 %shard_map.169 = (bf16[128,2048]{1,0:T(8,128)(2,1)}, bf16[1024,2560]{1,0:T(8,128)(2,1)}) custom-call(f32[128,2048]{1,0:T(8,128)} %get-tuple-element.19.mine_ref, f32[128,128]{1,0:T(8,128)} %get-tuple-element.20.ss_ref, bf16[128,2304]{1,0:T(8,128)(2,1)} %copy-done.2, bf16[128,2304]{1,0:T(8,128)(2,1)} %copy-done.3, bf16[128,2304]{1,0:T(8,128)(2,1)} %copy-done.4, ...), custom_call_target="tpu_custom_call" | custom-call | tf_op jit(solution)/shard_map/pallas_call | solution.py:305
  182.7 8.8 %all-to-all-start.2 = ((bf16[128,8,2560]{2,1,0:T(8,128)(2,1)}), bf16[128,8,2560]{2,1,0:T(8,128)(2,1)}, u32[]{:S(2)}, u32[]{:S(2)}) async-start(bf16[128,8,2560]{2,1,0:T(8,128)(2,1)} %bitcast.17), calls=%async_computation.2 | async-start | bytes 10485760 | tf_op jit(solution)/shard_map/all_to_all | solution.py:471
  191.5 10.7 %shard_map.170 = (f32[1280,768]{1,0:T(8,128)}, bf16[256,2048]{1,0:T(8,128)(2,1)}) custom-call(bf16[1024,2560]{1,0:T(8,128)(2,1)} %bitcast.9.rows_ref.tail_ref.scaled_ref, bf16[1024,2560]{1,0:T(8,128)(2,1)} %bitcast.9.rows_ref.tail_ref.scaled_ref, bf16[768,2048]{1,0:T(8,128)(2,1)} %bitcast.20), custom_call_target="tpu_custom_call" | custom-call | tf_op jit(solution)/shard_map/pallas_call | solution.py:355
  202.3 53.1 %all-to-all-done.2 = bf16[128,8,2560]{2,1,0:T(8,128)(2,1)} async-done(((bf16[128,8,2560]{2,1,0:T(8,128)(2,1)}), bf16[128,8,2560]{2,1,0:T(8,128)(2,1)}, u32[]{:S(2)}, u32[]{:S(2)}) %all-to-all-start.2) | async-done | bytes 5242912 | tf_op jit(solution)/shard_map/all_to_all | solution.py:471
  255.3 30.6 %shard_map.171 = (bf16[2048,768]{1,0:T(8,128)(2,1)}, bf16[2048,768]{1,0:T(8,128)(2,1)}, bf16[768,2048]{1,0:T(8,128)(2,1)}) custom-call(bf16[1024,2560]{1,0:T(8,128)(2,1)} %bitcast.7.x_ref.tail_ref, bf16[1024,2560]{1,0:T(8,128)(2,1)} %bitcast.7.x_ref.tail_ref, f32[1280,768]{1,0:T(8,128)} %get-tuple-element.27.back_ref, bf16[2048,768]{1,0:T(8,128)(2,1)} %bitcast.18, ...), custom_call_target="tpu_custom_call" | custom-call | tf_op jit(solution)/shard_map/pallas_call | solution.py:434
  (35 shorter events, 1.3 us)
Async XLA Ops:
  4.5 10.6 %all-to-all-start = ((bf16[4,128,256]{2,1,0:T(8,128)(2,1)}), bf16[4,128,256]{2,1,0:T(8,128)(2,1)S(1)}, u32[]{:S(2)}, u32[]{:S(2)}) async-start(bf16[4,128,256]{2,1,0:T(8,128)(2,1)} %shard_map.166), calls=%async_computation | async-start | bytes 524288 | tf_op jit(solution)/shard_map/all_to_all | solution.py:471
  15.1 0.7 copy-start.1
  21.7 21.7 %all-to-all-start.1 = ((bf16[8,528,128]{2,1,0:T(8,128)(2,1)}), bf16[8,528,128]{2,1,0:T(8,128)(2,1)S(1)}, u32[]{:S(2)}, u32[]{:S(2)}) async-start(bf16[8,528,128]{2,1,0:T(8,128)(2,1)} %shard_map.167), calls=%async_computation.1 | async-start | bytes 2162688 | tf_op jit(solution)/shard_map/all_to_all | solution.py:471
  43.4 1.0 copy-start
  43.4 8.5 %copy-start.5 = (bf16[128,2048]{1,0:T(8,128)(2,1)S(1)}, bf16[128,2048]{1,0:T(8,128)(2,1)}, u32[]{:S(2)}) copy-start(bf16[128,2048]{1,0:T(8,128)(2,1)} %refs_0_.1) | copy-start | bytes 1572868
  43.4 90.3 %copy-start.12 = (s32[4]{0:T(128)S(1)}, s32[4]{0:T(128)}, u32[]{:S(2)}) copy-start(s32[4]{0:T(128)} %constant.41.clone) | copy-start | bytes 52
  44.3 138.4 %all-to-all-start.3 = ((bf16[128,8,2560]{2,1,0:T(8,128)(2,1)}), bf16[128,8,2560]{2,1,0:T(8,128)(2,1)}, u32[]{:S(2)}, u32[]{:S(2)}) async-start(bf16[128,8,2560]{2,1,0:T(8,128)(2,1)} %bitcast.16), calls=%async_computation.3 | async-start | bytes 10485760 | tf_op jit(solution)/shard_map/all_to_all | solution.py:471
  51.8 97.3 %copy-start.11 = (bf16[2048]{0:T(1024)(128)(2,1)S(1)}, bf16[2048]{0:T(1024)(128)(2,1)}, u32[]{:S(2)}) copy-start(bf16[2048]{0:T(1024)(128)(2,1)} %param.20) | copy-start | bytes 12292
  51.8 70.0 %collective-permute-start.2 = (bf16[128,2048]{1,0:T(8,128)(2,1)S(1)}, bf16[128,2048]{1,0:T(8,128)(2,1)S(1)}, u32[]{:S(2)}, u32[]{:S(2)}) collective-permute-start(bf16[128,2048]{1,0:T(8,128)(2,1)S(1)} %copy-done.5), channel_id=1, source_target_pairs={{0,16},{8,24},{16,0},{24,8},{1,17},{9,25},{17,1},{25,9},{2,18},{10... | collective-permute-start | bytes 1572872 | tf_op jit(solution)/shard_map/ppermute | solution.py:467
  54.8 76.8 %collective-permute-start.1 = (bf16[128,2048]{1,0:T(8,128)(2,1)S(1)}, bf16[128,2048]{1,0:T(8,128)(2,1)S(1)}, u32[]{:S(2)}, u32[]{:S(2)}) collective-permute-start(bf16[128,2048]{1,0:T(8,128)(2,1)S(1)} %copy-done.5), channel_id=1, source_target_pairs={{0,24},{8,0},{16,8},{24,16},{1,25},{9,1},{17,9},{25,17},{2,26},{10... | collective-permute-start | bytes 1572872 | tf_op jit(solution)/shard_map/ppermute | solution.py:467
  55.7 77.2 %collective-permute-start = (bf16[128,2048]{1,0:T(8,128)(2,1)S(1)}, bf16[128,2048]{1,0:T(8,128)(2,1)S(1)}, u32[]{:S(2)}, u32[]{:S(2)}) collective-permute-start(bf16[128,2048]{1,0:T(8,128)(2,1)S(1)} %copy-done.5), channel_id=1, source_target_pairs={{0,8},{8,16},{16,24},{24,0},{1,9},{9,17},{17,25},{25,1},{2,10},{10... | collective-permute-start | bytes 1572872 | tf_op jit(solution)/shard_map/ppermute | solution.py:467
  56.2 78.2 %collective-permute-start.3 = (bf16[128,2048]{1,0:T(8,128)(2,1)S(1)}, bf16[128,2048]{1,0:T(8,128)(2,1)S(1)}, u32[]{:S(2)}, u32[]{:S(2)}) collective-permute-start(bf16[128,2048]{1,0:T(8,128)(2,1)S(1)} %copy-done.5), channel_id=1, source_target_pairs={{0,1},{1,0},{2,3},{3,2},{4,5},{5,4},{6,7},{7,6},{8,9},{9,8},{10,11... | collective-permute-start | bytes 1572872 | tf_op jit(solution)/shard_map/ppermute | solution.py:467
  121.8 13.5 %copy-start.6 = (bf16[128,2048]{1,0:T(8,128)(2,1)}, bf16[128,2048]{1,0:T(8,128)(2,1)S(1)}, u32[]{:S(2)}) copy-start(bf16[128,2048]{1,0:T(8,128)(2,1)S(1)} %collective-permute-done.2.refs_3_) | copy-start | bytes 1572868
  121.8 12.6 %collective-permute-start.6 = (bf16[128,2048]{1,0:T(8,128)(2,1)S(1)}, bf16[128,2048]{1,0:T(8,128)(2,1)S(1)}, u32[]{:S(2)}, u32[]{:S(2)}) collective-permute-start(bf16[128,2048]{1,0:T(8,128)(2,1)S(1)} %collective-permute-done.2.refs_3_), channel_id=1, source_target_pairs={{0,1},{1,0},{2,3},{3,2},{4,5},{5,4},{6,7},{7,6},{8,9},{9,8},{10,11... | collective-permute-start | bytes 1572872 | tf_op jit(solution)/shard_map/ppermute | solution.py:467
  131.6 3.7 %copy-start.7 = (bf16[128,2048]{1,0:T(8,128)(2,1)}, bf16[128,2048]{1,0:T(8,128)(2,1)S(1)}, u32[]{:S(2)}) copy-start(bf16[128,2048]{1,0:T(8,128)(2,1)S(1)} %collective-permute-done.1.refs_2_) | copy-start | bytes 1572868
  131.6 2.9 %collective-permute-start.5 = (bf16[128,2048]{1,0:T(8,128)(2,1)S(1)}, bf16[128,2048]{1,0:T(8,128)(2,1)}, u32[]{:S(2)}, u32[]{:S(2)}) collective-permute-start(bf16[128,2048]{1,0:T(8,128)(2,1)S(1)} %collective-permute-done.1.refs_2_), channel_id=1, source_target_pairs={{0,1},{1,0},{2,3},{3,2},{4,5},{5,4},{6,7},{7,6},{8,9},{9,8},{10,11... | collective-permute-start | bytes 1572872 | tf_op jit(solution)/shard_map/ppermute | solution.py:467
  132.8 2.5 copy-start.8
  132.8 2.5 collective-permute-start.4
  134.4 0.9 copy-start.9
  134.4 1.0 copy-start.10
  144.5 28.3 %collective-permute-start.7 = (bf16[128,2304]{1,0:T(8,128)(2,1)}, bf16[128,2304]{1,0:T(8,128)(2,1)S(1)}, u32[]{:S(2)}, u32[]{:S(2)}) collective-permute-start(bf16[128,2304]{1,0:T(8,128)(2,1)} %get-tuple-element.21), channel_id=1, source_target_pairs={{0,6},{2,0},{4,2},{6,4},{1,7},{3,1},{5,3},{7,5},{8,14},{10,8},{12,... | collective-permute-start | bytes 1769480 | tf_op jit(solution)/shard_map/ppermute | solution.py:467
  147.6 25.2 %collective-permute-start.8 = (bf16[128,2304]{1,0:T(8,128)(2,1)}, bf16[128,2304]{1,0:T(8,128)(2,1)S(1)}, u32[]{:S(2)}, u32[]{:S(2)}) collective-permute-start(bf16[128,2304]{1,0:T(8,128)(2,1)} %get-tuple-element.22), channel_id=1, source_target_pairs={{0,2},{2,4},{4,6},{6,0},{1,3},{3,5},{5,7},{7,1},{8,10},{10,12},{12... | collective-permute-start | bytes 1769480 | tf_op jit(solution)/shard_map/ppermute | solution.py:467
  147.6 27.2 %collective-permute-start.9 = (bf16[128,2304]{1,0:T(8,128)(2,1)}, bf16[128,2304]{1,0:T(8,128)(2,1)S(1)}, u32[]{:S(2)}, u32[]{:S(2)}) collective-permute-start(bf16[128,2304]{1,0:T(8,128)(2,1)} %get-tuple-element.23), channel_id=1, source_target_pairs={{0,4},{2,6},{4,0},{6,2},{1,5},{3,7},{5,1},{7,3},{8,12},{10,14},{12... | collective-permute-start | bytes 1769480 | tf_op jit(solution)/shard_map/ppermute | solution.py:467
  172.8 2.1 copy-start.2
  172.8 2.1 copy-start.3
  174.8 0.8 copy-start.4
  182.7 72.6 %all-to-all-start.2 = ((bf16[128,8,2560]{2,1,0:T(8,128)(2,1)}), bf16[128,8,2560]{2,1,0:T(8,128)(2,1)}, u32[]{:S(2)}, u32[]{:S(2)}) async-start(bf16[128,8,2560]{2,1,0:T(8,128)(2,1)} %bitcast.17), calls=%async_computation.2 | async-start | bytes 10485760 | tf_op jit(solution)/shard_map/all_to_all | solution.py:471

commit v6 on v5

--- a/solution.py
+++ b/solution.py
@@ -157,7 +157,7 @@
 BLOCKS = 4
 
 
-def pack_cot_kernel(routes_ref, weights_ref, cot_ref, out_ref, rank_s, weight_s):
+def pack_cot_kernel(routes_ref, weights_ref, cot_ref, first_ref, rest_ref, rank_s, weight_s):
     step = pl.program_id(0)
 
     @pl.when(step == 0)
@@ -184,15 +184,17 @@
     main, tail, quarter = picks(rank_s[part, :])
     table = cot_ref[...]
     scale = jnp.sum(jnp.where(main, weight8, 0.0), axis=1, keepdims=True)
-    width = table.shape[1]
-    out_ref[:, :width] = (dot(jnp.where(main, 1.0, 0.0).astype(BF), table) * scale).astype(BF)
+    half = first_ref.shape[1]
+    rows = (dot(jnp.where(main, 1.0, 0.0).astype(BF), table) * scale).astype(BF)
+    first_ref[...] = rows[:, :half]
+    rest_ref[:, :half] = rows[:, half:]
     scale = jnp.sum(jnp.where(tail, weight8, 0.0), axis=1, keepdims=True)
-    out_ref[:, width:] = (tail_rows(tail, quarter, table) * scale).astype(BF)
-
-
-def packed(width):
+    rest_ref[:, half:] = (tail_rows(tail, quarter, table) * scale).astype(BF)
+
+
+def packed(main, tail):
     rows = EXPERTS * MAIN
-    wide = width + width // QUART
+    wide = main + tail
     spec = pl.BlockSpec((rows // BLOCKS, wide), lambda i: (i, 0))
     return spec, jax.ShapeDtypeStruct((rows, wide), BF)
 
@@ -203,13 +205,13 @@
 
 def pack_cot(routes_t, weights_t, cotangent):
     tokens, width = cotangent.shape
-    spec, shape = packed(width)
+    first, rest = packed(width // 2, 0), packed(width // 2, width // QUART)
     return pl.pallas_call(
         pack_cot_kernel,
         grid=(BLOCKS,),
         in_specs=[whole(routes_t), whole(weights_t), whole(cotangent)],
-        out_specs=spec,
-        out_shape=shape,
+        out_specs=[first[0], rest[0]],
+        out_shape=[first[1], rest[1]],
         scratch_shapes=[pltpu.VMEM((EXPERTS * MAIN, tokens), F32)] * 2,
         compiler_params=params(),
     )(routes_t, weights_t, cotangent)
@@ -300,7 +302,7 @@
 
 def norm_pack(mine, squares, arrived, residual, gain, routes_t):
     tokens, width = residual.shape
-    spec, shape = packed(width)
+    spec, shape = packed(width, width // QUART)
     args = (mine, squares) + tuple(arrived) + (residual, gain, routes_t)
     return pl.pallas_call(
         norm_pack_kernel,
@@ -330,13 +332,15 @@
         keep(slice(q * width, (q + 1) * width), piece.astype(BF))
 
 
-def hidden_kernel(rows_ref, tail_ref, down_ref, out_ref, scaled_ref):
+def hidden_kernel(first_ref, second_ref, tail_ref, down_ref, out_ref, scaled_ref):
     step = pl.program_id(0)
     last = pl.num_programs(0) - 1
 
     @pl.when(step < last)
     def _():
-        out_ref[...] = dot(rows_ref[...], down_ref[...], 1, 1)
+        half = first_ref.shape[1]
+        total = dot(first_ref[...], down_ref[:, :half], 1, 1)
+        out_ref[...] = total + dot(second_ref[...], down_ref[:, half:], 1, 1)
 
     @pl.when(step == last)
     def _():
@@ -347,17 +351,19 @@
         out_ref[...] = dot(scaled_ref[...], down_ref[...], 1, 1)
 
 
-def hidden_grad(cot, down):
-    rows = cot.shape[0]
+def hidden_grad(first, rest, down):
+    rows, half = first.shape
     units, width = down.shape
     blocks = rows // ROWS
     tails = rows // MAIN * TAIL
+    part = pl.BlockSpec((ROWS, half), lambda i: (jnp.minimum(i, blocks - 1), 0))
     return pl.pallas_call(
         hidden_kernel,
         grid=(blocks + 1,),
         in_specs=[
-            pl.BlockSpec((ROWS, width), lambda i: (jnp.minimum(i, blocks - 1), 0)),
-            pl.BlockSpec((rows, width // QUART), lambda i: (0, QUART)),
+            part,
+            part,
+            pl.BlockSpec((rows, width // QUART), lambda i: (0, QUART // 2)),
             whole(down),
         ],
         out_specs=[
@@ -369,11 +375,11 @@
             jax.ShapeDtypeStruct((tails, width), BF),
         ],
         compiler_params=params(),
-    )(cot, cot, down)
+    )(first, rest, rest, down)
 
 
 def grads_kernel(
-    x_ref, tail_ref, back_ref, gate_ref, up_ref, scaled_ref, scaled_tail_ref,
+    x_ref, tail_ref, back_ref, gate_ref, up_ref, first_ref, second_ref, scaled_tail_ref,
     grad_gate_ref, grad_up_ref, grad_down_ref, x_s, hidden_s, pre_s,
 ):
     step = pl.program_id(0)
@@ -416,18 +422,26 @@
         both = dot(x, pre_s[...], 0, 0)
         grad_gate_ref[...] = both[:, :units].astype(BF)
         grad_up_ref[...] = both[:, units:].astype(BF)
-        main = scaled_ref.shape[0]
-        down = dot(hidden_s[:, :main], scaled_ref[...])
-        down = down + dot(hidden_s[:, main:], scaled_tail_ref[...])
-        grad_down_ref[...] = down.astype(BF)
-
-
-def expert_grads(moe, cot, scaled_tail, back, gate, up):
+        main = first_ref.shape[0]
+        rest = dot(hidden_s[:, main:], scaled_tail_ref[...])
+        middle = blocks + (pl.num_programs(0) - blocks) // 2
+
+        @pl.when(step < middle)
+        def _():
+            grad_down_ref[...] = (dot(hidden_s[:, :main], first_ref[...]) + rest).astype(BF)
+
+        @pl.when(step >= middle)
+        def _():
+            grad_down_ref[...] = (dot(hidden_s[:, :main], second_ref[...]) + rest).astype(BF)
+
+
+def expert_grads(moe, first, rest, scaled_tail, back, gate, up):
     main = moe.shape[0]
     width, units = gate.shape
     total = back.shape[0]
     blocks = total // ROWS
     block = 512
+    halves = width // 2 // block
     at_rows = lambda i: (jnp.minimum(i, blocks - 2), 0)
     at_cols = lambda i: (0, jnp.maximum(i - blocks, 0))
     at_out = lambda i: (jnp.maximum(i - blocks, 0), 0)
@@ -440,7 +454,8 @@
             pl.BlockSpec((ROWS, units), lambda i: (jnp.minimum(i, blocks - 1), 0)),
             whole(gate),
             whole(up),
-            pl.BlockSpec((main, block), at_cols),
+            pl.BlockSpec((main, block), lambda i: (0, jnp.clip(i - blocks, 0, halves - 1))),
+            pl.BlockSpec((main, block), lambda i: (0, jnp.maximum(i - blocks - halves, 0))),
             pl.BlockSpec((total - main, block), at_cols),
         ],
         out_specs=[
@@ -459,7 +474,7 @@
             pltpu.VMEM((total, 2 * units), BF),
         ],
         compiler_params=params(),
-    )(moe, moe, back, gate, up, cot, scaled_tail)
+    )(moe, moe, back, gate, up, first, rest, scaled_tail)
 
 
 def shift(array, axis, by):
@@ -495,21 +510,24 @@
     )
     heads = exchange(attention, ("x", "core"))
     routes_t = routes.T
-    cot = pack_cot(routes_t, route_weights.T, cotangent)
-    cot, heads = lax.optimization_barrier((cot, heads))
-    cot = exchange(cot.reshape(EXPERTS, MAIN, -1), ALL)
+    first, rest = pack_cot(routes_t, route_weights.T, cotangent)
+    first, heads = lax.optimization_barrier((first, heads))
+    first = exchange(first.reshape(EXPERTS, MAIN, -1), ALL)
 
     mine, squares, *partial = project(place, heads, pieces)
+    rest, first, _ = lax.optimization_barrier((rest, first, partial))
     arrived = [shift(part, "z", d) for part, d in zip(partial, NEAR[1:])]
+    rest = exchange(rest.reshape(EXPERTS, MAIN, -1), ALL)
     hidden_out, moe = norm_pack(
         mine, squares, arrived, residual, norm_gain[None], routes_t
     )
     moe = exchange(moe.reshape(EXPERTS, MAIN, -1), ALL)
 
     moe = moe.reshape(EXPERTS * MAIN, -1)
-    cot = cot.reshape(EXPERTS * MAIN, -1)
-    back, scaled_tail = hidden_grad(cot, w_down[0])
-    grads = expert_grads(moe, cot, scaled_tail, back, w_gate[0], w_up[0])
+    first = first.reshape(EXPERTS * MAIN, -1)
+    rest = rest.reshape(EXPERTS * MAIN, -1)
+    back, scaled_tail = hidden_grad(first, rest, w_down[0])
+    grads = expert_grads(moe, first, rest, scaled_tail, back, w_gate[0], w_up[0])
     return (hidden_out,) + tuple(g[None] for g in grads)
 
 

time: 287 us -> 297 us (1.035)
  starting transfers between devices: 41.2 us -> 49 us
    all_to_all x4 -> x5, starting transfers between devices: 27.7 us -> 35.2 us  [exchange(): return lax.all_to_all(array, axes, split_axis=0, concat_axis=0, tiled=True)]
    all_to_all x4 -> x5, waiting for transfers between devices: 67.9 us -> 68.4 us  [exchange(): return lax.all_to_all(array, axes, split_axis=0, concat_axis=0, tiled=True)]
  transfers between devices with their start and end apart: 14 -> 15, of which waited for: 9 -> 9; matrix products, arithmetic and copies ran while one was open for 1% -> 0% of each run, Pallas kernels for 11% -> 11%
where the time goes in v6:
time: 297 us
  waiting for transfers between devices  167 us (56%)
  Pallas kernels  74 us (25%)
  starting transfers between devices  49 us (16%)
  local copies, waits for them, and re-layouts  5.35 us (2%)
    ppermute x10, waiting for transfers between devices, shift(): lax.ppermute(array, axis, [(i, (i + by) % size) for i in range(size)])  98.7 us
    all_to_all x5, waiting for transfers between devices, exchange(): return lax.all_to_all(array, axes, split_axis=0, concat_axis=0, tiled=True)  68.4 us
    all_to_all x5, starting transfers between devices, exchange(): return lax.all_to_all(array, axes, split_axis=0, concat_axis=0, tiled=True)  35.2 us
    pallas_call x1, Pallas kernels, expert_grads(): pl.pallas_call(grads_kernel, grid=(blocks + width // block,), in_specs=[p...  31.8 us
    ppermute x10, starting transfers between devices, shift(): lax.ppermute(array, axis, [(i, (i + by) % size) for i in range(size)])  13.7 us
    pallas_call x1, Pallas kernels, hidden_grad(): pl.pallas_call(hidden_kernel, grid=(blocks + 1,), in_specs=[part, part, p...  10.7 us
    pallas_call x1, Pallas kernels, project(): pl.pallas_call(project_kernel, grid_spec=pltpu.PrefetchScalarGridSpec(num...  9.1 us
    pallas_call x1, Pallas kernels, norm_pack(): pl.pallas_call(norm_pack_kernel, grid=(BLOCKS,), in_specs=[whole(a) for a...  7.01 us
  transfers between devices with their start and end apart: 15, of which 9 were waited for; matrix products, arithmetic and copies ran while one was open for 0% of the time, Pallas kernels for 11%

profile of v6, /device:TPU:1, one launch (start us, length us, event | category | flops | bytes accessed | tf_op | source)
XLA Modules:
  0.0 296.8 jit_solution(4789564116962927123)
XLA Ops:
  0.6 3.9 %shard_map.166 = bf16[4,128,256]{2,1,0:T(8,128)(2,1)} custom-call(bf16[4096,128]{1,0:T(8,128)(2,1)} %k_ref.3, bf16[4096,128]{1,0:T(8,128)(2,1)} %v_ref.3), custom_call_target="tpu_custom_call" | custom-call | tf_op jit(solution)/shard_map/pallas_call | solution.py:57
  4.5 5.0 %all-to-all-start = ((bf16[4,128,256]{2,1,0:T(8,128)(2,1)}), bf16[4,128,256]{2,1,0:T(8,128)(2,1)S(1)}, u32[]{:S(2)}, u32[]{:S(2)}) async-start(bf16[4,128,256]{2,1,0:T(8,128)(2,1)} %shard_map.166), calls=%async_computation | async-start | bytes 524288 | tf_op jit(solution)/shard_map/all_to_all | solution.py:486
  9.5 5.6 %all-to-all-done.s_ref = bf16[4,128,256]{2,1,0:T(8,128)(2,1)S(1)} async-done(((bf16[4,128,256]{2,1,0:T(8,128)(2,1)}), bf16[4,128,256]{2,1,0:T(8,128)(2,1)S(1)}, u32[]{:S(2)}, u32[]{:S(2)}) %all-to-all-start) | async-done | bytes 262176 | tf_op jit(solution)/shard_map/all_to_all | solution.py:486
  15.1 0.7 copy-done.3
  15.8 5.9 %shard_map.167 = bf16[8,528,128]{2,1,0:T(8,128)(2,1)} custom-call(s32[1]{0:T(128)} %bitcast.4.at_ref, bf16[4096,128]{1,0:T(8,128)(2,1)} %q_ref.1, bf16[4096,128]{1,0:T(8,128)(2,1)} %k_ref.3, bf16[4096,128]{1,0:T(8,128)(2,1)} %v_ref.3, bf16[4,128,256]{2,1,0:T(8,128)(2,1)} %copy-done.3, bf16[1,128]{1,0:T(2,128)(2,1)} %bitcast.32), custom_call_target="tpu_custom_call" | custom-call | tf_op jit(solution)/shard_map/pallas_call | solution.py:107
  21.7 6.5 %all-to-all-start.1 = ((bf16[8,528,128]{2,1,0:T(8,128)(2,1)}), bf16[8,528,128]{2,1,0:T(8,128)(2,1)S(1)}, u32[]{:S(2)}, u32[]{:S(2)}) async-start(bf16[8,528,128]{2,1,0:T(8,128)(2,1)} %shard_map.167), calls=%async_computation.1 | async-start | bytes 2162688 | tf_op jit(solution)/shard_map/all_to_all | solution.py:486
  28.2 5.6 %shard_map.165 = (bf16[1024,1024]{1,0:T(8,128)(2,1)}, bf16[1024,1536]{1,0:T(8,128)(2,1)}) custom-call(s32[8,128]{1,0:T(8,128)} %bitcast.29, f32[8,128]{1,0:T(8,128)} %bitcast.31, bf16[128,2048]{1,0:T(8,128)(2,1)} %cot_ref.1), custom_call_target="tpu_custom_call" | custom-call | tf_op jit(solution)/shard_map/pallas_call | solution.py:209
  33.8 9.7 %all-to-all-done.1.x_ref = bf16[8,528,128]{2,1,0:T(8,128)(2,1)S(1)} async-done(((bf16[8,528,128]{2,1,0:T(8,128)(2,1)}), bf16[8,528,128]{2,1,0:T(8,128)(2,1)S(1)}, u32[]{:S(2)}, u32[]{:S(2)}) %all-to-all-start.1) | async-done | bytes 1081376 | tf_op jit(solution)/shard_map/all_to_all | solution.py:486
  43.5 7.1 %all-to-all-start.3 = ((bf16[128,8,1024]{2,1,0:T(8,128)(2,1)}), bf16[128,8,1024]{2,1,0:T(8,128)(2,1)S(1)}, u32[]{:S(2)}, u32[]{:S(2)}) async-start(bf16[128,8,1024]{2,1,0:T(8,128)(2,1)} %bitcast.28), calls=%async_computation.3 | async-start | bytes 4194304 | tf_op jit(solution)/shard_map/all_to_all | solution.py:486
  50.6 2.9 collective-permute-start.2
  53.5 0.9 collective-permute-start.1
  55.0 1.2 collective-permute-start.3
  56.3 31.0 %collective-permute-done.2.refs_3_ = bf16[128,2048]{1,0:T(8,128)(2,1)} collective-permute-done((bf16[128,2048]{1,0:T(8,128)(2,1)}, bf16[128,2048]{1,0:T(8,128)(2,1)}, u32[]{:S(2)}, u32[]{:S(2)}) %collective-permute-start.2) | collective-permute-done | bytes 524320 | tf_op jit(solution)/shard_map/ppermute | solution.py:482
  87.2 1.5 collective-permute-start.6
  88.8 8.2 %collective-permute-done.1.refs_2_ = bf16[128,2048]{1,0:T(8,128)(2,1)} collective-permute-done((bf16[128,2048]{1,0:T(8,128)(2,1)}, bf16[128,2048]{1,0:T(8,128)(2,1)}, u32[]{:S(2)}, u32[]{:S(2)}) %collective-permute-start.1) | collective-permute-done | bytes 524320 | tf_op jit(solution)/shard_map/ppermute | solution.py:482
  97.0 1.0 collective-permute-start.5
  98.4 0.8 collective-permute-start.4
  99.9 1.1 collective-permute-done.4.refs_5_
  101.0 9.1 %shard_map.168 = (f32[128,2048]{1,0:T(8,128)}, f32[128,128]{1,0:T(8,128)}, bf16[128,2304]{1,0:T(8,128)(2,1)}, bf16[128,2304]{1,0:T(8,128)(2,1)}, bf16[128,2304]{1,0:T(8,128)(2,1)}) custom-call(s32[12]{0:T(128)} %pad_add_fusion.1.place_ref, bf16[8,528,128]{2,1,0:T(8,128)(2,1)} %copy-done.2, bf16[128,2048]{1,0:T(8,128)(2,1)} %refs_0_.1, ...), custom_call_target="tpu_custom_call" | custom-call | tf_op jit(solution)/shard_map/pallas_call | solution.py:257
  110.2 1.3 copy-done.1
  111.5 8.8 %all-to-all-start.4 = ((bf16[128,8,1536]{2,1,0:T(8,128)(2,1)}), bf16[128,8,1536]{2,1,0:T(8,128)(2,1)S(1)}, u32[]{:S(2)}, u32[]{:S(2)}) async-start(bf16[128,8,1536]{2,1,0:T(8,128)(2,1)} %bitcast.26), calls=%async_computation.4 | async-start | bytes 6291456 | tf_op jit(solution)/shard_map/all_to_all | solution.py:486
  120.3 3.3 %collective-permute-start.7 = (bf16[128,2304]{1,0:T(8,128)(2,1)}, bf16[128,2304]{1,0:T(8,128)(2,1)S(1)}, u32[]{:S(2)}, u32[]{:S(2)}) collective-permute-start(bf16[128,2304]{1,0:T(8,128)(2,1)} %get-tuple-element.26), channel_id=1, source_target_pairs={{0,6},{2,0},{4,2},{6,4},{1,7},{3,1},{5,3},{7,5},{8,14},{10,8},{12,... | collective-permute-start | bytes 1769480 | tf_op jit(solution)/shard_map/ppermute | solution.py:482
  123.6 1.5 collective-permute-start.9
  125.7 43.2 %collective-permute-done.7.got_a = bf16[128,2304]{1,0:T(8,128)(2,1)S(1)} collective-permute-done((bf16[128,2304]{1,0:T(8,128)(2,1)}, bf16[128,2304]{1,0:T(8,128)(2,1)S(1)}, u32[]{:S(2)}, u32[]{:S(2)}) %collective-permute-start.7) | collective-permute-done | bytes 589856 | tf_op jit(solution)/shard_map/ppermute | solution.py:482
  168.9 14.8 %collective-permute-done.8.got_b = bf16[128,2304]{1,0:T(8,128)(2,1)S(1)} collective-permute-done((bf16[128,2304]{1,0:T(8,128)(2,1)}, bf16[128,2304]{1,0:T(8,128)(2,1)S(1)}, u32[]{:S(2)}, u32[]{:S(2)}) %collective-permute-start.8) | collective-permute-done | bytes 589856 | tf_op jit(solution)/shard_map/ppermute | solution.py:482
  183.7 0.8 copy-done.5
  184.7 7.0 %shard_map.169 = (bf16[128,2048]{1,0:T(8,128)(2,1)}, bf16[1024,2560]{1,0:T(8,128)(2,1)}) custom-call(f32[128,2048]{1,0:T(8,128)} %get-tuple-element.24.mine_ref, f32[128,128]{1,0:T(8,128)} %get-tuple-element.25.ss_ref, bf16[128,2304]{1,0:T(8,128)(2,1)} %copy-done.4, bf16[128,2304]{1,0:T(8,128)(2,1)} %copy-done.5, bf16[128,2304]{1,0:T(8,128)(2,1)} %copy-done.6, ...), custom_call_target="tpu_custom_call" | custom-call | tf_op jit(solution)/shard_map/pallas_call | solution.py:307
  191.7 1.6 copy-done
  193.4 7.8 %all-to-all-start.2 = ((bf16[128,8,2560]{2,1,0:T(8,128)(2,1)}), bf16[128,8,2560]{2,1,0:T(8,128)(2,1)}, u32[]{:S(2)}, u32[]{:S(2)}) async-start(bf16[128,8,2560]{2,1,0:T(8,128)(2,1)} %bitcast.23), calls=%async_computation.2 | async-start | bytes 10485760 | tf_op jit(solution)/shard_map/all_to_all | solution.py:486
  201.2 10.7 %shard_map.170 = (f32[1280,768]{1,0:T(8,128)}, bf16[256,2048]{1,0:T(8,128)(2,1)}) custom-call(bf16[1024,1024]{1,0:T(8,128)(2,1)} %bitcast.21, bf16[1024,1536]{1,0:T(8,128)(2,1)} %bitcast.18, bf16[1024,1536]{1,0:T(8,128)(2,1)} %bitcast.19, bf16[768,2048]{1,0:T(8,128)(2,1)} %bitcast.27), custom_call_target="tpu_custom_call" | custom-call | tf_op jit(solution)/shard_map/pallas_call | solution.py:360
  211.9 53.1 %all-to-all-done.2 = bf16[128,8,2560]{2,1,0:T(8,128)(2,1)} async-done(((bf16[128,8,2560]{2,1,0:T(8,128)(2,1)}), bf16[128,8,2560]{2,1,0:T(8,128)(2,1)}, u32[]{:S(2)}, u32[]{:S(2)}) %all-to-all-start.2) | async-done | bytes 5242912 | tf_op jit(solution)/shard_map/all_to_all | solution.py:486
  265.0 31.8 %shard_map.171 = (bf16[2048,768]{1,0:T(8,128)(2,1)}, bf16[2048,768]{1,0:T(8,128)(2,1)}, bf16[768,2048]{1,0:T(8,128)(2,1)}) custom-call(bf16[1024,2560]{1,0:T(8,128)(2,1)} %bitcast.7.x_ref.tail_ref, bf16[1024,2560]{1,0:T(8,128)(2,1)} %bitcast.7.x_ref.tail_ref, f32[1280,768]{1,0:T(8,128)} %get-tuple-element.35.back_ref, bf16[2048,768]{1,0:T(8,128)(2,1)} %bitcast.24, ...), custom_call_target="tpu_custom_call" | custom-call | tf_op jit(solution)/shard_map/pallas_call | solution.py:448
  (29 shorter events, 2.7 us)
Async XLA Ops:
  4.5 10.6 %all-to-all-start = ((bf16[4,128,256]{2,1,0:T(8,128)(2,1)}), bf16[4,128,256]{2,1,0:T(8,128)(2,1)S(1)}, u32[]{:S(2)}, u32[]{:S(2)}) async-start(bf16[4,128,256]{2,1,0:T(8,128)(2,1)} %shard_map.166), calls=%async_computation | async-start | bytes 524288 | tf_op jit(solution)/shard_map/all_to_all | solution.py:486
  15.1 0.7 copy-start.3
  21.7 77.5 %copy-start.8 = (s32[4]{0:T(128)S(1)}, s32[4]{0:T(128)}, u32[]{:S(2)}) copy-start(s32[4]{0:T(128)} %constant.41.clone) | copy-start | bytes 52
  21.7 21.8 %all-to-all-start.1 = ((bf16[8,528,128]{2,1,0:T(8,128)(2,1)}), bf16[8,528,128]{2,1,0:T(8,128)(2,1)S(1)}, u32[]{:S(2)}, u32[]{:S(2)}) async-start(bf16[8,528,128]{2,1,0:T(8,128)(2,1)} %shard_map.167), calls=%async_computation.1 | async-start | bytes 2162688 | tf_op jit(solution)/shard_map/all_to_all | solution.py:486
  43.5 57.6 %copy-start.2 = (bf16[8,528,128]{2,1,0:T(8,128)(2,1)}, bf16[8,528,128]{2,1,0:T(8,128)(2,1)S(1)}, u32[]{:S(2)}) copy-start(bf16[8,528,128]{2,1,0:T(8,128)(2,1)S(1)} %all-to-all-done.1.x_ref) | copy-start | bytes 3244036
  43.5 66.7 %all-to-all-start.3 = ((bf16[128,8,1024]{2,1,0:T(8,128)(2,1)}), bf16[128,8,1024]{2,1,0:T(8,128)(2,1)S(1)}, u32[]{:S(2)}, u32[]{:S(2)}) async-start(bf16[128,8,1024]{2,1,0:T(8,128)(2,1)} %bitcast.28), calls=%async_computation.3 | async-start | bytes 4194304 | tf_op jit(solution)/shard_map/all_to_all | solution.py:486
  50.6 36.7 %collective-permute-start.2 = (bf16[128,2048]{1,0:T(8,128)(2,1)}, bf16[128,2048]{1,0:T(8,128)(2,1)}, u32[]{:S(2)}, u32[]{:S(2)}) collective-permute-start(bf16[128,2048]{1,0:T(8,128)(2,1)} %refs_0_.1), channel_id=1, source_target_pairs={{0,16},{8,24},{16,0},{24,8},{1,17},{9,25},{17,1},{25,9},{2,18},{10... | collective-permute-start | bytes 1572872 | tf_op jit(solution)/shard_map/ppermute | solution.py:482
  53.5 43.5 %collective-permute-start.1 = (bf16[128,2048]{1,0:T(8,128)(2,1)}, bf16[128,2048]{1,0:T(8,128)(2,1)}, u32[]{:S(2)}, u32[]{:S(2)}) collective-permute-start(bf16[128,2048]{1,0:T(8,128)(2,1)} %refs_0_.1), channel_id=1, source_target_pairs={{0,24},{8,0},{16,8},{24,16},{1,25},{9,1},{17,9},{25,17},{2,26},{10... | collective-permute-start | bytes 1572872 | tf_op jit(solution)/shard_map/ppermute | solution.py:482
  54.4 44.0 %collective-permute-start = (bf16[128,2048]{1,0:T(8,128)(2,1)}, bf16[128,2048]{1,0:T(8,128)(2,1)}, u32[]{:S(2)}, u32[]{:S(2)}) collective-permute-start(bf16[128,2048]{1,0:T(8,128)(2,1)} %refs_0_.1), channel_id=1, source_target_pairs={{0,8},{8,16},{16,24},{24,0},{1,9},{9,17},{17,25},{25,1},{2,10},{10... | collective-permute-start | bytes 1572872 | tf_op jit(solution)/shard_map/ppermute | solution.py:482
  55.0 44.9 %collective-permute-start.3 = (bf16[128,2048]{1,0:T(8,128)(2,1)}, bf16[128,2048]{1,0:T(8,128)(2,1)}, u32[]{:S(2)}, u32[]{:S(2)}) collective-permute-start(bf16[128,2048]{1,0:T(8,128)(2,1)} %refs_0_.1), channel_id=1, source_target_pairs={{0,1},{1,0},{2,3},{3,2},{4,5},{5,4},{6,7},{7,6},{8,9},{9,8},{10,11... | collective-permute-start | bytes 1572872 | tf_op jit(solution)/shard_map/ppermute | solution.py:482
  87.2 12.7 %collective-permute-start.6 = (bf16[128,2048]{1,0:T(8,128)(2,1)}, bf16[128,2048]{1,0:T(8,128)(2,1)}, u32[]{:S(2)}, u32[]{:S(2)}) collective-permute-start(bf16[128,2048]{1,0:T(8,128)(2,1)} %collective-permute-done.2.refs_3_), channel_id=1, source_target_pairs={{0,1},{1,0},{2,3},{3,2},{4,5},{5,4},{6,7},{7,6},{8,9},{9,8},{10,11... | collective-permute-start | bytes 1572872 | tf_op jit(solution)/shard_map/ppermute | solution.py:482
  97.0 3.0 collective-permute-start.5
  98.4 2.7 collective-permute-start.4
  110.1 1.3 copy-start.1
  110.2 14.9 %copy-start.7 = (bf16[2048]{0:T(1024)(128)(2,1)S(1)}, bf16[2048]{0:T(1024)(128)(2,1)}, u32[]{:S(2)}) copy-start(bf16[2048]{0:T(1024)(128)(2,1)} %param.20) | copy-start | bytes 12292
  111.5 80.3 %all-to-all-start.4 = ((bf16[128,8,1536]{2,1,0:T(8,128)(2,1)}), bf16[128,8,1536]{2,1,0:T(8,128)(2,1)S(1)}, u32[]{:S(2)}, u32[]{:S(2)}) async-start(bf16[128,8,1536]{2,1,0:T(8,128)(2,1)} %bitcast.26), calls=%async_computation.4 | async-start | bytes 6291456 | tf_op jit(solution)/shard_map/all_to_all | solution.py:486
  120.3 48.6 %collective-permute-start.7 = (bf16[128,2304]{1,0:T(8,128)(2,1)}, bf16[128,2304]{1,0:T(8,128)(2,1)S(1)}, u32[]{:S(2)}, u32[]{:S(2)}) collective-permute-start(bf16[128,2304]{1,0:T(8,128)(2,1)} %get-tuple-element.26), channel_id=1, source_target_pairs={{0,6},{2,0},{4,2},{6,4},{1,7},{3,1},{5,3},{7,5},{8,14},{10,8},{12,... | collective-permute-start | bytes 1769480 | tf_op jit(solution)/shard_map/ppermute | solution.py:482
  123.6 60.1 %collective-permute-start.8 = (bf16[128,2304]{1,0:T(8,128)(2,1)}, bf16[128,2304]{1,0:T(8,128)(2,1)S(1)}, u32[]{:S(2)}, u32[]{:S(2)}) collective-permute-start(bf16[128,2304]{1,0:T(8,128)(2,1)} %get-tuple-element.27), channel_id=1, source_target_pairs={{0,2},{2,4},{4,6},{6,0},{1,3},{3,5},{5,7},{7,1},{8,10},{10,12},{12... | collective-permute-start | bytes 1769480 | tf_op jit(solution)/shard_map/ppermute | solution.py:482
  123.6 60.1 %collective-permute-start.9 = (bf16[128,2304]{1,0:T(8,128)(2,1)}, bf16[128,2304]{1,0:T(8,128)(2,1)S(1)}, u32[]{:S(2)}, u32[]{:S(2)}) collective-permute-start(bf16[128,2304]{1,0:T(8,128)(2,1)} %get-tuple-element.28), channel_id=1, source_target_pairs={{0,4},{2,6},{4,0},{6,2},{1,5},{3,7},{5,1},{7,3},{8,12},{10,14},{12... | collective-permute-start | bytes 1769480 | tf_op jit(solution)/shard_map/ppermute | solution.py:482
  168.9 14.8 %copy-start.4 = (bf16[128,2304]{1,0:T(8,128)(2,1)}, bf16[128,2304]{1,0:T(8,128)(2,1)S(1)}, u32[]{:S(2)}) copy-start(bf16[128,2304]{1,0:T(8,128)(2,1)S(1)} %collective-permute-done.7.got_a) | copy-start | bytes 1769476
  183.7 0.8 copy-start.5
  183.7 1.0 copy-start.6
  191.7 1.6 copy-start
  193.4 71.6 %all-to-all-start.2 = ((bf16[128,8,2560]{2,1,0:T(8,128)(2,1)}), bf16[128,8,2560]{2,1,0:T(8,128)(2,1)}, u32[]{:S(2)}, u32[]{:S(2)}) async-start(bf16[128,8,2560]{2,1,0:T(8,128)(2,1)} %bitcast.23), calls=%async_computation.2 | async-start | bytes 10485760 | tf_op jit(solution)/shard_map/all_to_all | solution.py:486

commit v7 on v5

--- a/solution.py
+++ b/solution.py
@@ -30,8 +30,8 @@
     return lax.dot_general(a, b, (((ca,), (cb,)), ((), ())), preferred_element_type=F32)
 
 
-def params(**kw):
-    return pltpu.CompilerParams(vmem_limit_bytes=56 * 1024 * 1024, **kw)
+def params(limit=28):
+    return pltpu.CompilerParams(vmem_limit_bytes=limit * 1024 * 1024)
 
 
 def state_kernel(k_ref, v_ref, o_ref, acc):
@@ -422,6 +422,10 @@
         grad_down_ref[...] = down.astype(BF)
 
 
+def held(array):
+    return pltpu.with_memory_space_constraint(array, pltpu.VMEM)
+
+
 def expert_grads(moe, cot, scaled_tail, back, gate, up):
     main = moe.shape[0]
     width, units = gate.shape
@@ -438,8 +442,8 @@
             pl.BlockSpec((ROWS, width), at_rows),
             pl.BlockSpec((main, width // QUART), lambda i: (0, QUART)),
             pl.BlockSpec((ROWS, units), lambda i: (jnp.minimum(i, blocks - 1), 0)),
-            whole(gate),
-            whole(up),
+            pl.BlockSpec(memory_space=pltpu.VMEM),
+            pl.BlockSpec(memory_space=pltpu.VMEM),
             pl.BlockSpec((main, block), at_cols),
             pl.BlockSpec((total - main, block), at_cols),
         ],
@@ -458,8 +462,8 @@
             pltpu.VMEM((units, total), BF),
             pltpu.VMEM((total, 2 * units), BF),
         ],
-        compiler_params=params(),
-    )(moe, moe, back, gate, up, cot, scaled_tail)
+        compiler_params=params(44),
+    )(moe, moe, back, held(gate), held(up), cot, scaled_tail)
 
 
 def shift(array, axis, by):
@@ -476,6 +480,7 @@
     routes, route_weights, cotangent, w_gate, w_up, w_down,
 ):
     n_ctx = lax.axis_size("ctx")
+    width = residual.shape[1]
     at = lax.axis_index("ctx").astype(jnp.int32).reshape(1)
     n_x, n_z = lax.axis_size("x"), lax.axis_size("z")
     n_core = lax.axis_size("core")
@@ -486,7 +491,10 @@
     sources = at_x[None, :] * n_core + jnp.stack([core, 1 - core])[:, None]
     place = jnp.concatenate([at_z, sources.reshape(-1)]).astype(jnp.int32)
 
-    pieces = [out_weight] + [shift(out_weight, "x", -d) for d in NEAR[1:]]
+    half = width // 2
+    left, right = shift(out_weight, "x", 1), shift(out_weight, "x", -1)
+    far = [shift(left[:, :half], "x", 1), shift(right[:, half:], "x", -1)]
+    pieces = [out_weight, left, right, jnp.concatenate(far, axis=1)]
     pieces += [shift(piece, "core", 1) for piece in pieces]
     states = span_states(key_heads, value_heads, n_ctx)
     states = exchange(states, "ctx")

time: 287 us -> 283 us (0.986)
  Pallas kernels: 73.3 us -> 57.1 us
  local copies, waits for them, and re-layouts: 3.32 us -> 18.7 us
  waiting for transfers between devices: 167 us -> 162 us
    unnamed x26 -> x41, local copies, waits for them, and re-layouts: 2.63 us -> 16.9 us
    pallas_call x1, Pallas kernels: 7.02 us -> 3.7 us  [norm_pack(): pl.pallas_call(norm_pack_kernel, grid=(BLOCKS,), in_specs=[whole(a) for a...]
    ppermute x10 -> x11, waiting for transfers between devices: 98.8 us -> 96.8 us  [shift(): lax.ppermute(array, axis, [(i, (i + by) % size) for i in range(size)])]
    ppermute x10 -> x11, starting transfers between devices: 13.5 us -> 14.1 us  [shift(): lax.ppermute(array, axis, [(i, (i + by) % size) for i in range(size)])]
  transfers between devices with their start and end apart: 14 -> 15, of which waited for: 9 -> 8; matrix products, arithmetic and copies ran while one was open for 1% -> 1% of each run, Pallas kernels for 11% -> 8%
where the time goes in v7:
time: 283 us; the launch traced here: 282 us
  waiting for transfers between devices  162 us (57%)
  Pallas kernels  57.1 us (20%)
  starting transfers between devices  43.1 us (15%)
  local copies, waits for them, and re-layouts  18.7 us (7%)
    ppermute x11, waiting for transfers between devices, shift(): lax.ppermute(array, axis, [(i, (i + by) % size) for i in range(size)])  96.8 us
    all_to_all x4, waiting for transfers between devices, exchange(): return lax.all_to_all(array, axes, split_axis=0, concat_axis=0, tiled=True)  65.7 us
    all_to_all x4, starting transfers between devices, exchange(): return lax.all_to_all(array, axes, split_axis=0, concat_axis=0, tiled=True)  29 us
    pallas_call x1, Pallas kernels, expert_grads(): pl.pallas_call(grads_kernel, grid=(blocks + width // block,), in_specs=[p...  28.6 us
    unnamed x41, local copies, waits for them, and re-layouts  16.9 us
    ppermute x11, starting transfers between devices, shift(): lax.ppermute(array, axis, [(i, (i + by) % size) for i in range(size)])  14.1 us
    pallas_call x1, Pallas kernels, hidden_grad(): pl.pallas_call(hidden_kernel, grid=(blocks + 1,), in_specs=[pl.BlockSpec(...  8.27 us
    pallas_call x1, Pallas kernels, project(): pl.pallas_call(project_kernel, grid_spec=pltpu.PrefetchScalarGridSpec(num...  6.71 us
  transfers between devices with their start and end apart: 15, of which 8 were waited for; matrix products, arithmetic and copies ran while one was open for 1% of the time, Pallas kernels for 8%

profile of v7, /device:TPU:1, one launch (start us, length us, event | category | flops | bytes accessed | tf_op | source)
XLA Modules:
  0.0 282.4 jit_solution(11286855523950939)
XLA Ops:
  3.1 2.1 shard_map.166
  5.2 5.0 %all-to-all-start = ((bf16[4,128,256]{2,1,0:T(8,128)(2,1)}), bf16[4,128,256]{2,1,0:T(8,128)(2,1)S(1)}, u32[]{:S(2)}, u32[]{:S(2)}) async-start(bf16[4,128,256]{2,1,0:T(8,128)(2,1)} %shard_map.166), calls=%async_computation | async-start | bytes 524288 | tf_op jit(solution)/shard_map/all_to_all | solution.py:475
  10.2 5.6 %all-to-all-done.s_ref = bf16[4,128,256]{2,1,0:T(8,128)(2,1)S(1)} async-done(((bf16[4,128,256]{2,1,0:T(8,128)(2,1)}), bf16[4,128,256]{2,1,0:T(8,128)(2,1)S(1)}, u32[]{:S(2)}, u32[]{:S(2)}) %all-to-all-start) | async-done | bytes 262176 | tf_op jit(solution)/shard_map/all_to_all | solution.py:475
  15.8 1.2 copy-done.10
  17.7 4.2 %shard_map.167 = bf16[8,528,128]{2,1,0:T(8,128)(2,1)} custom-call(s32[1]{0:T(128)} %bitcast.4.at_ref, bf16[4096,128]{1,0:T(8,128)(2,1)S(1)} %copy-done.10, bf16[4096,128]{1,0:T(8,128)(2,1)S(1)} %copy-done.3, bf16[4096,128]{1,0:T(8,128)(2,1)S(1)} %copy-done.5, bf16[4,128,256]{2,1,0:T(8,128)(2,1)S(1)} %all-to-all-done.s_ref, bf16[1,128]{1,0:T(2,128)(2,1)S(1)} %bitcast.24), custom_call_target="tpu_custom_call" | custom-call | tf_op jit(solution)/shard_map/pallas_call | solution.py:107
  21.8 6.4 %all-to-all-start.1 = ((bf16[8,528,128]{2,1,0:T(8,128)(2,1)}), bf16[8,528,128]{2,1,0:T(8,128)(2,1)S(1)}, u32[]{:S(2)}, u32[]{:S(2)}) async-start(bf16[8,528,128]{2,1,0:T(8,128)(2,1)} %shard_map.167), calls=%async_computation.1 | async-start | bytes 2162688 | tf_op jit(solution)/shard_map/all_to_all | solution.py:475
  28.2 3.6 %shard_map.165 = bf16[1024,2560]{1,0:T(8,128)(2,1)S(1)} custom-call(s32[8,128]{1,0:T(8,128)S(1)} %bitcast.21, f32[8,128]{1,0:T(8,128)S(1)} %bitcast.23, bf16[128,2048]{1,0:T(8,128)(2,1)S(1)} %copy-done.14), custom_call_target="tpu_custom_call" | custom-call | tf_op jit(solution)/shard_map/pallas_call | solution.py:207
  31.8 2.4 copy-done
  34.2 9.3 %all-to-all-done.1.x_ref = bf16[8,528,128]{2,1,0:T(8,128)(2,1)S(1)} async-done(((bf16[8,528,128]{2,1,0:T(8,128)(2,1)}), bf16[8,528,128]{2,1,0:T(8,128)(2,1)S(1)}, u32[]{:S(2)}, u32[]{:S(2)}) %all-to-all-start.1) | async-done | bytes 1081376 | tf_op jit(solution)/shard_map/all_to_all | solution.py:475
  43.5 7.5 %all-to-all-start.3 = ((bf16[128,8,2560]{2,1,0:T(8,128)(2,1)}), bf16[128,8,2560]{2,1,0:T(8,128)(2,1)}, u32[]{:S(2)}, u32[]{:S(2)}) async-start(bf16[128,8,2560]{2,1,0:T(8,128)(2,1)} %bitcast.16), calls=%async_computation.3 | async-start | bytes 10485760 | tf_op jit(solution)/shard_map/all_to_all | solution.py:475
  51.0 1.4 collective-permute-start
  52.5 1.3 collective-permute-start.1
  53.8 67.0 %collective-permute-done.refs_1_ = bf16[128,2048]{1,0:T(8,128)(2,1)S(1)} collective-permute-done((bf16[128,2048]{1,0:T(8,128)(2,1)}, bf16[128,2048]{1,0:T(8,128)(2,1)S(1)}, u32[]{:S(2)}, u32[]{:S(2)}) %collective-permute-start) | collective-permute-done | bytes 524320 | tf_op jit(solution)/shard_map/ppermute | solution.py:471
  121.6 2.7 collective-permute-start.3
  124.3 1.4 collective-permute-start.4
  126.3 2.9 %collective-permute-done.2 = bf16[128,1024]{1,0:T(8,128)(2,1)S(1)} collective-permute-done((bf16[128,1024]{1,0:T(8,128)(2,1)S(1)}, bf16[128,1024]{1,0:T(8,128)(2,1)S(1)}, u32[]{:S(2)}, u32[]{:S(2)}) %collective-permute-start.2) | collective-permute-done | bytes 262176 | tf_op jit(solution)/shard_map/ppermute | solution.py:471
  130.2 2.0 collective-permute-start.7
  132.4 1.4 collective-permute-done.7.refs_7_
  133.8 6.7 %shard_map.168 = (f32[128,2048]{1,0:T(8,128)S(1)}, f32[128,128]{1,0:T(8,128)S(1)}, bf16[128,2304]{1,0:T(8,128)(2,1)S(1)}, bf16[128,2304]{1,0:T(8,128)(2,1)S(1)}, bf16[128,2304]{1,0:T(8,128)(2,1)S(1)}) custom-call(s32[12]{0:T(128)S(1)} %pad_add_fusion.1.place_ref, bf16[8,528,128]{2,1,0:T(8,128)(2,1)S(1)} %all-to-all-done.1.x_ref, bf16[128,2048]{1,0:T(8,128)(2,1)} %refs_0_.1, ...), custom_call_target="tpu_custom_call" | custom-call | tf_op jit(solution)/shard_map/pallas_call | solution.py:255
  140.6 3.2 %collective-permute-start.8 = (bf16[128,2304]{1,0:T(8,128)(2,1)S(1)}, bf16[128,2304]{1,0:T(8,128)(2,1)S(1)}, u32[]{:S(2)}, u32[]{:S(2)}) collective-permute-start(bf16[128,2304]{1,0:T(8,128)(2,1)S(1)} %get-tuple-element.21), channel_id=1, source_target_pairs={{0,6},{2,0},{4,2},{6,4},{1,7},{3,1},{5,3},{7,5},{8,14},{10,8},{12,... | collective-permute-start | bytes 1769480 | tf_op jit(solution)/shard_map/ppermute | solution.py:471
  143.8 1.5 collective-permute-start.10
  145.3 23.3 %collective-permute-done.8.got_a = bf16[128,2304]{1,0:T(8,128)(2,1)S(1)} collective-permute-done((bf16[128,2304]{1,0:T(8,128)(2,1)S(1)}, bf16[128,2304]{1,0:T(8,128)(2,1)S(1)}, u32[]{:S(2)}, u32[]{:S(2)}) %collective-permute-start.8) | collective-permute-done | bytes 589856 | tf_op jit(solution)/shard_map/ppermute | solution.py:471
  168.6 2.1 collective-permute-done.10.got_c
  170.7 3.7 %shard_map.169 = (bf16[128,2048]{1,0:T(8,128)(2,1)}, bf16[1024,2560]{1,0:T(8,128)(2,1)S(1)}) custom-call(f32[128,2048]{1,0:T(8,128)S(1)} %get-tuple-element.19.mine_ref, f32[128,128]{1,0:T(8,128)S(1)} %get-tuple-element.20.ss_ref, bf16[128,2304]{1,0:T(8,128)(2,1)S(1)} %collective-permute-done.8.got_a, bf16[128,2304]{1,0:T(8,128)(2,1)S(1)} %collective-permute-done.9.got_b, ...), custom_call_target="tpu_custom_call" | custom-call | tf_op jit(solution)/shard_map/pallas_call | solution.py:305
  174.4 2.3 copy-done.1
  176.7 10.2 %all-to-all-start.2 = ((bf16[128,8,2560]{2,1,0:T(8,128)(2,1)}), bf16[128,8,2560]{2,1,0:T(8,128)(2,1)}, u32[]{:S(2)}, u32[]{:S(2)}) async-start(bf16[128,8,2560]{2,1,0:T(8,128)(2,1)} %bitcast.17), calls=%async_computation.2 | async-start | bytes 10485760 | tf_op jit(solution)/shard_map/all_to_all | solution.py:475
  186.9 1.9 copy-done.9
  188.8 8.3 %shard_map.170 = (f32[1280,768]{1,0:T(8,128)S(1)}, bf16[256,2048]{1,0:T(8,128)(2,1)S(1)}) custom-call(bf16[1024,2560]{1,0:T(8,128)(2,1)} %bitcast.9.rows_ref.tail_ref.scaled_ref, bf16[1024,2560]{1,0:T(8,128)(2,1)} %bitcast.9.rows_ref.tail_ref.scaled_ref, bf16[768,2048]{1,0:T(8,128)(2,1)S(1)} %bitcast.20), custom_call_target="tpu_custom_call" | custom-call | tf_op jit(solution)/shard_map/pallas_call | solution.py:355
  197.0 1.9 copy-done.6
  199.9 50.8 %all-to-all-done.2 = bf16[128,8,2560]{2,1,0:T(8,128)(2,1)} async-done(((bf16[128,8,2560]{2,1,0:T(8,128)(2,1)}), bf16[128,8,2560]{2,1,0:T(8,128)(2,1)}, u32[]{:S(2)}, u32[]{:S(2)}) %all-to-all-start.2) | async-done | bytes 5242912 | tf_op jit(solution)/shard_map/all_to_all | solution.py:475
  250.7 1.9 copy-done.8
  253.8 28.6 %shard_map.171 = (bf16[2048,768]{1,0:T(8,128)(2,1)}, bf16[2048,768]{1,0:T(8,128)(2,1)}, bf16[768,2048]{1,0:T(8,128)(2,1)}) custom-call(bf16[1024,2560]{1,0:T(8,128)(2,1)} %bitcast.7.x_ref.tail_ref, bf16[1024,2560]{1,0:T(8,128)(2,1)} %bitcast.7.x_ref.tail_ref, f32[1280,768]{1,0:T(8,128)} %copy-done.6, bf16[2048,768]{1,0:T(8,128)(2,1)S(1)} %bitcast.18, ...), custom_call_target="tpu_custom_call" | custom-call | tf_op jit(solution)/shard_map/pallas_call | solution.py:438
  (55 shorter events, 8.0 us)
Async XLA Ops:
  0.6 1.2 copy-start.2
  1.9 1.2 copy-start.4
  3.1 12.7 %copy-start.3 = (bf16[4096,128]{1,0:T(8,128)(2,1)S(1)}, bf16[4096,128]{1,0:T(8,128)(2,1)}, u32[]{:S(2)}) copy-start(bf16[4096,128]{1,0:T(8,128)(2,1)} %k_ref.3) | copy-start | bytes 3145732
  3.1 12.7 %copy-start.5 = (bf16[4096,128]{1,0:T(8,128)(2,1)S(1)}, bf16[4096,128]{1,0:T(8,128)(2,1)}, u32[]{:S(2)}) copy-start(bf16[4096,128]{1,0:T(8,128)(2,1)} %v_ref.3) | copy-start | bytes 3145732
  5.2 10.6 %all-to-all-start = ((bf16[4,128,256]{2,1,0:T(8,128)(2,1)}), bf16[4,128,256]{2,1,0:T(8,128)(2,1)S(1)}, u32[]{:S(2)}, u32[]{:S(2)}) async-start(bf16[4,128,256]{2,1,0:T(8,128)(2,1)} %shard_map.166), calls=%async_computation | async-start | bytes 524288 | tf_op jit(solution)/shard_map/all_to_all | solution.py:475
  15.8 1.2 copy-start.10
  17.7 10.6 %copy-start.14 = (bf16[128,2048]{1,0:T(8,128)(2,1)S(1)}, bf16[128,2048]{1,0:T(8,128)(2,1)}, u32[]{:S(2)}) copy-start(bf16[128,2048]{1,0:T(8,128)(2,1)} %cot_ref.1) | copy-start | bytes 1572868
  17.7 10.6 %copy-start.15 = (s32[128,8]{0,1:T(8,128)S(1)}, s32[128,8]{0,1:T(8,128)}, u32[]{:S(2)}) copy-start(s32[128,8]{0,1:T(8,128)} %param.21) | copy-start | bytes 12292
  17.7 10.6 %copy-start.16 = (f32[128,8]{0,1:T(8,128)S(1)}, f32[128,8]{0,1:T(8,128)}, u32[]{:S(2)}) copy-start(f32[128,8]{0,1:T(8,128)} %param.22) | copy-start | bytes 12292
  21.8 21.7 %all-to-all-start.1 = ((bf16[8,528,128]{2,1,0:T(8,128)(2,1)}), bf16[8,528,128]{2,1,0:T(8,128)(2,1)S(1)}, u32[]{:S(2)}, u32[]{:S(2)}) async-start(bf16[8,528,128]{2,1,0:T(8,128)(2,1)} %shard_map.167), calls=%async_computation.1 | async-start | bytes 2162688 | tf_op jit(solution)/shard_map/all_to_all | solution.py:475
  31.8 2.4 copy-start
  43.5 88.6 %copy-start.19 = (s32[4]{0:T(128)S(1)}, s32[4]{0:T(128)}, u32[]{:S(2)}) copy-start(s32[4]{0:T(128)} %constant.41.clone) | copy-start | bytes 52
  43.5 133.2 %all-to-all-start.3 = ((bf16[128,8,2560]{2,1,0:T(8,128)(2,1)}), bf16[128,8,2560]{2,1,0:T(8,128)(2,1)}, u32[]{:S(2)}, u32[]{:S(2)}) async-start(bf16[128,8,2560]{2,1,0:T(8,128)(2,1)} %bitcast.16), calls=%async_computation.3 | async-start | bytes 10485760 | tf_op jit(solution)/shard_map/all_to_all | solution.py:475
  51.0 69.8 %collective-permute-start = (bf16[128,2048]{1,0:T(8,128)(2,1)}, bf16[128,2048]{1,0:T(8,128)(2,1)S(1)}, u32[]{:S(2)}, u32[]{:S(2)}) collective-permute-start(bf16[128,2048]{1,0:T(8,128)(2,1)} %refs_0_.1), channel_id=1, source_target_pairs={{0,8},{8,16},{16,24},{24,0},{1,9},{9,17},{17,25},{25,1},{2,10},{10... | collective-permute-start | bytes 1572872 | tf_op jit(solution)/shard_map/ppermute | solution.py:471
  52.5 68.4 %collective-permute-start.1 = (bf16[128,2048]{1,0:T(8,128)(2,1)}, bf16[128,2048]{1,0:T(8,128)(2,1)S(1)}, u32[]{:S(2)}, u32[]{:S(2)}) collective-permute-start(bf16[128,2048]{1,0:T(8,128)(2,1)} %refs_0_.1), channel_id=1, source_target_pairs={{0,24},{8,0},{16,8},{24,16},{1,25},{9,1},{17,9},{25,17},{2,26},{10... | collective-permute-start | bytes 1572872 | tf_op jit(solution)/shard_map/ppermute | solution.py:471
  120.8 8.4 %collective-permute-start.2 = (bf16[128,1024]{1,0:T(8,128)(2,1)S(1)}, bf16[128,1024]{1,0:T(8,128)(2,1)S(1)}, u32[]{:S(2)}, u32[]{:S(2)}) collective-permute-start(bf16[128,1024]{1,0:T(8,128)(2,1)S(1)} %slice.8), channel_id=1, source_target_pairs={{0,8},{8,16},{16,24},{24,0},{1,9},{9,17},{17,25},{25,1},{2,10},{10... | collective-permute-start | bytes 786440 | tf_op jit(solution)/shard_map/ppermute | solution.py:471
  121.6 7.6 %collective-permute-start.3 = (bf16[128,1024]{1,0:T(8,128)(2,1)}, bf16[128,1024]{1,0:T(8,128)(2,1)}, u32[]{:S(2)}, u32[]{:S(2)}) collective-permute-start(bf16[128,1024]{1,0:T(8,128)(2,1)} %slice.9), channel_id=1, source_target_pairs={{0,24},{8,0},{16,8},{24,16},{1,25},{9,1},{17,9},{25,17},{2,26},{10... | collective-permute-start | bytes 786440 | tf_op jit(solution)/shard_map/ppermute | solution.py:471
  124.3 8.1 %collective-permute-start.4 = (bf16[128,2048]{1,0:T(8,128)(2,1)}, bf16[128,2048]{1,0:T(8,128)(2,1)}, u32[]{:S(2)}, u32[]{:S(2)}) collective-permute-start(bf16[128,2048]{1,0:T(8,128)(2,1)} %refs_0_.1), channel_id=1, source_target_pairs={{0,1},{1,0},{2,3},{3,2},{4,5},{5,4},{6,7},{7,6},{8,9},{9,8},{10,11... | collective-permute-start | bytes 1572872 | tf_op jit(solution)/shard_map/ppermute | solution.py:471
  125.7 19.6 %copy-start.18 = (bf16[2048]{0:T(1024)(128)(2,1)S(1)}, bf16[2048]{0:T(1024)(128)(2,1)}, u32[]{:S(2)}) copy-start(bf16[2048]{0:T(1024)(128)(2,1)} %param.20) | copy-start | bytes 12292
  125.7 45.0 %copy-start.13 = (bf16[128,2048]{1,0:T(8,128)(2,1)S(1)}, bf16[128,2048]{1,0:T(8,128)(2,1)}, u32[]{:S(2)}) copy-start(bf16[128,2048]{1,0:T(8,128)(2,1)} %residual_ref.1) | copy-start | bytes 1572868
  125.7 6.7 %collective-permute-start.6 = (bf16[128,2048]{1,0:T(8,128)(2,1)S(1)}, bf16[128,2048]{1,0:T(8,128)(2,1)}, u32[]{:S(2)}, u32[]{:S(2)}) collective-permute-start(bf16[128,2048]{1,0:T(8,128)(2,1)S(1)} %collective-permute-done.1.refs_2_), channel_id=1, source_target_pairs={{0,1},{1,0},{2,3},{3,2},{4,5},{5,4},{6,7},{7,6},{8,9},{9,8},{10,11... | collective-permute-start | bytes 1572872 | tf_op jit(solution)/shard_map/ppermute | solution.py:471
  125.8 6.7 %collective-permute-start.5 = (bf16[128,2048]{1,0:T(8,128)(2,1)S(1)}, bf16[128,2048]{1,0:T(8,128)(2,1)}, u32[]{:S(2)}, u32[]{:S(2)}) collective-permute-start(bf16[128,2048]{1,0:T(8,128)(2,1)S(1)} %collective-permute-done.refs_1_), channel_id=1, source_target_pairs={{0,1},{1,0},{2,3},{3,2},{4,5},{5,4},{6,7},{7,6},{8,9},{9,8},{10,11... | collective-permute-start | bytes 1572872 | tf_op jit(solution)/shard_map/ppermute | solution.py:471
  130.2 3.7 %collective-permute-start.7 = (bf16[128,2048]{1,0:T(8,128)(2,1)S(1)}, bf16[128,2048]{1,0:T(8,128)(2,1)}, u32[]{:S(2)}, u32[]{:S(2)}) collective-permute-start(bf16[128,2048]{1,0:T(8,128)(2,1)S(1)} %constant_dynamic-update-slice_fusion.refs_3_), channel_id=1, source_target_pairs={{0,1},{1,0},{2,3},{3,2},{4,5},{5,4},{6,7},{7,6},{8,9},{9,8},{10,11... | collective-permute-start | bytes 1572872 | tf_op jit(solution)/shard_map/ppermute | solution.py:471
  140.6 28.0 %collective-permute-start.8 = (bf16[128,2304]{1,0:T(8,128)(2,1)S(1)}, bf16[128,2304]{1,0:T(8,128)(2,1)S(1)}, u32[]{:S(2)}, u32[]{:S(2)}) collective-permute-start(bf16[128,2304]{1,0:T(8,128)(2,1)S(1)} %get-tuple-element.21), channel_id=1, source_target_pairs={{0,6},{2,0},{4,2},{6,4},{1,7},{3,1},{5,3},{7,5},{8,14},{10,8},{12,... | collective-permute-start | bytes 1769480 | tf_op jit(solution)/shard_map/ppermute | solution.py:471
  143.8 24.8 %collective-permute-start.9 = (bf16[128,2304]{1,0:T(8,128)(2,1)S(1)}, bf16[128,2304]{1,0:T(8,128)(2,1)S(1)}, u32[]{:S(2)}, u32[]{:S(2)}) collective-permute-start(bf16[128,2304]{1,0:T(8,128)(2,1)S(1)} %get-tuple-element.22), channel_id=1, source_target_pairs={{0,2},{2,4},{4,6},{6,0},{1,3},{3,5},{5,7},{7,1},{8,10},{10,12},{12... | collective-permute-start | bytes 1769480 | tf_op jit(solution)/shard_map/ppermute | solution.py:471
  143.8 27.0 %collective-permute-start.10 = (bf16[128,2304]{1,0:T(8,128)(2,1)S(1)}, bf16[128,2304]{1,0:T(8,128)(2,1)S(1)}, u32[]{:S(2)}, u32[]{:S(2)}) collective-permute-start(bf16[128,2304]{1,0:T(8,128)(2,1)S(1)} %get-tuple-element.23), channel_id=1, source_target_pairs={{0,4},{2,6},{4,0},{6,2},{1,5},{3,7},{5,1},{7,3},{8,12},{10,14},{12... | collective-permute-start | bytes 1769480 | tf_op jit(solution)/shard_map/ppermute | solution.py:471
  174.4 2.3 copy-start.1
  176.7 74.0 %all-to-all-start.2 = ((bf16[128,8,2560]{2,1,0:T(8,128)(2,1)}), bf16[128,8,2560]{2,1,0:T(8,128)(2,1)}, u32[]{:S(2)}, u32[]{:S(2)}) async-start(bf16[128,8,2560]{2,1,0:T(8,128)(2,1)} %bitcast.17), calls=%async_computation.2 | async-start | bytes 10485760 | tf_op jit(solution)/shard_map/all_to_all | solution.py:475
  186.9 1.9 copy-start.9
  188.8 61.9 %copy-start.7 = (bf16[1,2048,768]{2,1,0:T(8,128)(2,1)S(1)}, bf16[1,2048,768]{2,1,0:T(8,128)(2,1)}, u32[]{:S(2)}) copy-start(bf16[1,2048,768]{2,1,0:T(8,128)(2,1)} %param.24) | copy-start | bytes 9437188
  197.0 1.9 copy-start.6
  250.7 1.9 copy-start.8
  (3 other events, 2.8 us)

commit v8 on v7

--- a/solution.py
+++ b/solution.py
@@ -61,7 +61,7 @@
         out_specs=pl.BlockSpec((n_ctx, HD, 2 * HD), lambda i: (0, 0, 0)),
         out_shape=jax.ShapeDtypeStruct((n_ctx, HD, 2 * HD), BF),
         scratch_shapes=[pltpu.VMEM((HD, 2 * HD), F32)],
-        compiler_params=params(),
+        compiler_params=params(56),
     )(keys, values)
 
 
@@ -194,7 +194,7 @@
     rows = EXPERTS * MAIN
     wide = width + width // QUART
     spec = pl.BlockSpec((rows // BLOCKS, wide), lambda i: (i, 0))
-    return spec, jax.ShapeDtypeStruct((rows, wide), BF)
+    return spec, pltpu.HBM((rows, wide), BF)
 
 
 def whole(array):
@@ -365,8 +365,8 @@
             pl.BlockSpec((tails, width), lambda i: (0, 0)),
         ],
         out_shape=[
-            jax.ShapeDtypeStruct((rows + tails, units), F32),
-            jax.ShapeDtypeStruct((tails, width), BF),
+            pltpu.HBM((rows + tails, units), F32),
+            pltpu.HBM((tails, width), BF),
         ],
         compiler_params=params(),
     )(cot, cot, down)
@@ -422,8 +422,8 @@
         grad_down_ref[...] = down.astype(BF)
 
 
-def held(array):
-    return pltpu.with_memory_space_constraint(array, pltpu.VMEM)
+def held(array, space=pltpu.VMEM):
+    return pltpu.with_memory_space_constraint(array, space)
 
 
 def expert_grads(moe, cot, scaled_tail, back, gate, up):
@@ -443,7 +443,7 @@
             pl.BlockSpec((main, width // QUART), lambda i: (0, QUART)),
             pl.BlockSpec((ROWS, units), lambda i: (jnp.minimum(i, blocks - 1), 0)),
             pl.BlockSpec(memory_space=pltpu.VMEM),
-            pl.BlockSpec(memory_space=pltpu.VMEM),
+            whole(up),
             pl.BlockSpec((main, block), at_cols),
             pl.BlockSpec((total - main, block), at_cols),
         ],
@@ -463,7 +463,7 @@
             pltpu.VMEM((total, 2 * units), BF),
         ],
         compiler_params=params(44),
-    )(moe, moe, back, held(gate), held(up), cot, scaled_tail)
+    )(moe, moe, held(back, pltpu.HBM), gate, up, cot, held(scaled_tail, pltpu.HBM))
 
 
 def shift(array, axis, by):
@@ -516,8 +516,9 @@
 
     moe = moe.reshape(EXPERTS * MAIN, -1)
     cot = cot.reshape(EXPERTS * MAIN, -1)
+    gate, up = held(w_gate[0]), held(w_up[0], pltpu.HBM)
     back, scaled_tail = hidden_grad(cot, w_down[0])
-    grads = expert_grads(moe, cot, scaled_tail, back, w_gate[0], w_up[0])
+    grads = expert_grads(moe, cot, scaled_tail, back, gate, up)
     return (hidden_out,) + tuple(g[None] for g in grads)
 
 

time: 283 us -> 280 us (0.989)
  local copies, waits for them, and re-layouts: 18.7 us -> 5.62 us
  Pallas kernels: 57.1 us -> 65 us
  waiting for transfers between devices: 162 us -> 165 us
    unnamed x41 -> x25, local copies, waits for them, and re-layouts: 16.9 us -> 3.82 us
  transfers between devices with their start and end apart: 15 -> 15, of which waited for: 8 -> 8; matrix products, arithmetic and copies ran while one was open for 1% -> 1% of each run, Pallas kernels for 8% -> 10%
where the time goes in v8:
time: 280 us; the launch traced here: 279 us
  waiting for transfers between devices  165 us (59%)
  Pallas kernels  65 us (23%)
  starting transfers between devices  43.1 us (15%)
  local copies, waits for them, and re-layouts  5.62 us (2%)
    ppermute x11, waiting for transfers between devices, shift(): lax.ppermute(array, axis, [(i, (i + by) % size) for i in range(size)])  96.8 us
    all_to_all x4, waiting for transfers between devices, exchange(): return lax.all_to_all(array, axes, split_axis=0, concat_axis=0, tiled=True)  67.9 us
    pallas_call x1, Pallas kernels, expert_grads(): pl.pallas_call(grads_kernel, grid=(blocks + width // block,), in_specs=[p...  30 us
    all_to_all x4, starting transfers between devices, exchange(): return lax.all_to_all(array, axes, split_axis=0, concat_axis=0, tiled=True)  29 us
    ppermute x11, starting transfers between devices, shift(): lax.ppermute(array, axis, [(i, (i + by) % size) for i in range(size)])  14.1 us
    pallas_call x1, Pallas kernels, hidden_grad(): pl.pallas_call(hidden_kernel, grid=(blocks + 1,), in_specs=[pl.BlockSpec(...  9.9 us
    pallas_call x1, Pallas kernels, project(): pl.pallas_call(project_kernel, grid_spec=pltpu.PrefetchScalarGridSpec(num...  6.74 us
  transfers between devices with their start and end apart: 15, of which 8 were waited for; matrix products, arithmetic and copies ran while one was open for 1% of the time, Pallas kernels for 10%

profile of v8, /device:TPU:1, one launch (start us, length us, event | category | flops | bytes accessed | tf_op | source)
XLA Modules:
  0.0 279.4 jit_solution(17667921437185821390)
XLA Ops:
  0.7 4.0 %shard_map.166 = bf16[4,128,256]{2,1,0:T(8,128)(2,1)} custom-call(bf16[4096,128]{1,0:T(8,128)(2,1)} %k_ref.3, bf16[4096,128]{1,0:T(8,128)(2,1)} %v_ref.3), custom_call_target="tpu_custom_call" | custom-call | tf_op jit(solution)/shard_map/pallas_call | solution.py:57
  4.7 5.0 %all-to-all-start = ((bf16[4,128,256]{2,1,0:T(8,128)(2,1)}), bf16[4,128,256]{2,1,0:T(8,128)(2,1)S(1)}, u32[]{:S(2)}, u32[]{:S(2)}) async-start(bf16[4,128,256]{2,1,0:T(8,128)(2,1)} %shard_map.166), calls=%async_computation | async-start | bytes 524288 | tf_op jit(solution)/shard_map/all_to_all | solution.py:475
  9.7 5.6 %all-to-all-done.s_ref = bf16[4,128,256]{2,1,0:T(8,128)(2,1)S(1)} async-done(((bf16[4,128,256]{2,1,0:T(8,128)(2,1)}), bf16[4,128,256]{2,1,0:T(8,128)(2,1)S(1)}, u32[]{:S(2)}, u32[]{:S(2)}) %all-to-all-start) | async-done | bytes 262176 | tf_op jit(solution)/shard_map/all_to_all | solution.py:475
  15.2 1.2 copy-done.4
  16.5 0.7 copy-done.9
  17.1 4.2 %shard_map.167 = bf16[8,528,128]{2,1,0:T(8,128)(2,1)} custom-call(s32[1]{0:T(128)} %bitcast.4.at_ref, bf16[4096,128]{1,0:T(8,128)(2,1)S(1)} %copy-done.4, bf16[4096,128]{1,0:T(8,128)(2,1)S(1)} %copy-done, bf16[4096,128]{1,0:T(8,128)(2,1)S(1)} %copy-done.1, bf16[4,128,256]{2,1,0:T(8,128)(2,1)S(1)} %all-to-all-done.s_ref, bf16[1,128]{1,0:T(2,128)(2,1)S(1)} %bitcast.21), custom_call_target="tpu_custom_call" | custom-call | tf_op jit(solution)/shard_map/pallas_call | solution.py:107
  21.3 6.4 %all-to-all-start.1 = ((bf16[8,528,128]{2,1,0:T(8,128)(2,1)}), bf16[8,528,128]{2,1,0:T(8,128)(2,1)S(1)}, u32[]{:S(2)}, u32[]{:S(2)}) async-start(bf16[8,528,128]{2,1,0:T(8,128)(2,1)} %shard_map.167), calls=%async_computation.1 | async-start | bytes 2162688 | tf_op jit(solution)/shard_map/all_to_all | solution.py:475
  27.7 5.0 %shard_map.165 = bf16[1024,2560]{1,0:T(8,128)(2,1)} custom-call(s32[8,128]{1,0:T(8,128)S(1)} %bitcast.18, f32[8,128]{1,0:T(8,128)S(1)} %bitcast.20, bf16[128,2048]{1,0:T(8,128)(2,1)S(1)} %copy-done.6), custom_call_target="tpu_custom_call" | custom-call | tf_op jit(solution)/shard_map/pallas_call | solution.py:207
  32.7 10.3 %all-to-all-done.1.x_ref = bf16[8,528,128]{2,1,0:T(8,128)(2,1)S(1)} async-done(((bf16[8,528,128]{2,1,0:T(8,128)(2,1)}), bf16[8,528,128]{2,1,0:T(8,128)(2,1)S(1)}, u32[]{:S(2)}, u32[]{:S(2)}) %all-to-all-start.1) | async-done | bytes 1081376 | tf_op jit(solution)/shard_map/all_to_all | solution.py:475
  43.0 7.5 %all-to-all-start.3 = ((bf16[128,8,2560]{2,1,0:T(8,128)(2,1)}), bf16[128,8,2560]{2,1,0:T(8,128)(2,1)}, u32[]{:S(2)}, u32[]{:S(2)}) async-start(bf16[128,8,2560]{2,1,0:T(8,128)(2,1)} %bitcast.22), calls=%async_computation.3 | async-start | bytes 10485760 | tf_op jit(solution)/shard_map/all_to_all | solution.py:475
  50.5 1.4 collective-permute-start
  51.9 1.3 collective-permute-start.1
  53.3 67.0 %collective-permute-done.refs_1_ = bf16[128,2048]{1,0:T(8,128)(2,1)S(1)} collective-permute-done((bf16[128,2048]{1,0:T(8,128)(2,1)}, bf16[128,2048]{1,0:T(8,128)(2,1)S(1)}, u32[]{:S(2)}, u32[]{:S(2)}) %collective-permute-start) | collective-permute-done | bytes 524320 | tf_op jit(solution)/shard_map/ppermute | solution.py:471
  120.4 0.7 slice.9
  121.1 2.7 collective-permute-start.3
  123.8 1.4 collective-permute-start.4
  125.3 0.5 collective-permute-start.5
  125.8 2.9 %collective-permute-done.2 = bf16[128,1024]{1,0:T(8,128)(2,1)S(1)} collective-permute-done((bf16[128,1024]{1,0:T(8,128)(2,1)S(1)}, bf16[128,1024]{1,0:T(8,128)(2,1)S(1)}, u32[]{:S(2)}, u32[]{:S(2)}) %collective-permute-start.2) | collective-permute-done | bytes 262176 | tf_op jit(solution)/shard_map/ppermute | solution.py:471
  128.7 1.0 constant_dynamic-update-slice_fusion.refs_3_
  129.7 2.0 collective-permute-start.7
  131.9 1.4 collective-permute-done.7.refs_7_
  133.3 6.7 %shard_map.168 = (f32[128,2048]{1,0:T(8,128)S(1)}, f32[128,128]{1,0:T(8,128)S(1)}, bf16[128,2304]{1,0:T(8,128)(2,1)S(1)}, bf16[128,2304]{1,0:T(8,128)(2,1)S(1)}, bf16[128,2304]{1,0:T(8,128)(2,1)S(1)}) custom-call(s32[12]{0:T(128)S(1)} %pad_add_fusion.1.place_ref, bf16[8,528,128]{2,1,0:T(8,128)(2,1)S(1)} %all-to-all-done.1.x_ref, bf16[128,2048]{1,0:T(8,128)(2,1)} %refs_0_.1, ...), custom_call_target="tpu_custom_call" | custom-call | tf_op jit(solution)/shard_map/pallas_call | solution.py:255
  140.1 3.2 %collective-permute-start.8 = (bf16[128,2304]{1,0:T(8,128)(2,1)S(1)}, bf16[128,2304]{1,0:T(8,128)(2,1)S(1)}, u32[]{:S(2)}, u32[]{:S(2)}) collective-permute-start(bf16[128,2304]{1,0:T(8,128)(2,1)S(1)} %get-tuple-element.21), channel_id=1, source_target_pairs={{0,6},{2,0},{4,2},{6,4},{1,7},{3,1},{5,3},{7,5},{8,14},{10,8},{12,... | collective-permute-start | bytes 1769480 | tf_op jit(solution)/shard_map/ppermute | solution.py:471
  143.3 1.5 collective-permute-start.10
  144.8 23.3 %collective-permute-done.8.got_a = bf16[128,2304]{1,0:T(8,128)(2,1)S(1)} collective-permute-done((bf16[128,2304]{1,0:T(8,128)(2,1)S(1)}, bf16[128,2304]{1,0:T(8,128)(2,1)S(1)}, u32[]{:S(2)}, u32[]{:S(2)}) %collective-permute-start.8) | collective-permute-done | bytes 589856 | tf_op jit(solution)/shard_map/ppermute | solution.py:471
  168.1 2.2 collective-permute-done.10.got_c
  170.3 5.1 %shard_map.169 = (bf16[128,2048]{1,0:T(8,128)(2,1)}, bf16[1024,2560]{1,0:T(8,128)(2,1)}) custom-call(f32[128,2048]{1,0:T(8,128)S(1)} %get-tuple-element.19.mine_ref, f32[128,128]{1,0:T(8,128)S(1)} %get-tuple-element.20.ss_ref, bf16[128,2304]{1,0:T(8,128)(2,1)S(1)} %collective-permute-done.8.got_a, bf16[128,2304]{1,0:T(8,128)(2,1)S(1)} %collective-permute-done.9.got_b, ...), custom_call_target="tpu_custom_call" | custom-call | tf_op jit(solution)/shard_map/pallas_call | solution.py:305
  175.4 10.1 %all-to-all-start.2 = ((bf16[128,8,2560]{2,1,0:T(8,128)(2,1)}), bf16[128,8,2560]{2,1,0:T(8,128)(2,1)}, u32[]{:S(2)}, u32[]{:S(2)}) async-start(bf16[128,8,2560]{2,1,0:T(8,128)(2,1)} %bitcast.23), calls=%async_computation.2 | async-start | bytes 10485760 | tf_op jit(solution)/shard_map/all_to_all | solution.py:475
  185.5 1.9 copy-done.3
  187.4 9.9 %shard_map.170 = (f32[1280,768]{1,0:T(8,128)}, bf16[256,2048]{1,0:T(8,128)(2,1)}) custom-call(bf16[1024,2560]{1,0:T(8,128)(2,1)} %bitcast.9.rows_ref.tail_ref.scaled_ref, bf16[1024,2560]{1,0:T(8,128)(2,1)} %bitcast.9.rows_ref.tail_ref.scaled_ref, bf16[768,2048]{1,0:T(8,128)(2,1)S(1)} %bitcast.17), custom_call_target="tpu_custom_call" | custom-call | tf_op jit(solution)/shard_map/pallas_call | solution.py:355
  197.3 52.0 %all-to-all-done.2 = bf16[128,8,2560]{2,1,0:T(8,128)(2,1)} async-done(((bf16[128,8,2560]{2,1,0:T(8,128)(2,1)}), bf16[128,8,2560]{2,1,0:T(8,128)(2,1)}, u32[]{:S(2)}, u32[]{:S(2)}) %all-to-all-start.2) | async-done | bytes 5242912 | tf_op jit(solution)/shard_map/all_to_all | solution.py:475
  249.3 30.0 %shard_map.171 = (bf16[2048,768]{1,0:T(8,128)(2,1)}, bf16[2048,768]{1,0:T(8,128)(2,1)}, bf16[768,2048]{1,0:T(8,128)(2,1)}) custom-call(bf16[1024,2560]{1,0:T(8,128)(2,1)} %bitcast.7.x_ref.tail_ref, bf16[1024,2560]{1,0:T(8,128)(2,1)} %bitcast.7.x_ref.tail_ref, f32[1280,768]{1,0:T(8,128)} %get-tuple-element.27.back_ref, bf16[2048,768]{1,0:T(8,128)(2,1)S(1)} %bitcast.16, ...), custom_call_target="tpu_custom_call" | custom-call | tf_op jit(solution)/shard_map/pallas_call | solution.py:438
  (39 shorter events, 0.5 us)
Async XLA Ops:
  0.6 14.6 %copy-start.1 = (bf16[4096,128]{1,0:T(8,128)(2,1)S(1)}, bf16[4096,128]{1,0:T(8,128)(2,1)}, u32[]{:S(2)}) copy-start(bf16[4096,128]{1,0:T(8,128)(2,1)} %v_ref.3) | copy-start | bytes 3145732
  0.6 14.6 %copy-start = (bf16[4096,128]{1,0:T(8,128)(2,1)S(1)}, bf16[4096,128]{1,0:T(8,128)(2,1)}, u32[]{:S(2)}) copy-start(bf16[4096,128]{1,0:T(8,128)(2,1)} %k_ref.3) | copy-start | bytes 3145732
  4.7 10.6 %all-to-all-start = ((bf16[4,128,256]{2,1,0:T(8,128)(2,1)}), bf16[4,128,256]{2,1,0:T(8,128)(2,1)S(1)}, u32[]{:S(2)}, u32[]{:S(2)}) async-start(bf16[4,128,256]{2,1,0:T(8,128)(2,1)} %shard_map.166), calls=%async_computation | async-start | bytes 524288 | tf_op jit(solution)/shard_map/all_to_all | solution.py:475
  15.2 1.2 copy-start.4
  16.5 0.7 copy-start.9
  17.1 10.6 %copy-start.6 = (bf16[128,2048]{1,0:T(8,128)(2,1)S(1)}, bf16[128,2048]{1,0:T(8,128)(2,1)}, u32[]{:S(2)}) copy-start(bf16[128,2048]{1,0:T(8,128)(2,1)} %cot_ref.1) | copy-start | bytes 1572868
  17.1 10.6 %copy-start.7 = (s32[128,8]{0,1:T(8,128)S(1)}, s32[128,8]{0,1:T(8,128)}, u32[]{:S(2)}) copy-start(s32[128,8]{0,1:T(8,128)} %param.21) | copy-start | bytes 12292
  17.1 10.6 %copy-start.8 = (f32[128,8]{0,1:T(8,128)S(1)}, f32[128,8]{0,1:T(8,128)}, u32[]{:S(2)}) copy-start(f32[128,8]{0,1:T(8,128)} %param.22) | copy-start | bytes 12292
  21.3 21.7 %all-to-all-start.1 = ((bf16[8,528,128]{2,1,0:T(8,128)(2,1)}), bf16[8,528,128]{2,1,0:T(8,128)(2,1)S(1)}, u32[]{:S(2)}, u32[]{:S(2)}) async-start(bf16[8,528,128]{2,1,0:T(8,128)(2,1)} %shard_map.167), calls=%async_computation.1 | async-start | bytes 2162688 | tf_op jit(solution)/shard_map/all_to_all | solution.py:475
  43.0 88.6 %copy-start.11 = (s32[4]{0:T(128)S(1)}, s32[4]{0:T(128)}, u32[]{:S(2)}) copy-start(s32[4]{0:T(128)} %constant.41.clone) | copy-start | bytes 52
  43.0 132.3 %all-to-all-start.3 = ((bf16[128,8,2560]{2,1,0:T(8,128)(2,1)}), bf16[128,8,2560]{2,1,0:T(8,128)(2,1)}, u32[]{:S(2)}, u32[]{:S(2)}) async-start(bf16[128,8,2560]{2,1,0:T(8,128)(2,1)} %bitcast.22), calls=%async_computation.3 | async-start | bytes 10485760 | tf_op jit(solution)/shard_map/all_to_all | solution.py:475
  50.5 69.8 %collective-permute-start = (bf16[128,2048]{1,0:T(8,128)(2,1)}, bf16[128,2048]{1,0:T(8,128)(2,1)S(1)}, u32[]{:S(2)}, u32[]{:S(2)}) collective-permute-start(bf16[128,2048]{1,0:T(8,128)(2,1)} %refs_0_.1), channel_id=1, source_target_pairs={{0,8},{8,16},{16,24},{24,0},{1,9},{9,17},{17,25},{25,1},{2,10},{10... | collective-permute-start | bytes 1572872 | tf_op jit(solution)/shard_map/ppermute | solution.py:471
  51.9 68.4 %collective-permute-start.1 = (bf16[128,2048]{1,0:T(8,128)(2,1)}, bf16[128,2048]{1,0:T(8,128)(2,1)S(1)}, u32[]{:S(2)}, u32[]{:S(2)}) collective-permute-start(bf16[128,2048]{1,0:T(8,128)(2,1)} %refs_0_.1), channel_id=1, source_target_pairs={{0,24},{8,0},{16,8},{24,16},{1,25},{9,1},{17,9},{25,17},{2,26},{10... | collective-permute-start | bytes 1572872 | tf_op jit(solution)/shard_map/ppermute | solution.py:471
  120.3 8.4 %collective-permute-start.2 = (bf16[128,1024]{1,0:T(8,128)(2,1)S(1)}, bf16[128,1024]{1,0:T(8,128)(2,1)S(1)}, u32[]{:S(2)}, u32[]{:S(2)}) collective-permute-start(bf16[128,1024]{1,0:T(8,128)(2,1)S(1)} %slice.8), channel_id=1, source_target_pairs={{0,8},{8,16},{16,24},{24,0},{1,9},{9,17},{17,25},{25,1},{2,10},{10... | collective-permute-start | bytes 786440 | tf_op jit(solution)/shard_map/ppermute | solution.py:471
  121.1 7.6 %collective-permute-start.3 = (bf16[128,1024]{1,0:T(8,128)(2,1)}, bf16[128,1024]{1,0:T(8,128)(2,1)}, u32[]{:S(2)}, u32[]{:S(2)}) collective-permute-start(bf16[128,1024]{1,0:T(8,128)(2,1)} %slice.9), channel_id=1, source_target_pairs={{0,24},{8,0},{16,8},{24,16},{1,25},{9,1},{17,9},{25,17},{2,26},{10... | collective-permute-start | bytes 786440 | tf_op jit(solution)/shard_map/ppermute | solution.py:471
  123.8 8.1 %collective-permute-start.4 = (bf16[128,2048]{1,0:T(8,128)(2,1)}, bf16[128,2048]{1,0:T(8,128)(2,1)}, u32[]{:S(2)}, u32[]{:S(2)}) collective-permute-start(bf16[128,2048]{1,0:T(8,128)(2,1)} %refs_0_.1), channel_id=1, source_target_pairs={{0,1},{1,0},{2,3},{3,2},{4,5},{5,4},{6,7},{7,6},{8,9},{9,8},{10,11... | collective-permute-start | bytes 1572872 | tf_op jit(solution)/shard_map/ppermute | solution.py:471
  125.2 19.6 %copy-start.10 = (bf16[2048]{0:T(1024)(128)(2,1)S(1)}, bf16[2048]{0:T(1024)(128)(2,1)}, u32[]{:S(2)}) copy-start(bf16[2048]{0:T(1024)(128)(2,1)} %param.20) | copy-start | bytes 12292
  125.2 45.0 %copy-start.5 = (bf16[128,2048]{1,0:T(8,128)(2,1)S(1)}, bf16[128,2048]{1,0:T(8,128)(2,1)}, u32[]{:S(2)}) copy-start(bf16[128,2048]{1,0:T(8,128)(2,1)} %residual_ref.1) | copy-start | bytes 1572868
  125.2 6.7 %collective-permute-start.6 = (bf16[128,2048]{1,0:T(8,128)(2,1)S(1)}, bf16[128,2048]{1,0:T(8,128)(2,1)}, u32[]{:S(2)}, u32[]{:S(2)}) collective-permute-start(bf16[128,2048]{1,0:T(8,128)(2,1)S(1)} %collective-permute-done.1.refs_2_), channel_id=1, source_target_pairs={{0,1},{1,0},{2,3},{3,2},{4,5},{5,4},{6,7},{7,6},{8,9},{9,8},{10,11... | collective-permute-start | bytes 1572872 | tf_op jit(solution)/shard_map/ppermute | solution.py:471
  125.3 6.7 %collective-permute-start.5 = (bf16[128,2048]{1,0:T(8,128)(2,1)S(1)}, bf16[128,2048]{1,0:T(8,128)(2,1)}, u32[]{:S(2)}, u32[]{:S(2)}) collective-permute-start(bf16[128,2048]{1,0:T(8,128)(2,1)S(1)} %collective-permute-done.refs_1_), channel_id=1, source_target_pairs={{0,1},{1,0},{2,3},{3,2},{4,5},{5,4},{6,7},{7,6},{8,9},{9,8},{10,11... | collective-permute-start | bytes 1572872 | tf_op jit(solution)/shard_map/ppermute | solution.py:471
  129.7 3.7 %collective-permute-start.7 = (bf16[128,2048]{1,0:T(8,128)(2,1)S(1)}, bf16[128,2048]{1,0:T(8,128)(2,1)}, u32[]{:S(2)}, u32[]{:S(2)}) collective-permute-start(bf16[128,2048]{1,0:T(8,128)(2,1)S(1)} %constant_dynamic-update-slice_fusion.refs_3_), channel_id=1, source_target_pairs={{0,1},{1,0},{2,3},{3,2},{4,5},{5,4},{6,7},{7,6},{8,9},{9,8},{10,11... | collective-permute-start | bytes 1572872 | tf_op jit(solution)/shard_map/ppermute | solution.py:471
  140.1 28.0 %collective-permute-start.8 = (bf16[128,2304]{1,0:T(8,128)(2,1)S(1)}, bf16[128,2304]{1,0:T(8,128)(2,1)S(1)}, u32[]{:S(2)}, u32[]{:S(2)}) collective-permute-start(bf16[128,2304]{1,0:T(8,128)(2,1)S(1)} %get-tuple-element.21), channel_id=1, source_target_pairs={{0,6},{2,0},{4,2},{6,4},{1,7},{3,1},{5,3},{7,5},{8,14},{10,8},{12,... | collective-permute-start | bytes 1769480 | tf_op jit(solution)/shard_map/ppermute | solution.py:471
  143.3 24.8 %collective-permute-start.9 = (bf16[128,2304]{1,0:T(8,128)(2,1)S(1)}, bf16[128,2304]{1,0:T(8,128)(2,1)S(1)}, u32[]{:S(2)}, u32[]{:S(2)}) collective-permute-start(bf16[128,2304]{1,0:T(8,128)(2,1)S(1)} %get-tuple-element.22), channel_id=1, source_target_pairs={{0,2},{2,4},{4,6},{6,0},{1,3},{3,5},{5,7},{7,1},{8,10},{10,12},{12... | collective-permute-start | bytes 1769480 | tf_op jit(solution)/shard_map/ppermute | solution.py:471
  143.3 27.0 %collective-permute-start.10 = (bf16[128,2304]{1,0:T(8,128)(2,1)S(1)}, bf16[128,2304]{1,0:T(8,128)(2,1)S(1)}, u32[]{:S(2)}, u32[]{:S(2)}) collective-permute-start(bf16[128,2304]{1,0:T(8,128)(2,1)S(1)} %get-tuple-element.23), channel_id=1, source_target_pairs={{0,4},{2,6},{4,0},{6,2},{1,5},{3,7},{5,1},{7,3},{8,12},{10,14},{12... | collective-permute-start | bytes 1769480 | tf_op jit(solution)/shard_map/ppermute | solution.py:471
  175.4 73.9 %all-to-all-start.2 = ((bf16[128,8,2560]{2,1,0:T(8,128)(2,1)}), bf16[128,8,2560]{2,1,0:T(8,128)(2,1)}, u32[]{:S(2)}, u32[]{:S(2)}) async-start(bf16[128,8,2560]{2,1,0:T(8,128)(2,1)} %bitcast.23), calls=%async_computation.2 | async-start | bytes 10485760 | tf_op jit(solution)/shard_map/all_to_all | solution.py:475
  185.5 1.9 copy-start.3
  187.4 61.9 %copy-start.2 = (bf16[1,2048,768]{2,1,0:T(8,128)(2,1)S(1)}, bf16[1,2048,768]{2,1,0:T(8,128)(2,1)}, u32[]{:S(2)}) copy-start(bf16[1,2048,768]{2,1,0:T(8,128)(2,1)} %param.24) | copy-start | bytes 9437188

commit v9 on v8

--- a/solution.py
+++ b/solution.py
@@ -232,9 +232,10 @@
         if d == 0:
             ss_ref[...] = summed
         else:
-            high = summed.astype(BF)
-            out_refs[d - 1][:, total : total + HD] = high
-            out_refs[d - 1][:, total + HD :] = (summed - high.astype(F32)).astype(BF)
+            high = summed.astype(BF).astype(F32)
+            lane = lax.broadcasted_iota(jnp.int32, high.shape, 1)
+            both = jnp.where(lane < HD // 2, high, summed - high)
+            out_refs[d - 1][:, total:] = both.astype(BF)
 
     side = 512
     for n in range(total // side):
@@ -251,7 +252,7 @@
     tokens = (x.shape[1] - EXTRA) // 4
     width = pieces[0].shape[1]
     args = (x,) + tuple(pieces)
-    shapes = [(width, F32), (HD, F32)] + [(width + 2 * HD, BF)] * 3
+    shapes = [(width, F32), (HD, F32)] + [(width + HD, BF)] * 3
     return pl.pallas_call(
         project_kernel,
         grid_spec=pltpu.PrefetchScalarGridSpec(
@@ -275,13 +276,13 @@
     @pl.when(step == 0)
     def _():
         width = mine_ref.shape[1]
-        squares = ss_ref[...]
+        squares = ss_ref[:, :1]
         projected = mine_ref[...]
         for got in (got_a, got_b, got_c):
-            squares = squares + got[:, width : width + HD].astype(F32)
-            squares = squares + got[:, width + HD :].astype(F32)
+            sent = got[:, width:].astype(F32)
+            squares = squares + sent[:, :1] + sent[:, HD // 2 : HD // 2 + 1]
             projected = projected + got[:, :width].astype(F32)
-        inverse = lax.rsqrt(squares[:, :1] / (HEADS * HD) + EPS)
+        inverse = lax.rsqrt(squares / (HEADS * HD) + EPS)
         projected = projected * inverse
         hidden = (residual_ref[...].astype(F32) + projected).astype(BF)
         hidden_ref[...] = hidden

time: 280 us -> 279 us (level)
  no operation moved by 1% of the time
where the time goes in v9:
time: 279 us; the launch traced here: 278 us
  waiting for transfers between devices  163 us (58%)
  Pallas kernels  64.9 us (23%)
  starting transfers between devices  43.1 us (15%)
  local copies, waits for them, and re-layouts  5.62 us (2%)
    ppermute x11, waiting for transfers between devices, shift(): lax.ppermute(array, axis, [(i, (i + by) % size) for i in range(size)])  95.4 us
    all_to_all x4, waiting for transfers between devices, exchange(): return lax.all_to_all(array, axes, split_axis=0, concat_axis=0, tiled=True)  67.9 us
    pallas_call x1, Pallas kernels, expert_grads(): pl.pallas_call(grads_kernel, grid=(blocks + width // block,), in_specs=[p...  30 us
    all_to_all x4, starting transfers between devices, exchange(): return lax.all_to_all(array, axes, split_axis=0, concat_axis=0, tiled=True)  29 us
    ppermute x11, starting transfers between devices, shift(): lax.ppermute(array, axis, [(i, (i + by) % size) for i in range(size)])  14.1 us
    pallas_call x1, Pallas kernels, hidden_grad(): pl.pallas_call(hidden_kernel, grid=(blocks + 1,), in_specs=[pl.BlockSpec(...  9.91 us
    pallas_call x1, Pallas kernels, project(): pl.pallas_call(project_kernel, grid_spec=pltpu.PrefetchScalarGridSpec(num...  6.74 us
  transfers between devices with their start and end apart: 15, of which 8 were waited for; matrix products, arithmetic and copies ran while one was open for 1% of the time, Pallas kernels for 10%

profile of v9, /device:TPU:1, one launch (start us, length us, event | category | flops | bytes accessed | tf_op | source)
XLA Modules:
  0.0 277.9 jit_solution(14550381633983687917)
XLA Ops:
  0.7 4.0 %shard_map.166 = bf16[4,128,256]{2,1,0:T(8,128)(2,1)} custom-call(bf16[4096,128]{1,0:T(8,128)(2,1)} %k_ref.3, bf16[4096,128]{1,0:T(8,128)(2,1)} %v_ref.3), custom_call_target="tpu_custom_call" | custom-call | tf_op jit(solution)/shard_map/pallas_call | solution.py:57
  4.7 5.0 %all-to-all-start = ((bf16[4,128,256]{2,1,0:T(8,128)(2,1)}), bf16[4,128,256]{2,1,0:T(8,128)(2,1)S(1)}, u32[]{:S(2)}, u32[]{:S(2)}) async-start(bf16[4,128,256]{2,1,0:T(8,128)(2,1)} %shard_map.166), calls=%async_computation | async-start | bytes 524288 | tf_op jit(solution)/shard_map/all_to_all | solution.py:476
  9.7 5.6 %all-to-all-done.s_ref = bf16[4,128,256]{2,1,0:T(8,128)(2,1)S(1)} async-done(((bf16[4,128,256]{2,1,0:T(8,128)(2,1)}), bf16[4,128,256]{2,1,0:T(8,128)(2,1)S(1)}, u32[]{:S(2)}, u32[]{:S(2)}) %all-to-all-start) | async-done | bytes 262176 | tf_op jit(solution)/shard_map/all_to_all | solution.py:476
  15.2 1.2 copy-done.4
  16.5 0.7 copy-done.9
  17.1 4.2 %shard_map.167 = bf16[8,528,128]{2,1,0:T(8,128)(2,1)} custom-call(s32[1]{0:T(128)} %bitcast.4.at_ref, bf16[4096,128]{1,0:T(8,128)(2,1)S(1)} %copy-done.4, bf16[4096,128]{1,0:T(8,128)(2,1)S(1)} %copy-done, bf16[4096,128]{1,0:T(8,128)(2,1)S(1)} %copy-done.1, bf16[4,128,256]{2,1,0:T(8,128)(2,1)S(1)} %all-to-all-done.s_ref, bf16[1,128]{1,0:T(2,128)(2,1)S(1)} %bitcast.21), custom_call_target="tpu_custom_call" | custom-call | tf_op jit(solution)/shard_map/pallas_call | solution.py:107
  21.3 6.4 %all-to-all-start.1 = ((bf16[8,528,128]{2,1,0:T(8,128)(2,1)}), bf16[8,528,128]{2,1,0:T(8,128)(2,1)S(1)}, u32[]{:S(2)}, u32[]{:S(2)}) async-start(bf16[8,528,128]{2,1,0:T(8,128)(2,1)} %shard_map.167), calls=%async_computation.1 | async-start | bytes 2162688 | tf_op jit(solution)/shard_map/all_to_all | solution.py:476
  27.7 5.0 %shard_map.165 = bf16[1024,2560]{1,0:T(8,128)(2,1)} custom-call(s32[8,128]{1,0:T(8,128)S(1)} %bitcast.18, f32[8,128]{1,0:T(8,128)S(1)} %bitcast.20, bf16[128,2048]{1,0:T(8,128)(2,1)S(1)} %copy-done.6), custom_call_target="tpu_custom_call" | custom-call | tf_op jit(solution)/shard_map/pallas_call | solution.py:207
  32.7 10.3 %all-to-all-done.1.x_ref = bf16[8,528,128]{2,1,0:T(8,128)(2,1)S(1)} async-done(((bf16[8,528,128]{2,1,0:T(8,128)(2,1)}), bf16[8,528,128]{2,1,0:T(8,128)(2,1)S(1)}, u32[]{:S(2)}, u32[]{:S(2)}) %all-to-all-start.1) | async-done | bytes 1081376 | tf_op jit(solution)/shard_map/all_to_all | solution.py:476
  43.0 7.5 %all-to-all-start.3 = ((bf16[128,8,2560]{2,1,0:T(8,128)(2,1)}), bf16[128,8,2560]{2,1,0:T(8,128)(2,1)}, u32[]{:S(2)}, u32[]{:S(2)}) async-start(bf16[128,8,2560]{2,1,0:T(8,128)(2,1)} %bitcast.22), calls=%async_computation.3 | async-start | bytes 10485760 | tf_op jit(solution)/shard_map/all_to_all | solution.py:476
  50.5 1.4 collective-permute-start
  51.9 1.3 collective-permute-start.1
  53.3 67.0 %collective-permute-done.refs_1_ = bf16[128,2048]{1,0:T(8,128)(2,1)S(1)} collective-permute-done((bf16[128,2048]{1,0:T(8,128)(2,1)}, bf16[128,2048]{1,0:T(8,128)(2,1)S(1)}, u32[]{:S(2)}, u32[]{:S(2)}) %collective-permute-start) | collective-permute-done | bytes 524320 | tf_op jit(solution)/shard_map/ppermute | solution.py:472
  120.4 0.7 slice.9
  121.1 2.7 collective-permute-start.3
  123.8 1.4 collective-permute-start.4
  125.3 0.5 collective-permute-start.5
  125.8 2.9 %collective-permute-done.2 = bf16[128,1024]{1,0:T(8,128)(2,1)S(1)} collective-permute-done((bf16[128,1024]{1,0:T(8,128)(2,1)S(1)}, bf16[128,1024]{1,0:T(8,128)(2,1)S(1)}, u32[]{:S(2)}, u32[]{:S(2)}) %collective-permute-start.2) | collective-permute-done | bytes 262176 | tf_op jit(solution)/shard_map/ppermute | solution.py:472
  128.7 1.0 constant_dynamic-update-slice_fusion.refs_3_
  129.7 2.0 collective-permute-start.7
  131.9 1.4 collective-permute-done.7.refs_7_
  133.3 6.7 %shard_map.168 = (f32[128,2048]{1,0:T(8,128)S(1)}, f32[128,128]{1,0:T(8,128)S(1)}, bf16[128,2176]{1,0:T(8,128)(2,1)S(1)}, bf16[128,2176]{1,0:T(8,128)(2,1)S(1)}, bf16[128,2176]{1,0:T(8,128)(2,1)S(1)}) custom-call(s32[12]{0:T(128)S(1)} %pad_add_fusion.1.place_ref, bf16[8,528,128]{2,1,0:T(8,128)(2,1)S(1)} %all-to-all-done.1.x_ref, bf16[128,2048]{1,0:T(8,128)(2,1)} %refs_0_.1, ...), custom_call_target="tpu_custom_call" | custom-call | tf_op jit(solution)/shard_map/pallas_call | solution.py:256
  140.1 3.2 %collective-permute-start.8 = (bf16[128,2176]{1,0:T(8,128)(2,1)S(1)}, bf16[128,2176]{1,0:T(8,128)(2,1)S(1)}, u32[]{:S(2)}, u32[]{:S(2)}) collective-permute-start(bf16[128,2176]{1,0:T(8,128)(2,1)S(1)} %get-tuple-element.21), channel_id=1, source_target_pairs={{0,6},{2,0},{4,2},{6,4},{1,7},{3,1},{5,3},{7,5},{8,14},{10,8},{12,... | collective-permute-start | bytes 1671176 | tf_op jit(solution)/shard_map/ppermute | solution.py:472
  143.3 1.5 collective-permute-start.10
  144.8 21.9 %collective-permute-done.8.got_a = bf16[128,2176]{1,0:T(8,128)(2,1)S(1)} collective-permute-done((bf16[128,2176]{1,0:T(8,128)(2,1)S(1)}, bf16[128,2176]{1,0:T(8,128)(2,1)S(1)}, u32[]{:S(2)}, u32[]{:S(2)}) %collective-permute-start.8) | collective-permute-done | bytes 557088 | tf_op jit(solution)/shard_map/ppermute | solution.py:472
  166.7 2.2 collective-permute-done.10.got_c
  168.9 5.0 %shard_map.169 = (bf16[128,2048]{1,0:T(8,128)(2,1)}, bf16[1024,2560]{1,0:T(8,128)(2,1)}) custom-call(f32[128,2048]{1,0:T(8,128)S(1)} %get-tuple-element.19.mine_ref, f32[128,128]{1,0:T(8,128)S(1)} %get-tuple-element.20.ss_ref, bf16[128,2176]{1,0:T(8,128)(2,1)S(1)} %collective-permute-done.8.got_a, bf16[128,2176]{1,0:T(8,128)(2,1)S(1)} %collective-permute-done.9.got_b, ...), custom_call_target="tpu_custom_call" | custom-call | tf_op jit(solution)/shard_map/pallas_call | solution.py:306
  173.9 10.1 %all-to-all-start.2 = ((bf16[128,8,2560]{2,1,0:T(8,128)(2,1)}), bf16[128,8,2560]{2,1,0:T(8,128)(2,1)}, u32[]{:S(2)}, u32[]{:S(2)}) async-start(bf16[128,8,2560]{2,1,0:T(8,128)(2,1)} %bitcast.23), calls=%async_computation.2 | async-start | bytes 10485760 | tf_op jit(solution)/shard_map/all_to_all | solution.py:476
  184.0 1.9 copy-done.3
  185.9 9.9 %shard_map.170 = (f32[1280,768]{1,0:T(8,128)}, bf16[256,2048]{1,0:T(8,128)(2,1)}) custom-call(bf16[1024,2560]{1,0:T(8,128)(2,1)} %bitcast.9.rows_ref.tail_ref.scaled_ref, bf16[1024,2560]{1,0:T(8,128)(2,1)} %bitcast.9.rows_ref.tail_ref.scaled_ref, bf16[768,2048]{1,0:T(8,128)(2,1)S(1)} %bitcast.17), custom_call_target="tpu_custom_call" | custom-call | tf_op jit(solution)/shard_map/pallas_call | solution.py:356
  195.8 52.0 %all-to-all-done.2 = bf16[128,8,2560]{2,1,0:T(8,128)(2,1)} async-done(((bf16[128,8,2560]{2,1,0:T(8,128)(2,1)}), bf16[128,8,2560]{2,1,0:T(8,128)(2,1)}, u32[]{:S(2)}, u32[]{:S(2)}) %all-to-all-start.2) | async-done | bytes 5242912 | tf_op jit(solution)/shard_map/all_to_all | solution.py:476
  247.8 30.0 %shard_map.171 = (bf16[2048,768]{1,0:T(8,128)(2,1)}, bf16[2048,768]{1,0:T(8,128)(2,1)}, bf16[768,2048]{1,0:T(8,128)(2,1)}) custom-call(bf16[1024,2560]{1,0:T(8,128)(2,1)} %bitcast.7.x_ref.tail_ref, bf16[1024,2560]{1,0:T(8,128)(2,1)} %bitcast.7.x_ref.tail_ref, f32[1280,768]{1,0:T(8,128)} %get-tuple-element.27.back_ref, bf16[2048,768]{1,0:T(8,128)(2,1)S(1)} %bitcast.16, ...), custom_call_target="tpu_custom_call" | custom-call | tf_op jit(solution)/shard_map/pallas_call | solution.py:439
  (39 shorter events, 0.5 us)
Async XLA Ops:
  0.6 14.6 %copy-start.1 = (bf16[4096,128]{1,0:T(8,128)(2,1)S(1)}, bf16[4096,128]{1,0:T(8,128)(2,1)}, u32[]{:S(2)}) copy-start(bf16[4096,128]{1,0:T(8,128)(2,1)} %v_ref.3) | copy-start | bytes 3145732
  0.6 14.6 %copy-start = (bf16[4096,128]{1,0:T(8,128)(2,1)S(1)}, bf16[4096,128]{1,0:T(8,128)(2,1)}, u32[]{:S(2)}) copy-start(bf16[4096,128]{1,0:T(8,128)(2,1)} %k_ref.3) | copy-start | bytes 3145732
  4.7 10.6 %all-to-all-start = ((bf16[4,128,256]{2,1,0:T(8,128)(2,1)}), bf16[4,128,256]{2,1,0:T(8,128)(2,1)S(1)}, u32[]{:S(2)}, u32[]{:S(2)}) async-start(bf16[4,128,256]{2,1,0:T(8,128)(2,1)} %shard_map.166), calls=%async_computation | async-start | bytes 524288 | tf_op jit(solution)/shard_map/all_to_all | solution.py:476
  15.2 1.2 copy-start.4
  16.5 0.7 copy-start.9
  17.1 10.6 %copy-start.6 = (bf16[128,2048]{1,0:T(8,128)(2,1)S(1)}, bf16[128,2048]{1,0:T(8,128)(2,1)}, u32[]{:S(2)}) copy-start(bf16[128,2048]{1,0:T(8,128)(2,1)} %cot_ref.1) | copy-start | bytes 1572868
  17.1 10.6 %copy-start.7 = (s32[128,8]{0,1:T(8,128)S(1)}, s32[128,8]{0,1:T(8,128)}, u32[]{:S(2)}) copy-start(s32[128,8]{0,1:T(8,128)} %param.21) | copy-start | bytes 12292
  17.1 10.6 %copy-start.8 = (f32[128,8]{0,1:T(8,128)S(1)}, f32[128,8]{0,1:T(8,128)}, u32[]{:S(2)}) copy-start(f32[128,8]{0,1:T(8,128)} %param.22) | copy-start | bytes 12292
  21.3 21.7 %all-to-all-start.1 = ((bf16[8,528,128]{2,1,0:T(8,128)(2,1)}), bf16[8,528,128]{2,1,0:T(8,128)(2,1)S(1)}, u32[]{:S(2)}, u32[]{:S(2)}) async-start(bf16[8,528,128]{2,1,0:T(8,128)(2,1)} %shard_map.167), calls=%async_computation.1 | async-start | bytes 2162688 | tf_op jit(solution)/shard_map/all_to_all | solution.py:476
  43.0 88.6 %copy-start.11 = (s32[4]{0:T(128)S(1)}, s32[4]{0:T(128)}, u32[]{:S(2)}) copy-start(s32[4]{0:T(128)} %constant.41.clone) | copy-start | bytes 52
  43.0 130.8 %all-to-all-start.3 = ((bf16[128,8,2560]{2,1,0:T(8,128)(2,1)}), bf16[128,8,2560]{2,1,0:T(8,128)(2,1)}, u32[]{:S(2)}, u32[]{:S(2)}) async-start(bf16[128,8,2560]{2,1,0:T(8,128)(2,1)} %bitcast.22), calls=%async_computation.3 | async-start | bytes 10485760 | tf_op jit(solution)/shard_map/all_to_all | solution.py:476
  50.5 69.8 %collective-permute-start = (bf16[128,2048]{1,0:T(8,128)(2,1)}, bf16[128,2048]{1,0:T(8,128)(2,1)S(1)}, u32[]{:S(2)}, u32[]{:S(2)}) collective-permute-start(bf16[128,2048]{1,0:T(8,128)(2,1)} %refs_0_.1), channel_id=1, source_target_pairs={{0,8},{8,16},{16,24},{24,0},{1,9},{9,17},{17,25},{25,1},{2,10},{10... | collective-permute-start | bytes 1572872 | tf_op jit(solution)/shard_map/ppermute | solution.py:472
  51.9 68.4 %collective-permute-start.1 = (bf16[128,2048]{1,0:T(8,128)(2,1)}, bf16[128,2048]{1,0:T(8,128)(2,1)S(1)}, u32[]{:S(2)}, u32[]{:S(2)}) collective-permute-start(bf16[128,2048]{1,0:T(8,128)(2,1)} %refs_0_.1), channel_id=1, source_target_pairs={{0,24},{8,0},{16,8},{24,16},{1,25},{9,1},{17,9},{25,17},{2,26},{10... | collective-permute-start | bytes 1572872 | tf_op jit(solution)/shard_map/ppermute | solution.py:472
  120.3 8.4 %collective-permute-start.2 = (bf16[128,1024]{1,0:T(8,128)(2,1)S(1)}, bf16[128,1024]{1,0:T(8,128)(2,1)S(1)}, u32[]{:S(2)}, u32[]{:S(2)}) collective-permute-start(bf16[128,1024]{1,0:T(8,128)(2,1)S(1)} %slice.8), channel_id=1, source_target_pairs={{0,8},{8,16},{16,24},{24,0},{1,9},{9,17},{17,25},{25,1},{2,10},{10... | collective-permute-start | bytes 786440 | tf_op jit(solution)/shard_map/ppermute | solution.py:472
  121.1 7.6 %collective-permute-start.3 = (bf16[128,1024]{1,0:T(8,128)(2,1)}, bf16[128,1024]{1,0:T(8,128)(2,1)}, u32[]{:S(2)}, u32[]{:S(2)}) collective-permute-start(bf16[128,1024]{1,0:T(8,128)(2,1)} %slice.9), channel_id=1, source_target_pairs={{0,24},{8,0},{16,8},{24,16},{1,25},{9,1},{17,9},{25,17},{2,26},{10... | collective-permute-start | bytes 786440 | tf_op jit(solution)/shard_map/ppermute | solution.py:472
  123.8 8.1 %collective-permute-start.4 = (bf16[128,2048]{1,0:T(8,128)(2,1)}, bf16[128,2048]{1,0:T(8,128)(2,1)}, u32[]{:S(2)}, u32[]{:S(2)}) collective-permute-start(bf16[128,2048]{1,0:T(8,128)(2,1)} %refs_0_.1), channel_id=1, source_target_pairs={{0,1},{1,0},{2,3},{3,2},{4,5},{5,4},{6,7},{7,6},{8,9},{9,8},{10,11... | collective-permute-start | bytes 1572872 | tf_op jit(solution)/shard_map/ppermute | solution.py:472
  125.2 19.6 %copy-start.10 = (bf16[2048]{0:T(1024)(128)(2,1)S(1)}, bf16[2048]{0:T(1024)(128)(2,1)}, u32[]{:S(2)}) copy-start(bf16[2048]{0:T(1024)(128)(2,1)} %param.20) | copy-start | bytes 12292
  125.2 43.6 %copy-start.5 = (bf16[128,2048]{1,0:T(8,128)(2,1)S(1)}, bf16[128,2048]{1,0:T(8,128)(2,1)}, u32[]{:S(2)}) copy-start(bf16[128,2048]{1,0:T(8,128)(2,1)} %residual_ref.1) | copy-start | bytes 1572868
  125.2 6.7 %collective-permute-start.6 = (bf16[128,2048]{1,0:T(8,128)(2,1)S(1)}, bf16[128,2048]{1,0:T(8,128)(2,1)}, u32[]{:S(2)}, u32[]{:S(2)}) collective-permute-start(bf16[128,2048]{1,0:T(8,128)(2,1)S(1)} %collective-permute-done.1.refs_2_), channel_id=1, source_target_pairs={{0,1},{1,0},{2,3},{3,2},{4,5},{5,4},{6,7},{7,6},{8,9},{9,8},{10,11... | collective-permute-start | bytes 1572872 | tf_op jit(solution)/shard_map/ppermute | solution.py:472
  125.3 6.7 %collective-permute-start.5 = (bf16[128,2048]{1,0:T(8,128)(2,1)S(1)}, bf16[128,2048]{1,0:T(8,128)(2,1)}, u32[]{:S(2)}, u32[]{:S(2)}) collective-permute-start(bf16[128,2048]{1,0:T(8,128)(2,1)S(1)} %collective-permute-done.refs_1_), channel_id=1, source_target_pairs={{0,1},{1,0},{2,3},{3,2},{4,5},{5,4},{6,7},{7,6},{8,9},{9,8},{10,11... | collective-permute-start | bytes 1572872 | tf_op jit(solution)/shard_map/ppermute | solution.py:472
  129.7 3.7 %collective-permute-start.7 = (bf16[128,2048]{1,0:T(8,128)(2,1)S(1)}, bf16[128,2048]{1,0:T(8,128)(2,1)}, u32[]{:S(2)}, u32[]{:S(2)}) collective-permute-start(bf16[128,2048]{1,0:T(8,128)(2,1)S(1)} %constant_dynamic-update-slice_fusion.refs_3_), channel_id=1, source_target_pairs={{0,1},{1,0},{2,3},{3,2},{4,5},{5,4},{6,7},{7,6},{8,9},{9,8},{10,11... | collective-permute-start | bytes 1572872 | tf_op jit(solution)/shard_map/ppermute | solution.py:472
  140.1 26.6 %collective-permute-start.8 = (bf16[128,2176]{1,0:T(8,128)(2,1)S(1)}, bf16[128,2176]{1,0:T(8,128)(2,1)S(1)}, u32[]{:S(2)}, u32[]{:S(2)}) collective-permute-start(bf16[128,2176]{1,0:T(8,128)(2,1)S(1)} %get-tuple-element.21), channel_id=1, source_target_pairs={{0,6},{2,0},{4,2},{6,4},{1,7},{3,1},{5,3},{7,5},{8,14},{10,8},{12,... | collective-permute-start | bytes 1671176 | tf_op jit(solution)/shard_map/ppermute | solution.py:472
  143.3 23.4 %collective-permute-start.9 = (bf16[128,2176]{1,0:T(8,128)(2,1)S(1)}, bf16[128,2176]{1,0:T(8,128)(2,1)S(1)}, u32[]{:S(2)}, u32[]{:S(2)}) collective-permute-start(bf16[128,2176]{1,0:T(8,128)(2,1)S(1)} %get-tuple-element.22), channel_id=1, source_target_pairs={{0,2},{2,4},{4,6},{6,0},{1,3},{3,5},{5,7},{7,1},{8,10},{10,12},{12... | collective-permute-start | bytes 1671176 | tf_op jit(solution)/shard_map/ppermute | solution.py:472
  143.3 25.6 %collective-permute-start.10 = (bf16[128,2176]{1,0:T(8,128)(2,1)S(1)}, bf16[128,2176]{1,0:T(8,128)(2,1)S(1)}, u32[]{:S(2)}, u32[]{:S(2)}) collective-permute-start(bf16[128,2176]{1,0:T(8,128)(2,1)S(1)} %get-tuple-element.23), channel_id=1, source_target_pairs={{0,4},{2,6},{4,0},{6,2},{1,5},{3,7},{5,1},{7,3},{8,12},{10,14},{12... | collective-permute-start | bytes 1671176 | tf_op jit(solution)/shard_map/ppermute | solution.py:472
  173.9 74.0 %all-to-all-start.2 = ((bf16[128,8,2560]{2,1,0:T(8,128)(2,1)}), bf16[128,8,2560]{2,1,0:T(8,128)(2,1)}, u32[]{:S(2)}, u32[]{:S(2)}) async-start(bf16[128,8,2560]{2,1,0:T(8,128)(2,1)} %bitcast.23), calls=%async_computation.2 | async-start | bytes 10485760 | tf_op jit(solution)/shard_map/all_to_all | solution.py:476
  184.0 1.9 copy-start.3
  185.9 61.9 %copy-start.2 = (bf16[1,2048,768]{2,1,0:T(8,128)(2,1)S(1)}, bf16[1,2048,768]{2,1,0:T(8,128)(2,1)}, u32[]{:S(2)}) copy-start(bf16[1,2048,768]{2,1,0:T(8,128)(2,1)} %param.24) | copy-start | bytes 9437188
